TPU v7x, 32 devices: a whole 2x2x4 slice. The times are simulated.
32 devices in a mesh: expert: 8 (over z, x), fsdp: 4 (over y, core).
Axes of the slice: x: 2, y: 2, z: 4, core: 2. Of those that a mesh axis runs over, the one named last changes fastest.
Arguments:
- tokens: bfloat16 [2048, 7168], P('expert', 'fsdp'), may hold values from -6 to 6
- output_grad: bfloat16 [2048, 7168], P('expert', 'fsdp'), may hold values from -6 to 6
- route_weight: float32 [2048, 8], P('expert'), may hold values from 0.05 to 0.5
- expert_ids: int32 [2048, 8], P('expert'), may hold values from 0 to 255, all different within a row; in each aligned block of 256 rows (0 to 255, 256 to 511, ...) at most 12 rows name the same one
- gate_weight: bfloat16 [8, 7168, 512], P('expert', 'fsdp'), may hold values from -0.0625 to 0.0625
- up_weight: bfloat16 [8, 7168, 512], P('expert', 'fsdp'), may hold values from -0.0625 to 0.0625
- down_weight: bfloat16 [8, 512, 7168], P('expert', None, 'fsdp'), may hold values from -0.1875 to 0.1875
Outputs:
- token_grad: bfloat16 [2048, 7168], P('expert', 'fsdp')
- gate_grad: bfloat16 [8, 7168, 512], P('expert', 'fsdp')
- up_grad: bfloat16 [8, 7168, 512], P('expert', 'fsdp')
- down_grad: bfloat16 [8, 512, 7168], P('expert', None, 'fsdp')
Inputs may be any that keep to these rules, and one draw needn't show every extreme that they name: `expert_ids`: in each block of 256 rows (the tokens held by one position along `expert` (one block of 256 consecutive rows)) no expert is named by more than 12 rows, a bound that some block reaches.
All inputs are finite; a program needn't handle non-finite values.
Results may differ from a plain program's by a relative error of at most 0.025.
Values may be sent and summed in bfloat16 or wider, within the bound.
No kernel may reach another device: no remote copies, remote signals or barrier semaphores. Data moves between devices by JAX's collectives and lax.ppermute only.
A program may use at most 64 MiB of HBM per device.

v0:
```python
import functools

import jax
import jax.numpy as jnp
from jax import lax
from jax.experimental import pallas as pl
from jax.experimental.pallas import tpu as pltpu
from jax.sharding import PartitionSpec as P


CAP = 12
PAIR = 2 * CAP
BF16, F32 = jnp.bfloat16, jnp.float32
OVER_COLUMNS = (((1,), (1,)), ((), ()))
OVER_ROWS = (((0,), (0,)), ((), ()))


def dot(a, b, dims=None):
    if dims is None:
        dims = (((1,), (0,)), ((), ()))
    return lax.dot_general(a, b, dims, preferred_element_type=F32)


def upper(rows, columns):
    shape = (rows // PAIR, PAIR, columns)
    return (lax.broadcasted_iota(jnp.int32, shape, 1) < CAP).reshape(rows, columns)


def swapped(v, first):
    rows = v.shape[0]
    return jnp.where(first, pltpu.roll(v, rows - CAP, 0), pltpu.roll(v, CAP, 0))


def call(kernel, outs, *args, vmem=24, **kw):
    space = pl.BlockSpec(memory_space=pltpu.VMEM)
    return pl.pallas_call(
        kernel,
        out_shape=outs,
        in_specs=[space] * len(args),
        out_specs=jax.tree.map(lambda _: space, outs),
        compiler_params=pltpu.CompilerParams(vmem_limit_bytes=vmem << 20),
        **kw,
    )(*args)


def in_hbm(v):
    return pltpu.with_memory_space_constraint(v, pltpu.HBM)


def shape(dims, dtype=BF16):
    return jax.ShapeDtypeStruct(dims, dtype)


def columns(refs):
    if len(refs) == 2:
        return refs
    w = refs[0].shape[1] // 2
    return refs[0].at[:, 0:w], refs[0].at[:, w : 2 * w]


def place_kernel(window, halves, *refs):
    e_ref, ids_hbm, w_hbm = refs[:3]
    sources = columns(refs[3 : 3 + halves]) + columns(refs[3 + halves : 3 + 2 * halves])
    outs = refs[3 + 2 * halves : -4]
    held, ids_ref, w_ref, sems = refs[-4:]
    messages, (p0_ref, p1_ref) = outs[:window], outs[window:]
    copies = [pltpu.make_async_copy(src, dst, sem) for src, dst, sem in zip(
        (ids_hbm, w_hbm) + tuple(sources),
        (ids_ref, w_ref) + tuple(held.at[i] for i in range(4)),
        [sems.at[i] for i in range(6)],
    )]
    for copy in copies:
        copy.start()
    copies[0].wait()
    copies[1].wait()
    top, tok = ids_ref.shape
    dims = (window, PAIR, tok)
    rows = window * PAIR
    expert = lax.broadcasted_iota(jnp.int32, dims, 0) + e_ref[0]
    expert = jnp.where(expert >= window, expert - window, expert)
    slot = lax.broadcasted_iota(jnp.int32, dims, 1).astype(F32).reshape(rows, tok)
    hit = jnp.zeros(dims, F32)
    weight = jnp.zeros(dims, F32)
    for k in range(top):
        same = ids_ref[k : k + 1, :][None] == expert
        hit = jnp.where(same, 1.0, hit)
        weight = jnp.where(same, w_ref[k : k + 1, :][None], weight)
    hit = hit.reshape(rows, tok)
    weight = weight.reshape(rows, tok)
    before = lax.broadcasted_iota(jnp.int32, (tok, tok), 0) < lax.broadcasted_iota(
        jnp.int32, (tok, tok), 1
    )
    rank = dot(hit.astype(BF16), before.astype(F32).astype(BF16))
    p0 = jnp.where(rank == slot, hit, 0.0)
    p1 = jnp.where(rank + CAP == slot, hit, 0.0)
    scale = jnp.sum((p0 + p1) * weight, axis=1, keepdims=True)
    p0, p1 = p0.astype(BF16), p1.astype(BF16)
    p0_ref[...] = p0
    p1_ref[...] = p1
    copies[2].wait()
    copies[3].wait()
    message = dot(p0, held[0]) + dot(p1, held[1])
    for d in range(window):
        messages[d][:PAIR] = message[d * PAIR : (d + 1) * PAIR].astype(BF16)
    copies[4].wait()
    copies[5].wait()
    message = (dot(p0, held[2]) + dot(p1, held[3])) * scale
    for d in range(window):
        messages[d][PAIR:] = message[d * PAIR : (d + 1) * PAIR].astype(BF16)


def load_kernel(*refs):
    n = (len(refs) - 1) // 2
    copies = [pltpu.make_async_copy(refs[i], refs[n + i], refs[-1].at[i]) for i in range(n)]
    for copy in copies:
        copy.start()
    for copy in copies:
        copy.wait()


def joined(refs):
    return jnp.concatenate([r[...].astype(F32) for r in refs], axis=0)


def received(own, other, part):
    take = slice(part * PAIR, (part + 1) * PAIR)
    blocks = [ref[take].astype(F32) for ref in own]
    for d in range(len(own)):
        start = 2 * d * PAIR + part * PAIR
        blocks.append(other[start : start + PAIR].astype(F32))
    return jnp.concatenate(blocks, axis=0)


def product_kernel(count, *refs):
    own, other, (gate_ref, up_ref, down_ref, out_ref) = refs[:count], refs[count], refs[count + 1 :]
    w = other.shape[1]
    n = count * PAIR
    rows = received(own, other, 0)
    first = upper(*rows.shape)
    turned = swapped(rows, first).astype(BF16)
    rows = rows.astype(BF16)
    gate = dot(rows, gate_ref[0, :w]) + dot(turned, gate_ref[0, w:])
    up = dot(turned, up_ref[0, :w]) + dot(rows, up_ref[0, w:])
    out_ref[: 2 * n] = jnp.where(upper(*gate.shape), gate, up).astype(BF16)
    grads = received(own, other, 1)
    turned = swapped(grads, first)
    low = jnp.concatenate([grads[:n], turned[n:]], axis=0).astype(BF16)
    high = jnp.concatenate([turned[:n], grads[n:]], axis=0).astype(BF16)
    part = dot(low, down_ref[0, :, :w], OVER_COLUMNS) + dot(high, down_ref[0, :, w:], OVER_COLUMNS)
    out_ref[2 * n :] = jnp.where(upper(n, part.shape[1]), part[:n], part[n:]).astype(BF16)


def delta_kernel(a_ref, b_ref, gate_ref, up_ref, act_ref, d_ref, dt_ref, own_ref, other_ref):
    n, w = own_ref.shape
    total = a_ref[...].astype(F32) + b_ref[...].astype(F32)
    gu, h = total[: 2 * n], total[2 * n :]
    first = upper(*gu.shape)
    half = upper(*h.shape)
    gu_t, h_t = swapped(gu, first), swapped(h, half)
    gate, up = jnp.where(first, gu, gu_t), jnp.where(first, gu_t, gu)
    hidden = jnp.concatenate([jnp.where(half, h, h_t), jnp.where(half, h_t, h)], axis=0)
    sig = jax.nn.sigmoid(gate)
    act_ref[...] = (gate * sig * up).astype(BF16)
    gate_delta = hidden * up * sig * (1.0 + gate * (1.0 - sig))
    up_delta = hidden * gate * sig
    d = jnp.where(first, gate_delta, up_delta).astype(BF16)
    dt = jnp.where(first, up_delta, gate_delta).astype(BF16)
    d_ref[...] = d
    dt_ref[...] = dt
    low = dot(d, gate_ref[0, :w], OVER_COLUMNS) + dot(dt, up_ref[0, :w], OVER_COLUMNS)
    high = dot(dt, gate_ref[0, w:], OVER_COLUMNS) + dot(d, up_ref[0, w:], OVER_COLUMNS)
    back = jnp.where(upper(*low.shape), low, high).astype(BF16)
    own_ref[...] = back[:n]
    other_ref[...] = back[n:]


def gate_up_grad_kernel(counts, *refs):
    gate_ref, up_ref = refs[-2:]
    low = pl.program_id(0) == 0
    rows, d, dt, at = [], [], [], 0
    for count in counts:
        rows.append(received(refs[at : at + count], refs[at + count], 0))
        at += count + 1
    for i in range(len(counts)):
        d.append(refs[at + 2 * i][...].astype(F32))
        dt.append(refs[at + 2 * i + 1][...].astype(F32))
    rows, d, dt = (jnp.concatenate(v, axis=0) for v in (rows, d, dt))
    rows = rows.astype(BF16)
    keep = jnp.logical_xor(upper(*d.shape), jnp.logical_not(low))
    gate = jnp.where(keep, jnp.where(low, d, dt), 0.0).astype(BF16)
    up = jnp.where(keep, jnp.where(low, dt, d), 0.0).astype(BF16)
    gate_ref[0] = dot(rows, gate, OVER_ROWS).astype(BF16)
    up_ref[0] = dot(rows, up, OVER_ROWS).astype(BF16)


def down_grad_kernel(counts, *refs):
    out_ref = refs[-1]
    grads, act, at = [], [], 0
    for count in counts:
        grads.append(received(refs[at : at + count], refs[at + count], 1))
        at += count + 1
    for i in range(len(counts)):
        act.append(refs[at + i][...].astype(F32))
    grads, act = (jnp.concatenate(v, axis=0) for v in (grads, act))
    keep = jnp.logical_xor(upper(*act.shape), pl.program_id(0) == 1)
    act = jnp.where(keep, act, 0.0).astype(BF16)
    out_ref[0] = dot(act, grads.astype(BF16), OVER_ROWS).astype(BF16)


def combine_kernel(count, *refs):
    blocks, (p0_ref, p1_ref), outs = refs[:count], refs[count : count + 2], refs[count + 2 :]
    rows = joined(blocks).astype(BF16)
    lo_ref, hi_ref = columns(outs)
    lo_ref[...] = dot(p0_ref[...], rows, OVER_ROWS).astype(BF16)
    hi_ref[...] = dot(p1_ref[...], rows, OVER_ROWS).astype(BF16)


def body(tokens, output_grad, route_weight, expert_ids, gate_weight, up_weight, down_weight):
    expert_count, fsdp_count = lax.axis_size("expert"), lax.axis_size("fsdp")
    window = expert_count // 2
    tok, slab = tokens.shape
    w = slab // 2
    aligned = w % 128 == 0
    hidden = gate_weight.shape[2]
    rows = window * PAIR
    first_expert = (lax.axis_index("expert") // 2).astype(jnp.int32).reshape(1)

    def shift(v, d):
        perm = [
            (c * 2 + h, ((c + d) % window) * 2 + h) for c in range(window) for h in range(2)
        ]
        return lax.ppermute(v, "expert", perm)

    def other_half(v):
        return lax.ppermute(v, "expert", [(e, e ^ 1) for e in range(expert_count)])

    def reduced(part):
        bit = 1
        while bit < fsdp_count:
            last = bit * 2 >= fsdp_count
            got = lax.ppermute(part, "fsdp", [(f, f ^ bit) for f in range(fsdp_count)])
            if last:
                return part, got
            part = (part.astype(F32) + got.astype(F32)).astype(BF16)
            bit *= 2

    def halves(v):
        return (v,) if aligned else (v[:, :w], v[:, w:])

    def whole(v):
        return pl.BlockSpec(v.shape, lambda i: (0,) * v.ndim)

    space = pl.BlockSpec(memory_space=pltpu.VMEM)
    smem = pl.BlockSpec(memory_space=pltpu.SMEM)
    hbm = pl.BlockSpec(memory_space=pltpu.HBM)
    params = pltpu.CompilerParams(vmem_limit_bytes=16 << 20)
    message = shape((2 * PAIR, w))
    far = halves(tokens) + halves(output_grad)
    placed = pl.pallas_call(
        functools.partial(place_kernel, window, len(far) // 2),
        out_shape=(message,) * window + (shape((rows, tok)),) * 2,
        in_specs=[smem] + [hbm] * (2 + len(far)),
        out_specs=(space,) * (window + 2),
        scratch_shapes=[
            pltpu.VMEM((4, tok, w), BF16),
            pltpu.VMEM(expert_ids.shape[::-1], jnp.int32),
            pltpu.VMEM(route_weight.shape[::-1], F32),
            pltpu.SemaphoreType.DMA((6,)),
        ],
        compiler_params=params,
    )(first_expert, *(in_hbm(v) for v in (expert_ids.T, route_weight.T, *far)))
    p0, p1 = placed[window:]
    arrived = [placed[0]] + [shift(placed[k], k) for k in range(1, window)]
    weights = (gate_weight, up_weight, down_weight)
    gate_w, up_w, down_w = pl.pallas_call(
        load_kernel,
        out_shape=tuple(shape(v.shape) for v in weights),
        in_specs=[hbm] * 3,
        out_specs=(space,) * 3,
        scratch_shapes=[pltpu.SemaphoreType.DMA((3,))],
        compiler_params=params,
    )(*(in_hbm(v) for v in weights))

    chunks = [range(window // 2), range(window // 2, window)]
    counts = tuple(len(chunk) for chunk in chunks)
    own = [[arrived[d] for d in chunk] for chunk in chunks]
    other = [other_half(jnp.concatenate(v, axis=0)) for v in own]
    sums = []
    for i, count in enumerate(counts):
        part = call(
            functools.partial(product_kernel, count),
            shape((3 * count * PAIR, hidden)),
            *own[i], other[i], gate_w, up_w, down_w,
        )
        sums.append(reduced(part))
    deltas, home = [], []
    for i, count in enumerate(counts):
        n = count * PAIR
        *delta, back_own, back_other = call(
            delta_kernel,
            (shape((2 * n, hidden)),) * 3 + (shape((n, w)),) * 2,
            *sums[i], gate_w, up_w,
        )
        deltas.append(delta)
        returned = other_half(back_other)
        back = (back_own.astype(F32) + returned.astype(F32)).astype(BF16)
        for k, d in enumerate(chunks[i]):
            block = back[k * PAIR : (k + 1) * PAIR]
            home.append(shift(block, window - d) if d else block)

    blocks = tuple(v for i in range(len(chunks)) for v in (*own[i], other[i]))
    grad_args = blocks + tuple(v for delta in deltas for v in delta[1:])
    gate_grad, up_grad = pl.pallas_call(
        functools.partial(gate_up_grad_kernel, counts),
        grid=(2,),
        out_shape=(shape(gate_weight.shape),) * 2,
        in_specs=[whole(v) for v in grad_args],
        out_specs=(pl.BlockSpec((1, w, hidden), lambda i: (0, i, 0)),) * 2,
        compiler_params=params,
    )(*grad_args)
    down_args = blocks + tuple(delta[0] for delta in deltas)
    down_grad = pl.pallas_call(
        functools.partial(down_grad_kernel, counts),
        grid=(2,),
        out_shape=shape(down_weight.shape if aligned else (2, hidden, w)),
        in_specs=[whole(v) for v in down_args],
        out_specs=pl.BlockSpec(
            (1, hidden, w), (lambda i: (0, 0, i)) if aligned else (lambda i: (i, 0, 0))
        ),
        compiler_params=params,
    )(*down_args)
    if not aligned:
        down_grad = jnp.concatenate([down_grad[:1], down_grad[1:]], axis=2)
    out = call(
        functools.partial(combine_kernel, len(home)),
        (shape((tok, slab)),) if aligned else (shape((tok, w)),) * 2,
        *home, p0, p1,
    )
    token_grad = out[0] if aligned else jnp.concatenate(out, axis=1)
    return token_grad, gate_grad, up_grad, down_grad


def solution(mesh):
    placed = (
        P("expert", "fsdp"),
        P("expert", "fsdp"),
        P("expert", None),
        P("expert", None),
        P("expert", "fsdp", None),
        P("expert", "fsdp", None),
        P("expert", None, "fsdp"),
    )
    return jax.shard_map(
        body,
        mesh=mesh,
        in_specs=placed,
        out_specs=(
            P("expert", "fsdp"),
            P("expert", "fsdp", None),
            P("expert", "fsdp", None),
            P("expert", None, "fsdp"),
        ),
        check_vma=False,
    )
```

profile of v0, /device:TPU:0, one launch (start us, length us, event | category | flops | bytes accessed | tf_op | source)
XLA Modules:
  0.0 48.9 jit_solution(8648387789362681257)
XLA Ops:
  0.6 1.9 %shard_map.102 = (bf16[48,896]{1,0:T(8,128)(2,1)S(1)}, bf16[48,896]{1,0:T(8,128)(2,1)S(1)}, bf16[48,896]{1,0:T(8,128)(2,1)S(1)}, bf16[48,896]{1,0:T(8,128)(2,1)S...) custom-call(s32[1]{0:T(128)} %bitcast.refs_0_, s32[8,256]{1,0:T(8,128)} %bitcast.3, f32[8,256]{1,0:T(8,128)} %bitcast.4, ...), custom_call_target="tpu_custom_call" | custom-call | tf_op jit(solution)/shard_map/pallas_call | solution.py:259
  2.5 4.1 %collective-permute-start.6 = (bf16[48,896]{1,0:T(8,128)(2,1)S(1)}, bf16[48,896]{1,0:T(8,128)(2,1)S(1)}, u32[]{:S(2)}, u32[]{:S(2)}) collective-permute-start(bf16[48,896]{1,0:T(8,128)(2,1)S(1)} %get-tuple-element.32), channel_id=1, source_target_pairs={{0,16},{4,20},{8,24},{12,28},{16,0},{20,4},{24,8},{28,12},{1,17},{... | collective-permute-start | bytes 258056 | tf_op jit(solution)/shard_map/ppermute | solution.py:232
  6.6 1.4 %collective-permute-start.7 = (bf16[48,896]{1,0:T(8,128)(2,1)S(1)}, bf16[48,896]{1,0:T(8,128)(2,1)S(1)}, u32[]{:S(2)}, u32[]{:S(2)}) collective-permute-start(bf16[48,896]{1,0:T(8,128)(2,1)S(1)} %get-tuple-element.33), channel_id=1, source_target_pairs={{0,24},{4,28},{8,0},{12,4},{16,8},{20,12},{24,16},{28,20},{1,25},{... | collective-permute-start | bytes 258056 | tf_op jit(solution)/shard_map/ppermute | solution.py:232
  8.0 0.7 %collective-permute-start = (bf16[48,896]{1,0:T(8,128)(2,1)S(1)}, bf16[48,896]{1,0:T(8,128)(2,1)S(1)}, u32[]{:S(2)}, u32[]{:S(2)}) collective-permute-start(bf16[48,896]{1,0:T(8,128)(2,1)S(1)} %get-tuple-element.26), channel_id=1, source_target_pairs={{0,8},{4,12},{8,16},{12,20},{16,24},{20,28},{24,0},{28,4},{1,9},{5... | collective-permute-start | bytes 258056 | tf_op jit(solution)/shard_map/ppermute | solution.py:232
  8.7 2.8 %collective-permute-done.6.refs_0_.refs_3_ = bf16[48,896]{1,0:T(8,128)(2,1)S(1)} collective-permute-done((bf16[48,896]{1,0:T(8,128)(2,1)S(1)}, bf16[48,896]{1,0:T(8,128)(2,1)S(1)}, u32[]{:S(2)}, u32[]{:S(2)}) %collective-permute-start.6) | collective-permute-done | bytes 86048 | tf_op jit(solution)/shard_map/ppermute | solution.py:232
  11.4 0.0 collective-permute-done.7.refs_1_.refs_4_
  11.5 1.9 %collective-permute-start.8 = (bf16[96,896]{1,0:T(8,128)(2,1)S(1)}, bf16[96,896]{1,0:T(8,128)(2,1)S(1)}, u32[]{:S(2)}, u32[]{:S(2)}) collective-permute-start(bf16[96,896]{1,0:T(8,128)(2,1)S(1)} %pad_maximum_fusion.1), channel_id=1, source_target_pairs={{0,4},{4,0},{8,12},{12,8},{16,20},{20,16},{24,28},{28,24},{1,5},{5... | collective-permute-start | bytes 516104 | tf_op jit(solution)/shard_map/ppermute | solution.py:235
  13.4 0.9 %collective-permute-done.refs_1_ = bf16[48,896]{1,0:T(8,128)(2,1)S(1)} collective-permute-done((bf16[48,896]{1,0:T(8,128)(2,1)S(1)}, bf16[48,896]{1,0:T(8,128)(2,1)S(1)}, u32[]{:S(2)}, u32[]{:S(2)}) %collective-permute-start) | collective-permute-done | bytes 86048 | tf_op jit(solution)/shard_map/ppermute | solution.py:232
  14.3 1.5 %collective-permute-start.1 = (bf16[96,896]{1,0:T(8,128)(2,1)S(1)}, bf16[96,896]{1,0:T(8,128)(2,1)S(1)}, u32[]{:S(2)}, u32[]{:S(2)}) collective-permute-start(bf16[96,896]{1,0:T(8,128)(2,1)S(1)} %pad_maximum_fusion), channel_id=1, source_target_pairs={{0,4},{4,0},{8,12},{12,8},{16,20},{20,16},{24,28},{28,24},{1,5},{5... | collective-permute-start | bytes 516104 | tf_op jit(solution)/shard_map/ppermute | solution.py:235
  15.8 2.6 %shard_map.103 = (bf16[1,1792,512]{2,1,0:T(8,128)(2,1)S(1)}, bf16[1,1792,512]{2,1,0:T(8,128)(2,1)S(1)}, bf16[1,512,1792]{2,1,0:T(8,128)(2,1)S(1)}) custom-call(bf16[1,1792,512]{2,1,0:T(8,128)(2,1)} %refs_0_.1, bf16[1,1792,512]{2,1,0:T(8,128)(2,1)} %refs_1_.1, bf16[1,512,1792]{2,1,0:T(8,128)(2,1)} %refs_2_.1), custom_call_target="tpu_custom_call" | custom-call | tf_op jit(solution)/shard_map/pallas_call | solution.py:275
  18.5 0.0 collective-permute-done.8.refs_2_.refs_5_
  18.5 1.3 %shard_map.106 = bf16[144,512]{1,0:T(8,128)(2,1)S(1)} custom-call(bf16[48,896]{1,0:T(8,128)(2,1)S(1)} %collective-permute-done.6.refs_0_.refs_3_, bf16[48,896]{1,0:T(8,128)(2,1)S(1)} %collective-permute-done.7.refs_1_.refs_4_, bf16[96,896]{1,0:T(8,128)(2,1)S(1)} %collective-permute-done.8.refs_2_.refs_5_, ...), custom_call_target="tpu_custom_call" | custom-call | tf_op jit(solution)/shard_map/pallas_call | solution.py:36
  19.8 0.1 collective-permute-start.9
  19.9 0.7 %collective-permute-done.1.refs_2_ = bf16[96,896]{1,0:T(8,128)(2,1)S(1)} collective-permute-done((bf16[96,896]{1,0:T(8,128)(2,1)S(1)}, bf16[96,896]{1,0:T(8,128)(2,1)S(1)}, u32[]{:S(2)}, u32[]{:S(2)}) %collective-permute-start.1) | collective-permute-done | bytes 172064 | tf_op jit(solution)/shard_map/ppermute | solution.py:235
  20.6 1.3 %shard_map.104 = bf16[144,512]{1,0:T(8,128)(2,1)S(1)} custom-call(bf16[48,896]{1,0:T(8,128)(2,1)S(1)} %get-tuple-element.25.refs_0_, bf16[48,896]{1,0:T(8,128)(2,1)S(1)} %collective-permute-done.refs_1_, bf16[96,896]{1,0:T(8,128)(2,1)S(1)} %collective-permute-done.1.refs_2_, bf16[1,1792,512]{2,1,0:T(8,128)(2,1)S(1)} %get-tuple-element.27.refs_3_.gate_ref, ...), custom_call_target="tpu_custom_call" | custom-call | tf_op jit(solution)/shard_map/pallas_call | solution.py:36
  21.9 0.1 collective-permute-start.2
  22.0 0.0 collective-permute-done.9
  22.1 1.9 %collective-permute-start.10 = (bf16[144,512]{1,0:T(8,128)(2,1)S(1)}, bf16[144,512]{1,0:T(8,128)(2,1)S(1)}, u32[]{:S(2)}, u32[]{:S(2)}) collective-permute-start(bf16[144,512]{1,0:T(8,128)(2,1)S(1)} %add_convert_fusion.a_ref), channel_id=1, source_target_pairs={{0,2},{1,3},{2,0},{3,1},{4,6},{5,7},{6,4},{7,5},{8,10},{9,11},{10,... | collective-permute-start | bytes 442376 | tf_op jit(solution)/shard_map/ppermute | solution.py:241
  24.0 0.0 collective-permute-done.2
  24.0 1.3 %collective-permute-start.3 = (bf16[144,512]{1,0:T(8,128)(2,1)S(1)}, bf16[144,512]{1,0:T(8,128)(2,1)S(1)}, u32[]{:S(2)}, u32[]{:S(2)}) collective-permute-start(bf16[144,512]{1,0:T(8,128)(2,1)S(1)} %add_convert_fusion.1.a_ref), channel_id=1, source_target_pairs={{0,2},{1,3},{2,0},{3,1},{4,6},{5,7},{6,4},{7,5},{8,10},{9,11},{10,... | collective-permute-start | bytes 442376 | tf_op jit(solution)/shard_map/ppermute | solution.py:241
  25.3 3.5 %collective-permute-done.10.b_ref = bf16[144,512]{1,0:T(8,128)(2,1)S(1)} collective-permute-done((bf16[144,512]{1,0:T(8,128)(2,1)S(1)}, bf16[144,512]{1,0:T(8,128)(2,1)S(1)}, u32[]{:S(2)}, u32[]{:S(2)}) %collective-permute-start.10) | collective-permute-done | bytes 147488 | tf_op jit(solution)/shard_map/ppermute | solution.py:241
  28.8 1.2 %shard_map.107 = (bf16[96,512]{1,0:T(8,128)(2,1)S(1)}, bf16[96,512]{1,0:T(8,128)(2,1)S(1)}, bf16[96,512]{1,0:T(8,128)(2,1)S(1)}, bf16[48,896]{1,0:T(8,128)(2,1)S(1)}, bf16[48,896]{1,0:T(8,128)(2,1)S(1)}) custom-call(bf16[144,512]{1,0:T(8,128)(2,1)S(1)} %add_convert_fusion.a_ref, bf16[144,512]{1,0:T(8,128)(2,1)S(1)} %collective-permute-done.10.b_ref, ...), custom_call_target="tpu_custom_call" | custom-call | tf_op jit(solution)/shard_map/pallas_call | solution.py:36
  30.1 1.9 %collective-permute-start.11 = (bf16[48,896]{1,0:T(8,128)(2,1)S(1)}, bf16[48,896]{1,0:T(8,128)(2,1)S(1)}, u32[]{:S(2)}, u32[]{:S(2)}) collective-permute-start(bf16[48,896]{1,0:T(8,128)(2,1)S(1)} %get-tuple-element.35), channel_id=1, source_target_pairs={{0,4},{4,0},{8,12},{12,8},{16,20},{20,16},{24,28},{28,24},{1,5},{5... | collective-permute-start | bytes 258056 | tf_op jit(solution)/shard_map/ppermute | solution.py:235
  32.0 0.0 collective-permute-done.3.b_ref
  32.0 1.2 %shard_map.105 = (bf16[96,512]{1,0:T(8,128)(2,1)S(1)}, bf16[96,512]{1,0:T(8,128)(2,1)S(1)}, bf16[96,512]{1,0:T(8,128)(2,1)S(1)}, bf16[48,896]{1,0:T(8,128)(2,1)S(1)}, bf16[48,896]{1,0:T(8,128)(2,1)S(1)}) custom-call(bf16[144,512]{1,0:T(8,128)(2,1)S(1)} %add_convert_fusion.1.a_ref, bf16[144,512]{1,0:T(8,128)(2,1)S(1)} %collective-permute-done.3.b_ref, ...), custom_call_target="tpu_custom_call" | custom-call | tf_op jit(solution)/shard_map/pallas_call | solution.py:36
  33.2 1.4 %collective-permute-start.4 = (bf16[48,896]{1,0:T(8,128)(2,1)S(1)}, bf16[48,896]{1,0:T(8,128)(2,1)S(1)}, u32[]{:S(2)}, u32[]{:S(2)}) collective-permute-start(bf16[48,896]{1,0:T(8,128)(2,1)S(1)} %get-tuple-element.31), channel_id=1, source_target_pairs={{0,4},{4,0},{8,12},{12,8},{16,20},{20,16},{24,28},{28,24},{1,5},{5... | collective-permute-start | bytes 258056 | tf_op jit(solution)/shard_map/ppermute | solution.py:235
  34.6 0.0 collective-permute-done.11
  34.7 3.1 %collective-permute-start.12 = (bf16[24,896]{1,0:T(8,128)(2,1)S(1)}, bf16[24,896]{1,0:T(8,128)(2,1)S(1)}, u32[]{:S(2)}, u32[]{:S(2)}) collective-permute-start(bf16[24,896]{1,0:T(8,128)(2,1)S(1)} %get-tuple-element.47), channel_id=1, source_target_pairs={{0,16},{4,20},{8,24},{12,28},{16,0},{20,4},{24,8},{28,12},{1,17},{... | collective-permute-start | bytes 129032 | tf_op jit(solution)/shard_map/ppermute | solution.py:232
  37.8 3.3 %collective-permute-start.13 = (bf16[24,896]{1,0:T(8,128)(2,1)S(1)}, bf16[24,896]{1,0:T(8,128)(2,1)S(1)}, u32[]{:S(2)}, u32[]{:S(2)}) collective-permute-start(bf16[24,896]{1,0:T(8,128)(2,1)S(1)} %get-tuple-element.46), channel_id=1, source_target_pairs={{0,8},{4,12},{8,16},{12,20},{16,24},{20,28},{24,0},{28,4},{1,9},{5... | collective-permute-start | bytes 129032 | tf_op jit(solution)/shard_map/ppermute | solution.py:232
  41.1 0.0 collective-permute-done.4
  41.1 2.2 %collective-permute-start.5 = (bf16[24,896]{1,0:T(8,128)(2,1)S(1)}, bf16[24,896]{1,0:T(8,128)(2,1)S(1)}, u32[]{:S(2)}, u32[]{:S(2)}) collective-permute-start(bf16[24,896]{1,0:T(8,128)(2,1)S(1)} %get-tuple-element.48), channel_id=1, source_target_pairs={{0,24},{4,28},{8,0},{12,4},{16,8},{20,12},{24,16},{28,20},{1,25},{... | collective-permute-start | bytes 129032 | tf_op jit(solution)/shard_map/ppermute | solution.py:232
  43.3 1.9 %shard_map.110 = bf16[1,512,1792]{2,1,0:T(8,128)(2,1)} custom-call(bf16[48,896]{1,0:T(8,128)(2,1)S(1)} %get-tuple-element.25.refs_0_, bf16[48,896]{1,0:T(8,128)(2,1)S(1)} %collective-permute-done.refs_1_, bf16[96,896]{1,0:T(8,128)(2,1)S(1)} %collective-permute-done.1.refs_2_, bf16[48,896]{1,0:T(8,128)(2,1)S(1)} %collective-permute-done.6.refs_0_.refs_3_, ...), custom_call_target="tpu_custom_call" | custom-call | tf_op jit(solution)/shard_map/pallas_call | solution.py:322
  45.2 2.4 %shard_map.109 = (bf16[1,1792,512]{2,1,0:T(8,128)(2,1)}, bf16[1,1792,512]{2,1,0:T(8,128)(2,1)}) custom-call(bf16[48,896]{1,0:T(8,128)(2,1)S(1)} %get-tuple-element.25.refs_0_, bf16[48,896]{1,0:T(8,128)(2,1)S(1)} %collective-permute-done.refs_1_, bf16[96,896]{1,0:T(8,128)(2,1)S(1)} %collective-permute-done.1.refs_2_, ...), custom_call_target="tpu_custom_call" | custom-call | tf_op jit(solution)/shard_map/pallas_call | solution.py:313
  47.6 0.0 collective-permute-done.12.refs_2_
  47.6 0.0 collective-permute-done.13.refs_3_
  47.6 0.0 collective-permute-done.5.refs_1_
  47.6 1.3 %shard_map.108 = bf16[256,1792]{1,0:T(8,128)(2,1)} custom-call(bf16[24,896]{1,0:T(8,128)(2,1)S(1)} %get-tuple-element.49.refs_0_, bf16[24,896]{1,0:T(8,128)(2,1)S(1)} %collective-permute-done.5.refs_1_, bf16[24,896]{1,0:T(8,128)(2,1)S(1)} %collective-permute-done.12.refs_2_, bf16[24,896]{1,0:T(8,128)(2,1)S(1)} %collective-permute-done.13.refs_3_, ...), custom_call_target="tpu_custom_call" | custom-call | tf_op jit(solution)/shard_map/pallas_call | solution.py:36
  (8 shorter events, 0.2 us)
Async XLA Ops:
  2.5 8.9 %collective-permute-start.6 = (bf16[48,896]{1,0:T(8,128)(2,1)S(1)}, bf16[48,896]{1,0:T(8,128)(2,1)S(1)}, u32[]{:S(2)}, u32[]{:S(2)}) collective-permute-start(bf16[48,896]{1,0:T(8,128)(2,1)S(1)} %get-tuple-element.32), channel_id=1, source_target_pairs={{0,16},{4,20},{8,24},{12,28},{16,0},{20,4},{24,8},{28,12},{1,17},{... | collective-permute-start | bytes 258056 | tf_op jit(solution)/shard_map/ppermute | solution.py:232
  6.6 4.8 %collective-permute-start.7 = (bf16[48,896]{1,0:T(8,128)(2,1)S(1)}, bf16[48,896]{1,0:T(8,128)(2,1)S(1)}, u32[]{:S(2)}, u32[]{:S(2)}) collective-permute-start(bf16[48,896]{1,0:T(8,128)(2,1)S(1)} %get-tuple-element.33), channel_id=1, source_target_pairs={{0,24},{4,28},{8,0},{12,4},{16,8},{20,12},{24,16},{28,20},{1,25},{... | collective-permute-start | bytes 258056 | tf_op jit(solution)/shard_map/ppermute | solution.py:232
  8.0 6.3 %collective-permute-start = (bf16[48,896]{1,0:T(8,128)(2,1)S(1)}, bf16[48,896]{1,0:T(8,128)(2,1)S(1)}, u32[]{:S(2)}, u32[]{:S(2)}) collective-permute-start(bf16[48,896]{1,0:T(8,128)(2,1)S(1)} %get-tuple-element.26), channel_id=1, source_target_pairs={{0,8},{4,12},{8,16},{12,20},{16,24},{20,28},{24,0},{28,4},{1,9},{5... | collective-permute-start | bytes 258056 | tf_op jit(solution)/shard_map/ppermute | solution.py:232
  11.5 7.0 %collective-permute-start.8 = (bf16[96,896]{1,0:T(8,128)(2,1)S(1)}, bf16[96,896]{1,0:T(8,128)(2,1)S(1)}, u32[]{:S(2)}, u32[]{:S(2)}) collective-permute-start(bf16[96,896]{1,0:T(8,128)(2,1)S(1)} %pad_maximum_fusion.1), channel_id=1, source_target_pairs={{0,4},{4,0},{8,12},{12,8},{16,20},{20,16},{24,28},{28,24},{1,5},{5... | collective-permute-start | bytes 516104 | tf_op jit(solution)/shard_map/ppermute | solution.py:235
  14.3 6.3 %collective-permute-start.1 = (bf16[96,896]{1,0:T(8,128)(2,1)S(1)}, bf16[96,896]{1,0:T(8,128)(2,1)S(1)}, u32[]{:S(2)}, u32[]{:S(2)}) collective-permute-start(bf16[96,896]{1,0:T(8,128)(2,1)S(1)} %pad_maximum_fusion), channel_id=1, source_target_pairs={{0,4},{4,0},{8,12},{12,8},{16,20},{20,16},{24,28},{28,24},{1,5},{5... | collective-permute-start | bytes 516104 | tf_op jit(solution)/shard_map/ppermute | solution.py:235
  19.8 2.2 %collective-permute-start.9 = (bf16[144,512]{1,0:T(8,128)(2,1)S(1)}, bf16[144,512]{1,0:T(8,128)(2,1)S(1)}, u32[]{:S(2)}, u32[]{:S(2)}) collective-permute-start(bf16[144,512]{1,0:T(8,128)(2,1)S(1)} %shard_map.106), channel_id=1, source_target_pairs={{0,1},{1,0},{2,3},{3,2},{4,5},{5,4},{6,7},{7,6},{8,9},{9,8},{10,11... | collective-permute-start | bytes 442376 | tf_op jit(solution)/shard_map/ppermute | solution.py:241
  21.9 2.1 %collective-permute-start.2 = (bf16[144,512]{1,0:T(8,128)(2,1)S(1)}, bf16[144,512]{1,0:T(8,128)(2,1)S(1)}, u32[]{:S(2)}, u32[]{:S(2)}) collective-permute-start(bf16[144,512]{1,0:T(8,128)(2,1)S(1)} %shard_map.104), channel_id=1, source_target_pairs={{0,1},{1,0},{2,3},{3,2},{4,5},{5,4},{6,7},{7,6},{8,9},{9,8},{10,11... | collective-permute-start | bytes 442376 | tf_op jit(solution)/shard_map/ppermute | solution.py:241
  22.1 6.8 %collective-permute-start.10 = (bf16[144,512]{1,0:T(8,128)(2,1)S(1)}, bf16[144,512]{1,0:T(8,128)(2,1)S(1)}, u32[]{:S(2)}, u32[]{:S(2)}) collective-permute-start(bf16[144,512]{1,0:T(8,128)(2,1)S(1)} %add_convert_fusion.a_ref), channel_id=1, source_target_pairs={{0,2},{1,3},{2,0},{3,1},{4,6},{5,7},{6,4},{7,5},{8,10},{9,11},{10,... | collective-permute-start | bytes 442376 | tf_op jit(solution)/shard_map/ppermute | solution.py:241
  24.0 7.9 %collective-permute-start.3 = (bf16[144,512]{1,0:T(8,128)(2,1)S(1)}, bf16[144,512]{1,0:T(8,128)(2,1)S(1)}, u32[]{:S(2)}, u32[]{:S(2)}) collective-permute-start(bf16[144,512]{1,0:T(8,128)(2,1)S(1)} %add_convert_fusion.1.a_ref), channel_id=1, source_target_pairs={{0,2},{1,3},{2,0},{3,1},{4,6},{5,7},{6,4},{7,5},{8,10},{9,11},{10,... | collective-permute-start | bytes 442376 | tf_op jit(solution)/shard_map/ppermute | solution.py:241
  30.1 4.6 %collective-permute-start.11 = (bf16[48,896]{1,0:T(8,128)(2,1)S(1)}, bf16[48,896]{1,0:T(8,128)(2,1)S(1)}, u32[]{:S(2)}, u32[]{:S(2)}) collective-permute-start(bf16[48,896]{1,0:T(8,128)(2,1)S(1)} %get-tuple-element.35), channel_id=1, source_target_pairs={{0,4},{4,0},{8,12},{12,8},{16,20},{20,16},{24,28},{28,24},{1,5},{5... | collective-permute-start | bytes 258056 | tf_op jit(solution)/shard_map/ppermute | solution.py:235
  33.2 7.9 %collective-permute-start.4 = (bf16[48,896]{1,0:T(8,128)(2,1)S(1)}, bf16[48,896]{1,0:T(8,128)(2,1)S(1)}, u32[]{:S(2)}, u32[]{:S(2)}) collective-permute-start(bf16[48,896]{1,0:T(8,128)(2,1)S(1)} %get-tuple-element.31), channel_id=1, source_target_pairs={{0,4},{4,0},{8,12},{12,8},{16,20},{20,16},{24,28},{28,24},{1,5},{5... | collective-permute-start | bytes 258056 | tf_op jit(solution)/shard_map/ppermute | solution.py:235
  34.7 12.9 %collective-permute-start.12 = (bf16[24,896]{1,0:T(8,128)(2,1)S(1)}, bf16[24,896]{1,0:T(8,128)(2,1)S(1)}, u32[]{:S(2)}, u32[]{:S(2)}) collective-permute-start(bf16[24,896]{1,0:T(8,128)(2,1)S(1)} %get-tuple-element.47), channel_id=1, source_target_pairs={{0,16},{4,20},{8,24},{12,28},{16,0},{20,4},{24,8},{28,12},{1,17},{... | collective-permute-start | bytes 129032 | tf_op jit(solution)/shard_map/ppermute | solution.py:232
  37.8 9.8 %collective-permute-start.13 = (bf16[24,896]{1,0:T(8,128)(2,1)S(1)}, bf16[24,896]{1,0:T(8,128)(2,1)S(1)}, u32[]{:S(2)}, u32[]{:S(2)}) collective-permute-start(bf16[24,896]{1,0:T(8,128)(2,1)S(1)} %get-tuple-element.46), channel_id=1, source_target_pairs={{0,8},{4,12},{8,16},{12,20},{16,24},{20,28},{24,0},{28,4},{1,9},{5... | collective-permute-start | bytes 129032 | tf_op jit(solution)/shard_map/ppermute | solution.py:232
  41.1 6.4 %collective-permute-start.5 = (bf16[24,896]{1,0:T(8,128)(2,1)S(1)}, bf16[24,896]{1,0:T(8,128)(2,1)S(1)}, u32[]{:S(2)}, u32[]{:S(2)}) collective-permute-start(bf16[24,896]{1,0:T(8,128)(2,1)S(1)} %get-tuple-element.48), channel_id=1, source_target_pairs={{0,24},{4,28},{8,0},{12,4},{16,8},{20,12},{24,16},{28,20},{1,25},{... | collective-permute-start | bytes 129032 | tf_op jit(solution)/shard_map/ppermute | solution.py:232
where the time goes:
time: 49.1 us; the launch traced here: 48.9 us
  starting transfers between devices  24.9 us (51%)
  Pallas kernels  15.2 us (31%)
  waiting for transfers between devices  7.97 us (16%)
  between operations  0.76 us (2%)
    ppermute x6, starting transfers between devices, shift(): return lax.ppermute(v, 'expert', perm)  14.7 us
    ppermute x4, starting transfers between devices, other_half(): return lax.ppermute(v, 'expert', [(e, e ^ 1) for e in range(expert_count)])  6.78 us
    pallas_call x5, Pallas kernels, call(): pl.pallas_call(kernel, out_shape=outs, in_specs=[space] * len(args), out_...  6.41 us
    ppermute x6, waiting for transfers between devices, shift(): return lax.ppermute(v, 'expert', perm)  3.71 us
    ppermute x4, waiting for transfers between devices, reduced(): got = lax.ppermute(part, 'fsdp', [(f, f ^ bit) for f in range(fsdp_count)])  3.52 us
    ppermute x4, starting transfers between devices, reduced(): got = lax.ppermute(part, 'fsdp', [(f, f ^ bit) for f in range(fsdp_count)])  3.38 us
    pallas_call x1, Pallas kernels, body(): pl.pallas_call(load_kernel, out_shape=tuple((shape(v.shape) for v in weig...  2.63 us
    pallas_call x1, Pallas kernels, body(): pl.pallas_call(functools.partial(gate_up_grad_kernel, counts), grid=(2,),...  2.38 us
  transfers between devices with their start and end apart: 14, of which 4 were waited for; matrix products, arithmetic and copies ran while one was open for 0% of the time, Pallas kernels for 24%

commit v1 on v0

--- a/solution.py
+++ b/solution.py
@@ -71,26 +71,26 @@
     )]
     for copy in copies:
         copy.start()
-    copies[0].wait()
-    copies[1].wait()
     top, tok = ids_ref.shape
     dims = (window, PAIR, tok)
     rows = window * PAIR
-    expert = lax.broadcasted_iota(jnp.int32, dims, 0) + e_ref[0]
-    expert = jnp.where(expert >= window, expert - window, expert)
+    expert = lax.broadcasted_iota(jnp.int32, dims, 0) ^ e_ref[0]
     slot = lax.broadcasted_iota(jnp.int32, dims, 1).astype(F32).reshape(rows, tok)
+    before = lax.broadcasted_iota(jnp.int32, (tok, tok), 0) < lax.broadcasted_iota(
+        jnp.int32, (tok, tok), 1
+    )
+    before = before.astype(F32).astype(BF16)
     hit = jnp.zeros(dims, F32)
     weight = jnp.zeros(dims, F32)
+    copies[0].wait()
+    copies[1].wait()
     for k in range(top):
         same = ids_ref[k : k + 1, :][None] == expert
         hit = jnp.where(same, 1.0, hit)
         weight = jnp.where(same, w_ref[k : k + 1, :][None], weight)
     hit = hit.reshape(rows, tok)
     weight = weight.reshape(rows, tok)
-    before = lax.broadcasted_iota(jnp.int32, (tok, tok), 0) < lax.broadcasted_iota(
-        jnp.int32, (tok, tok), 1
-    )
-    rank = dot(hit.astype(BF16), before.astype(F32).astype(BF16))
+    rank = dot(hit.astype(BF16), before)
     p0 = jnp.where(rank == slot, hit, 0.0)
     p1 = jnp.where(rank + CAP == slot, hit, 0.0)
     scale = jnp.sum((p0 + p1) * weight, axis=1, keepdims=True)
@@ -208,11 +208,16 @@
 
 
 def combine_kernel(count, *refs):
-    blocks, (p0_ref, p1_ref), outs = refs[:count], refs[count : count + 2], refs[count + 2 :]
+    blocks, p_refs = refs[:count], refs[count : count + 2]
+    outs, (held, sems) = refs[count + 2 : -2], refs[-2:]
     rows = joined(blocks).astype(BF16)
-    lo_ref, hi_ref = columns(outs)
-    lo_ref[...] = dot(p0_ref[...], rows, OVER_ROWS).astype(BF16)
-    hi_ref[...] = dot(p1_ref[...], rows, OVER_ROWS).astype(BF16)
+    copies = []
+    for i, (p_ref, out) in enumerate(zip(p_refs, columns(outs))):
+        held[i] = dot(p_ref[...], rows, OVER_ROWS).astype(BF16)
+        copies.append(pltpu.make_async_copy(held.at[i], out, sems.at[i]))
+        copies[-1].start()
+    for copy in copies:
+        copy.wait()
 
 
 def body(tokens, output_grad, route_weight, expert_ids, gate_weight, up_weight, down_weight):
@@ -223,12 +228,10 @@
     aligned = w % 128 == 0
     hidden = gate_weight.shape[2]
     rows = window * PAIR
-    first_expert = (lax.axis_index("expert") // 2).astype(jnp.int32).reshape(1)
-
-    def shift(v, d):
-        perm = [
-            (c * 2 + h, ((c + d) % window) * 2 + h) for c in range(window) for h in range(2)
-        ]
+    first_expert = lax.shift_right_logical(lax.axis_index("expert"), 1).reshape(1)
+
+    def across(v, d):
+        perm = [(c * 2 + h, (c ^ d) * 2 + h) for c in range(window) for h in range(2)]
         return lax.ppermute(v, "expert", perm)
 
     def other_half(v):
@@ -270,14 +273,14 @@
         compiler_params=params,
     )(first_expert, *(in_hbm(v) for v in (expert_ids.T, route_weight.T, *far)))
     p0, p1 = placed[window:]
-    arrived = [placed[0]] + [shift(placed[k], k) for k in range(1, window)]
-    weights = (gate_weight, up_weight, down_weight)
-    gate_w, up_w, down_w = pl.pallas_call(
+    arrived = [placed[0]] + [across(placed[k], k) for k in range(1, window)]
+    weights = (up_weight, down_weight)
+    up_w, down_w = pl.pallas_call(
         load_kernel,
         out_shape=tuple(shape(v.shape) for v in weights),
-        in_specs=[hbm] * 3,
-        out_specs=(space,) * 3,
-        scratch_shapes=[pltpu.SemaphoreType.DMA((3,))],
+        in_specs=[hbm] * 2,
+        out_specs=(space,) * 2,
+        scratch_shapes=[pltpu.SemaphoreType.DMA((2,))],
         compiler_params=params,
     )(*(in_hbm(v) for v in weights))
 
@@ -290,23 +293,23 @@
         part = call(
             functools.partial(product_kernel, count),
             shape((3 * count * PAIR, hidden)),
-            *own[i], other[i], gate_w, up_w, down_w,
+            *own[i], other[i], gate_weight, up_w, down_w,
         )
         sums.append(reduced(part))
-    deltas, home = [], []
+    deltas, home = [], [None] * window
     for i, count in enumerate(counts):
         n = count * PAIR
         *delta, back_own, back_other = call(
             delta_kernel,
             (shape((2 * n, hidden)),) * 3 + (shape((n, w)),) * 2,
-            *sums[i], gate_w, up_w,
+            *sums[i], gate_weight, up_w,
         )
         deltas.append(delta)
         returned = other_half(back_other)
         back = (back_own.astype(F32) + returned.astype(F32)).astype(BF16)
         for k, d in enumerate(chunks[i]):
             block = back[k * PAIR : (k + 1) * PAIR]
-            home.append(shift(block, window - d) if d else block)
+            home[d] = across(block, d) if d else block
 
     blocks = tuple(v for i in range(len(chunks)) for v in (*own[i], other[i]))
     grad_args = blocks + tuple(v for delta in deltas for v in delta[1:])
@@ -331,11 +334,15 @@
     )(*down_args)
     if not aligned:
         down_grad = jnp.concatenate([down_grad[:1], down_grad[1:]], axis=2)
-    out = call(
+    out_shape = (shape((tok, slab)),) if aligned else (shape((tok, w)),) * 2
+    out = pl.pallas_call(
         functools.partial(combine_kernel, len(home)),
-        (shape((tok, slab)),) if aligned else (shape((tok, w)),) * 2,
-        *home, p0, p1,
-    )
+        out_shape=out_shape,
+        in_specs=[space] * (len(home) + 2),
+        out_specs=(hbm,) * len(out_shape),
+        scratch_shapes=[pltpu.VMEM((2, tok, w), BF16), pltpu.SemaphoreType.DMA((2,))],
+        compiler_params=params,
+    )(*home, p0, p1)
     token_grad = out[0] if aligned else jnp.concatenate(out, axis=1)
     return token_grad, gate_grad, up_grad, down_grad
 

time: 49.1 us -> 48.8 us (level)
  waiting for transfers between devices: 7.97 us -> 12.3 us
  starting transfers between devices: 24.9 us -> 20.8 us
  Pallas kernels: 15.2 us -> 14.5 us
    ppermute x6, starting transfers between devices: 14.7 us -> 12.5 us  [across(): return lax.ppermute(v, 'expert', perm)]
    ppermute x6, waiting for transfers between devices: 3.71 us -> 5.92 us  [across(): return lax.ppermute(v, 'expert', perm)]
    ppermute x4, waiting for transfers between devices: 0.74 us -> 2.46 us  [other_half(): return lax.ppermute(v, 'expert', [(e, e ^ 1) for e in range(expert_count)])]
    ppermute x4, starting transfers between devices: 6.78 us -> 5.32 us  [other_half(): return lax.ppermute(v, 'expert', [(e, e ^ 1) for e in range(expert_count)])]
    pallas_call x5 -> x4, Pallas kernels: 6.41 us -> 5.08 us  [call(): pl.pallas_call(kernel, out_shape=outs, in_specs=[space] * len(args), out_...]
    pallas_call x0 -> x1, Pallas kernels: none -> 1.26 us  [body(): pl.pallas_call(functools.partial(combine_kernel, len(home)), out_shape=ou...]
    pallas_call x1, Pallas kernels: 2.63 us -> 2.1 us  [body(): pl.pallas_call(load_kernel, out_shape=tuple((shape(v.shape) for v in weig...]
  transfers between devices with their start and end apart: 14 -> 14, of which waited for: 4 -> 7; matrix products, arithmetic and copies ran while one was open for 0% -> 0% of each run, Pallas kernels for 24% -> 24%
where the time goes in v1:
time: 48.8 us; the launch traced here: 48.6 us
  starting transfers between devices  20.8 us (43%)
  Pallas kernels  14.5 us (30%)
  waiting for transfers between devices  12.3 us (25%)
  between operations  0.73 us (1%)
    ppermute x6, starting transfers between devices, across(): return lax.ppermute(v, 'expert', perm)  12.5 us
    ppermute x6, waiting for transfers between devices, across(): return lax.ppermute(v, 'expert', perm)  5.92 us
    ppermute x4, starting transfers between devices, other_half(): return lax.ppermute(v, 'expert', [(e, e ^ 1) for e in range(expert_count)])  5.32 us
    pallas_call x4, Pallas kernels, call(): pl.pallas_call(kernel, out_shape=outs, in_specs=[space] * len(args), out_...  5.08 us
    ppermute x4, waiting for transfers between devices, reduced(): got = lax.ppermute(part, 'fsdp', [(f, f ^ bit) for f in range(fsdp_count)])  3.9 us
    ppermute x4, starting transfers between devices, reduced(): got = lax.ppermute(part, 'fsdp', [(f, f ^ bit) for f in range(fsdp_count)])  3.04 us
    ppermute x4, waiting for transfers between devices, other_half(): return lax.ppermute(v, 'expert', [(e, e ^ 1) for e in range(expert_count)])  2.46 us
    pallas_call x1, Pallas kernels, body(): pl.pallas_call(functools.partial(gate_up_grad_kernel, counts), grid=(2,),...  2.39 us
  transfers between devices with their start and end apart: 14, of which 7 were waited for; matrix products, arithmetic and copies ran while one was open for 0% of the time, Pallas kernels for 24%

profile of v1, /device:TPU:0, one launch (start us, length us, event | category | flops | bytes accessed | tf_op | source)
XLA Modules:
  0.0 48.6 jit_solution(5092294831638048910)
XLA Ops:
  0.6 1.9 %shard_map.102 = (bf16[48,896]{1,0:T(8,128)(2,1)S(1)}, bf16[48,896]{1,0:T(8,128)(2,1)S(1)}, bf16[48,896]{1,0:T(8,128)(2,1)S(1)}, bf16[48,896]{1,0:T(8,128)(2,1)S...) custom-call(s32[1]{0:T(128)} %bitcast.refs_0_, s32[8,256]{1,0:T(8,128)} %bitcast.3, f32[8,256]{1,0:T(8,128)} %bitcast.4, ...), custom_call_target="tpu_custom_call" | custom-call | tf_op jit(solution)/shard_map/pallas_call | solution.py:262
  2.5 4.1 %collective-permute-start.6 = (bf16[48,896]{1,0:T(8,128)(2,1)S(1)}, bf16[48,896]{1,0:T(8,128)(2,1)S(1)}, u32[]{:S(2)}, u32[]{:S(2)}) collective-permute-start(bf16[48,896]{1,0:T(8,128)(2,1)S(1)} %get-tuple-element.30), channel_id=1, source_target_pairs={{0,16},{4,20},{8,24},{12,28},{16,0},{20,4},{24,8},{28,12},{1,17},{... | collective-permute-start | bytes 258056 | tf_op jit(solution)/shard_map/ppermute | solution.py:235
  6.6 1.3 %collective-permute-start.7 = (bf16[48,896]{1,0:T(8,128)(2,1)S(1)}, bf16[48,896]{1,0:T(8,128)(2,1)S(1)}, u32[]{:S(2)}, u32[]{:S(2)}) collective-permute-start(bf16[48,896]{1,0:T(8,128)(2,1)S(1)} %get-tuple-element.31), channel_id=1, source_target_pairs={{0,24},{4,28},{8,16},{12,20},{16,8},{20,12},{24,0},{28,4},{1,25},{... | collective-permute-start | bytes 258056 | tf_op jit(solution)/shard_map/ppermute | solution.py:235
  8.0 0.2 collective-permute-start
  8.2 4.7 %collective-permute-done.6.refs_0_.refs_3_ = bf16[48,896]{1,0:T(8,128)(2,1)S(1)} collective-permute-done((bf16[48,896]{1,0:T(8,128)(2,1)S(1)}, bf16[48,896]{1,0:T(8,128)(2,1)S(1)}, u32[]{:S(2)}, u32[]{:S(2)}) %collective-permute-start.6) | collective-permute-done | bytes 86048 | tf_op jit(solution)/shard_map/ppermute | solution.py:235
  12.9 0.5 %collective-permute-done.7.refs_1_.refs_4_ = bf16[48,896]{1,0:T(8,128)(2,1)S(1)} collective-permute-done((bf16[48,896]{1,0:T(8,128)(2,1)S(1)}, bf16[48,896]{1,0:T(8,128)(2,1)S(1)}, u32[]{:S(2)}, u32[]{:S(2)}) %collective-permute-start.7) | collective-permute-done | bytes 86048 | tf_op jit(solution)/shard_map/ppermute | solution.py:235
  13.5 1.8 %collective-permute-start.8 = (bf16[96,896]{1,0:T(8,128)(2,1)S(1)}, bf16[96,896]{1,0:T(8,128)(2,1)S(1)}, u32[]{:S(2)}, u32[]{:S(2)}) collective-permute-start(bf16[96,896]{1,0:T(8,128)(2,1)S(1)} %pad_maximum_fusion.1), channel_id=1, source_target_pairs={{0,4},{4,0},{8,12},{12,8},{16,20},{20,16},{24,28},{28,24},{1,5},{5... | collective-permute-start | bytes 516104 | tf_op jit(solution)/shard_map/ppermute | solution.py:238
  15.3 0.0 collective-permute-done.refs_1_
  15.3 0.0 copy-start
  15.3 0.5 %collective-permute-start.1 = (bf16[96,896]{1,0:T(8,128)(2,1)S(1)}, bf16[96,896]{1,0:T(8,128)(2,1)S(1)}, u32[]{:S(2)}, u32[]{:S(2)}) collective-permute-start(bf16[96,896]{1,0:T(8,128)(2,1)S(1)} %pad_maximum_fusion), channel_id=1, source_target_pairs={{0,4},{4,0},{8,12},{12,8},{16,20},{20,16},{24,28},{28,24},{1,5},{5... | collective-permute-start | bytes 516104 | tf_op jit(solution)/shard_map/ppermute | solution.py:238
  15.8 2.1 %shard_map.103 = (bf16[1,1792,512]{2,1,0:T(8,128)(2,1)S(1)}, bf16[1,512,1792]{2,1,0:T(8,128)(2,1)S(1)}) custom-call(bf16[1,1792,512]{2,1,0:T(8,128)(2,1)} %refs_0_.1, bf16[1,512,1792]{2,1,0:T(8,128)(2,1)} %refs_1_.1), custom_call_target="tpu_custom_call" | custom-call | tf_op jit(solution)/shard_map/pallas_call | solution.py:278
  18.0 1.7 %collective-permute-done.8.refs_2_.refs_5_ = bf16[96,896]{1,0:T(8,128)(2,1)S(1)} collective-permute-done((bf16[96,896]{1,0:T(8,128)(2,1)S(1)}, bf16[96,896]{1,0:T(8,128)(2,1)S(1)}, u32[]{:S(2)}, u32[]{:S(2)}) %collective-permute-start.8) | collective-permute-done | bytes 172064 | tf_op jit(solution)/shard_map/ppermute | solution.py:238
  19.6 0.0 copy-done
  19.6 1.3 %shard_map.106 = bf16[144,512]{1,0:T(8,128)(2,1)S(1)} custom-call(bf16[48,896]{1,0:T(8,128)(2,1)S(1)} %collective-permute-done.6.refs_0_.refs_3_, bf16[48,896]{1,0:T(8,128)(2,1)S(1)} %collective-permute-done.7.refs_1_.refs_4_, bf16[96,896]{1,0:T(8,128)(2,1)S(1)} %collective-permute-done.8.refs_2_.refs_5_, bf16[1,1792,512]{2,1,0:T(8,128)(2,1)S(1)} %copy-done, ...), custom_call_target="tpu_custom_call" | custom-call | tf_op jit(solution)/shard_map/pallas_call | solution.py:36
  20.9 0.1 collective-permute-start.9
  21.0 0.4 collective-permute-done.1.refs_2_
  21.5 1.3 %shard_map.104 = bf16[144,512]{1,0:T(8,128)(2,1)S(1)} custom-call(bf16[48,896]{1,0:T(8,128)(2,1)S(1)} %get-tuple-element.24.refs_0_, bf16[48,896]{1,0:T(8,128)(2,1)S(1)} %collective-permute-done.refs_1_, bf16[96,896]{1,0:T(8,128)(2,1)S(1)} %collective-permute-done.1.refs_2_, bf16[1,1792,512]{2,1,0:T(8,128)(2,1)S(1)} %copy-done, ...), custom_call_target="tpu_custom_call" | custom-call | tf_op jit(solution)/shard_map/pallas_call | solution.py:36
  22.8 0.1 collective-permute-start.2
  22.9 0.0 collective-permute-done.9
  22.9 1.6 %collective-permute-start.10 = (bf16[144,512]{1,0:T(8,128)(2,1)S(1)}, bf16[144,512]{1,0:T(8,128)(2,1)S(1)}, u32[]{:S(2)}, u32[]{:S(2)}) collective-permute-start(bf16[144,512]{1,0:T(8,128)(2,1)S(1)} %add_convert_fusion.a_ref), channel_id=1, source_target_pairs={{0,2},{1,3},{2,0},{3,1},{4,6},{5,7},{6,4},{7,5},{8,10},{9,11},{10,... | collective-permute-start | bytes 442376 | tf_op jit(solution)/shard_map/ppermute | solution.py:244
  24.5 0.0 collective-permute-done.2
  24.6 1.3 %collective-permute-start.3 = (bf16[144,512]{1,0:T(8,128)(2,1)S(1)}, bf16[144,512]{1,0:T(8,128)(2,1)S(1)}, u32[]{:S(2)}, u32[]{:S(2)}) collective-permute-start(bf16[144,512]{1,0:T(8,128)(2,1)S(1)} %add_convert_fusion.1.a_ref), channel_id=1, source_target_pairs={{0,2},{1,3},{2,0},{3,1},{4,6},{5,7},{6,4},{7,5},{8,10},{9,11},{10,... | collective-permute-start | bytes 442376 | tf_op jit(solution)/shard_map/ppermute | solution.py:244
  25.8 3.9 %collective-permute-done.10.b_ref = bf16[144,512]{1,0:T(8,128)(2,1)S(1)} collective-permute-done((bf16[144,512]{1,0:T(8,128)(2,1)S(1)}, bf16[144,512]{1,0:T(8,128)(2,1)S(1)}, u32[]{:S(2)}, u32[]{:S(2)}) %collective-permute-start.10) | collective-permute-done | bytes 147488 | tf_op jit(solution)/shard_map/ppermute | solution.py:244
  29.7 1.2 %shard_map.107 = (bf16[96,512]{1,0:T(8,128)(2,1)S(1)}, bf16[96,512]{1,0:T(8,128)(2,1)S(1)}, bf16[96,512]{1,0:T(8,128)(2,1)S(1)}, bf16[48,896]{1,0:T(8,128)(2,1)S(1)}, bf16[48,896]{1,0:T(8,128)(2,1)S(1)}) custom-call(bf16[144,512]{1,0:T(8,128)(2,1)S(1)} %add_convert_fusion.a_ref, bf16[144,512]{1,0:T(8,128)(2,1)S(1)} %collective-permute-done.10.b_ref, ...), custom_call_target="tpu_custom_call" | custom-call | tf_op jit(solution)/shard_map/pallas_call | solution.py:36
  31.0 1.6 %collective-permute-start.11 = (bf16[48,896]{1,0:T(8,128)(2,1)S(1)}, bf16[48,896]{1,0:T(8,128)(2,1)S(1)}, u32[]{:S(2)}, u32[]{:S(2)}) collective-permute-start(bf16[48,896]{1,0:T(8,128)(2,1)S(1)} %get-tuple-element.33), channel_id=1, source_target_pairs={{0,4},{4,0},{8,12},{12,8},{16,20},{20,16},{24,28},{28,24},{1,5},{5... | collective-permute-start | bytes 258056 | tf_op jit(solution)/shard_map/ppermute | solution.py:238
  32.5 0.0 collective-permute-done.3.b_ref
  32.5 1.2 %shard_map.105 = (bf16[96,512]{1,0:T(8,128)(2,1)S(1)}, bf16[96,512]{1,0:T(8,128)(2,1)S(1)}, bf16[96,512]{1,0:T(8,128)(2,1)S(1)}, bf16[48,896]{1,0:T(8,128)(2,1)S(1)}, bf16[48,896]{1,0:T(8,128)(2,1)S(1)}) custom-call(bf16[144,512]{1,0:T(8,128)(2,1)S(1)} %add_convert_fusion.1.a_ref, bf16[144,512]{1,0:T(8,128)(2,1)S(1)} %collective-permute-done.3.b_ref, ...), custom_call_target="tpu_custom_call" | custom-call | tf_op jit(solution)/shard_map/pallas_call | solution.py:36
  33.7 1.4 %collective-permute-start.4 = (bf16[48,896]{1,0:T(8,128)(2,1)S(1)}, bf16[48,896]{1,0:T(8,128)(2,1)S(1)}, u32[]{:S(2)}, u32[]{:S(2)}) collective-permute-start(bf16[48,896]{1,0:T(8,128)(2,1)S(1)} %get-tuple-element.29), channel_id=1, source_target_pairs={{0,4},{4,0},{8,12},{12,8},{16,20},{20,16},{24,28},{28,24},{1,5},{5... | collective-permute-start | bytes 258056 | tf_op jit(solution)/shard_map/ppermute | solution.py:238
  35.2 0.3 collective-permute-done.11
  35.6 5.9 %collective-permute-start.12 = (bf16[24,896]{1,0:T(8,128)(2,1)S(1)}, bf16[24,896]{1,0:T(8,128)(2,1)S(1)}, u32[]{:S(2)}, u32[]{:S(2)}) collective-permute-start(bf16[24,896]{1,0:T(8,128)(2,1)S(1)} %get-tuple-element.45), channel_id=1, source_target_pairs={{0,16},{4,20},{8,24},{12,28},{16,0},{20,4},{24,8},{28,12},{1,17},{... | collective-permute-start | bytes 129032 | tf_op jit(solution)/shard_map/ppermute | solution.py:235
  41.5 0.4 collective-permute-start.13
  41.9 0.0 collective-permute-done.4
  42.0 0.4 collective-permute-start.5
  42.4 1.9 %shard_map.110 = bf16[1,512,1792]{2,1,0:T(8,128)(2,1)} custom-call(bf16[48,896]{1,0:T(8,128)(2,1)S(1)} %get-tuple-element.24.refs_0_, bf16[48,896]{1,0:T(8,128)(2,1)S(1)} %collective-permute-done.refs_1_, bf16[96,896]{1,0:T(8,128)(2,1)S(1)} %collective-permute-done.1.refs_2_, bf16[48,896]{1,0:T(8,128)(2,1)S(1)} %collective-permute-done.6.refs_0_.refs_3_, ...), custom_call_target="tpu_custom_call" | custom-call | tf_op jit(solution)/shard_map/pallas_call | solution.py:325
  44.2 2.4 %shard_map.109 = (bf16[1,1792,512]{2,1,0:T(8,128)(2,1)}, bf16[1,1792,512]{2,1,0:T(8,128)(2,1)}) custom-call(bf16[48,896]{1,0:T(8,128)(2,1)S(1)} %get-tuple-element.24.refs_0_, bf16[48,896]{1,0:T(8,128)(2,1)S(1)} %collective-permute-done.refs_1_, bf16[96,896]{1,0:T(8,128)(2,1)S(1)} %collective-permute-done.1.refs_2_, ...), custom_call_target="tpu_custom_call" | custom-call | tf_op jit(solution)/shard_map/pallas_call | solution.py:316
  46.6 0.0 collective-permute-done.12.refs_2_
  46.6 0.7 %collective-permute-done.13.refs_3_ = bf16[24,896]{1,0:T(8,128)(2,1)S(1)} collective-permute-done((bf16[24,896]{1,0:T(8,128)(2,1)S(1)}, bf16[24,896]{1,0:T(8,128)(2,1)S(1)}, u32[]{:S(2)}, u32[]{:S(2)}) %collective-permute-start.13) | collective-permute-done | bytes 43040 | tf_op jit(solution)/shard_map/ppermute | solution.py:235
  47.3 0.0 collective-permute-done.5.refs_1_
  47.3 1.3 %shard_map.108 = bf16[256,1792]{1,0:T(8,128)(2,1)} custom-call(bf16[24,896]{1,0:T(8,128)(2,1)S(1)} %get-tuple-element.47.refs_0_, bf16[24,896]{1,0:T(8,128)(2,1)S(1)} %collective-permute-done.5.refs_1_, bf16[24,896]{1,0:T(8,128)(2,1)S(1)} %collective-permute-done.12.refs_2_, bf16[24,896]{1,0:T(8,128)(2,1)S(1)} %collective-permute-done.13.refs_3_, ...), custom_call_target="tpu_custom_call" | custom-call | tf_op jit(solution)/shard_map/pallas_call | solution.py:338
  (8 shorter events, 0.2 us)
Async XLA Ops:
  2.5 10.4 %collective-permute-start.6 = (bf16[48,896]{1,0:T(8,128)(2,1)S(1)}, bf16[48,896]{1,0:T(8,128)(2,1)S(1)}, u32[]{:S(2)}, u32[]{:S(2)}) collective-permute-start(bf16[48,896]{1,0:T(8,128)(2,1)S(1)} %get-tuple-element.30), channel_id=1, source_target_pairs={{0,16},{4,20},{8,24},{12,28},{16,0},{20,4},{24,8},{28,12},{1,17},{... | collective-permute-start | bytes 258056 | tf_op jit(solution)/shard_map/ppermute | solution.py:235
  6.6 6.8 %collective-permute-start.7 = (bf16[48,896]{1,0:T(8,128)(2,1)S(1)}, bf16[48,896]{1,0:T(8,128)(2,1)S(1)}, u32[]{:S(2)}, u32[]{:S(2)}) collective-permute-start(bf16[48,896]{1,0:T(8,128)(2,1)S(1)} %get-tuple-element.31), channel_id=1, source_target_pairs={{0,24},{4,28},{8,16},{12,20},{16,8},{20,12},{24,0},{28,4},{1,25},{... | collective-permute-start | bytes 258056 | tf_op jit(solution)/shard_map/ppermute | solution.py:235
  8.0 7.3 %collective-permute-start = (bf16[48,896]{1,0:T(8,128)(2,1)S(1)}, bf16[48,896]{1,0:T(8,128)(2,1)S(1)}, u32[]{:S(2)}, u32[]{:S(2)}) collective-permute-start(bf16[48,896]{1,0:T(8,128)(2,1)S(1)} %get-tuple-element.25), channel_id=1, source_target_pairs={{0,8},{4,12},{8,0},{12,4},{16,24},{20,28},{24,16},{28,20},{1,9},{5... | collective-permute-start | bytes 258056 | tf_op jit(solution)/shard_map/ppermute | solution.py:235
  13.5 6.2 %collective-permute-start.8 = (bf16[96,896]{1,0:T(8,128)(2,1)S(1)}, bf16[96,896]{1,0:T(8,128)(2,1)S(1)}, u32[]{:S(2)}, u32[]{:S(2)}) collective-permute-start(bf16[96,896]{1,0:T(8,128)(2,1)S(1)} %pad_maximum_fusion.1), channel_id=1, source_target_pairs={{0,4},{4,0},{8,12},{12,8},{16,20},{20,16},{24,28},{28,24},{1,5},{5... | collective-permute-start | bytes 516104 | tf_op jit(solution)/shard_map/ppermute | solution.py:238
  15.3 4.3 %copy-start = (bf16[1,1792,512]{2,1,0:T(8,128)(2,1)S(1)}, bf16[1,1792,512]{2,1,0:T(8,128)(2,1)}, u32[]{:S(2)}) copy-start(bf16[1,1792,512]{2,1,0:T(8,128)(2,1)} %gate_ref.3) | copy-start | bytes 5505028
  15.3 6.2 %collective-permute-start.1 = (bf16[96,896]{1,0:T(8,128)(2,1)S(1)}, bf16[96,896]{1,0:T(8,128)(2,1)S(1)}, u32[]{:S(2)}, u32[]{:S(2)}) collective-permute-start(bf16[96,896]{1,0:T(8,128)(2,1)S(1)} %pad_maximum_fusion), channel_id=1, source_target_pairs={{0,4},{4,0},{8,12},{12,8},{16,20},{20,16},{24,28},{28,24},{1,5},{5... | collective-permute-start | bytes 516104 | tf_op jit(solution)/shard_map/ppermute | solution.py:238
  20.9 1.9 %collective-permute-start.9 = (bf16[144,512]{1,0:T(8,128)(2,1)S(1)}, bf16[144,512]{1,0:T(8,128)(2,1)S(1)}, u32[]{:S(2)}, u32[]{:S(2)}) collective-permute-start(bf16[144,512]{1,0:T(8,128)(2,1)S(1)} %shard_map.106), channel_id=1, source_target_pairs={{0,1},{1,0},{2,3},{3,2},{4,5},{5,4},{6,7},{7,6},{8,9},{9,8},{10,11... | collective-permute-start | bytes 442376 | tf_op jit(solution)/shard_map/ppermute | solution.py:244
  22.8 1.7 %collective-permute-start.2 = (bf16[144,512]{1,0:T(8,128)(2,1)S(1)}, bf16[144,512]{1,0:T(8,128)(2,1)S(1)}, u32[]{:S(2)}, u32[]{:S(2)}) collective-permute-start(bf16[144,512]{1,0:T(8,128)(2,1)S(1)} %shard_map.104), channel_id=1, source_target_pairs={{0,1},{1,0},{2,3},{3,2},{4,5},{5,4},{6,7},{7,6},{8,9},{9,8},{10,11... | collective-permute-start | bytes 442376 | tf_op jit(solution)/shard_map/ppermute | solution.py:244
  22.9 6.8 %collective-permute-start.10 = (bf16[144,512]{1,0:T(8,128)(2,1)S(1)}, bf16[144,512]{1,0:T(8,128)(2,1)S(1)}, u32[]{:S(2)}, u32[]{:S(2)}) collective-permute-start(bf16[144,512]{1,0:T(8,128)(2,1)S(1)} %add_convert_fusion.a_ref), channel_id=1, source_target_pairs={{0,2},{1,3},{2,0},{3,1},{4,6},{5,7},{6,4},{7,5},{8,10},{9,11},{10,... | collective-permute-start | bytes 442376 | tf_op jit(solution)/shard_map/ppermute | solution.py:244
  24.6 8.0 %collective-permute-start.3 = (bf16[144,512]{1,0:T(8,128)(2,1)S(1)}, bf16[144,512]{1,0:T(8,128)(2,1)S(1)}, u32[]{:S(2)}, u32[]{:S(2)}) collective-permute-start(bf16[144,512]{1,0:T(8,128)(2,1)S(1)} %add_convert_fusion.1.a_ref), channel_id=1, source_target_pairs={{0,2},{1,3},{2,0},{3,1},{4,6},{5,7},{6,4},{7,5},{8,10},{9,11},{10,... | collective-permute-start | bytes 442376 | tf_op jit(solution)/shard_map/ppermute | solution.py:244
  31.0 4.5 %collective-permute-start.11 = (bf16[48,896]{1,0:T(8,128)(2,1)S(1)}, bf16[48,896]{1,0:T(8,128)(2,1)S(1)}, u32[]{:S(2)}, u32[]{:S(2)}) collective-permute-start(bf16[48,896]{1,0:T(8,128)(2,1)S(1)} %get-tuple-element.33), channel_id=1, source_target_pairs={{0,4},{4,0},{8,12},{12,8},{16,20},{20,16},{24,28},{28,24},{1,5},{5... | collective-permute-start | bytes 258056 | tf_op jit(solution)/shard_map/ppermute | solution.py:238
  33.7 8.2 %collective-permute-start.4 = (bf16[48,896]{1,0:T(8,128)(2,1)S(1)}, bf16[48,896]{1,0:T(8,128)(2,1)S(1)}, u32[]{:S(2)}, u32[]{:S(2)}) collective-permute-start(bf16[48,896]{1,0:T(8,128)(2,1)S(1)} %get-tuple-element.29), channel_id=1, source_target_pairs={{0,4},{4,0},{8,12},{12,8},{16,20},{20,16},{24,28},{28,24},{1,5},{5... | collective-permute-start | bytes 258056 | tf_op jit(solution)/shard_map/ppermute | solution.py:238
  35.6 11.1 %collective-permute-start.12 = (bf16[24,896]{1,0:T(8,128)(2,1)S(1)}, bf16[24,896]{1,0:T(8,128)(2,1)S(1)}, u32[]{:S(2)}, u32[]{:S(2)}) collective-permute-start(bf16[24,896]{1,0:T(8,128)(2,1)S(1)} %get-tuple-element.45), channel_id=1, source_target_pairs={{0,16},{4,20},{8,24},{12,28},{16,0},{20,4},{24,8},{28,12},{1,17},{... | collective-permute-start | bytes 129032 | tf_op jit(solution)/shard_map/ppermute | solution.py:235
  41.5 5.8 %collective-permute-start.13 = (bf16[24,896]{1,0:T(8,128)(2,1)S(1)}, bf16[24,896]{1,0:T(8,128)(2,1)S(1)}, u32[]{:S(2)}, u32[]{:S(2)}) collective-permute-start(bf16[24,896]{1,0:T(8,128)(2,1)S(1)} %get-tuple-element.44), channel_id=1, source_target_pairs={{0,24},{4,28},{8,16},{12,20},{16,8},{20,12},{24,0},{28,4},{1,25},{... | collective-permute-start | bytes 129032 | tf_op jit(solution)/shard_map/ppermute | solution.py:235
  42.0 5.3 %collective-permute-start.5 = (bf16[24,896]{1,0:T(8,128)(2,1)S(1)}, bf16[24,896]{1,0:T(8,128)(2,1)S(1)}, u32[]{:S(2)}, u32[]{:S(2)}) collective-permute-start(bf16[24,896]{1,0:T(8,128)(2,1)S(1)} %get-tuple-element.46), channel_id=1, source_target_pairs={{0,8},{4,12},{8,0},{12,4},{16,24},{20,28},{24,16},{28,20},{1,9},{5... | collective-permute-start | bytes 129032 | tf_op jit(solution)/shard_map/ppermute | solution.py:235

commit v2 on v1

--- a/solution.py
+++ b/solution.py
@@ -131,29 +131,43 @@
     return jnp.concatenate(blocks, axis=0)
 
 
+def unfolded(v):
+    first = upper(*v.shape)
+    turned = swapped(v, first)
+    low, high = jnp.where(first, v, turned), jnp.where(first, turned, v)
+    return jnp.concatenate([low.astype(BF16), high.astype(BF16)], axis=1)
+
+
+def gate_up_kernel(count, *refs):
+    own, other, (gate_ref, up_ref, out_ref) = refs[:count], refs[count], refs[count + 1 :]
+    rows = unfolded(received(own, other, 0))
+    gate, up = dot(rows, gate_ref[0]), dot(rows, up_ref[0])
+    out_ref[: gate.shape[0]] = jnp.where(upper(*gate.shape), gate, up).astype(BF16)
+
+
+def hidden_kernel(count, *refs):
+    own, other, (down_ref, out_ref) = refs[:count], refs[count], refs[count + 1 :]
+    n = count * PAIR
+    grads = unfolded(received(own, other, 1))
+    part = dot(grads, down_ref[0], OVER_COLUMNS)
+    start = out_ref.shape[0] - n
+    out_ref[start:] = jnp.where(upper(n, part.shape[1]), part[:n], part[n:]).astype(BF16)
+
+
 def product_kernel(count, *refs):
-    own, other, (gate_ref, up_ref, down_ref, out_ref) = refs[:count], refs[count], refs[count + 1 :]
-    w = other.shape[1]
-    n = count * PAIR
-    rows = received(own, other, 0)
-    first = upper(*rows.shape)
-    turned = swapped(rows, first).astype(BF16)
-    rows = rows.astype(BF16)
-    gate = dot(rows, gate_ref[0, :w]) + dot(turned, gate_ref[0, w:])
-    up = dot(turned, up_ref[0, :w]) + dot(rows, up_ref[0, w:])
-    out_ref[: 2 * n] = jnp.where(upper(*gate.shape), gate, up).astype(BF16)
-    grads = received(own, other, 1)
-    turned = swapped(grads, first)
-    low = jnp.concatenate([grads[:n], turned[n:]], axis=0).astype(BF16)
-    high = jnp.concatenate([turned[:n], grads[n:]], axis=0).astype(BF16)
-    part = dot(low, down_ref[0, :, :w], OVER_COLUMNS) + dot(high, down_ref[0, :, w:], OVER_COLUMNS)
-    out_ref[2 * n :] = jnp.where(upper(n, part.shape[1]), part[:n], part[n:]).astype(BF16)
-
-
-def delta_kernel(a_ref, b_ref, gate_ref, up_ref, act_ref, d_ref, dt_ref, own_ref, other_ref):
-    n, w = own_ref.shape
-    total = a_ref[...].astype(F32) + b_ref[...].astype(F32)
-    gu, h = total[: 2 * n], total[2 * n :]
+    blocks, (gate_ref, up_ref, down_ref, out_ref) = refs[: count + 1], refs[count + 1 :]
+    gate_up_kernel(count, *blocks, gate_ref, up_ref, out_ref)
+    hidden_kernel(count, *blocks, down_ref, out_ref)
+
+
+def delta_kernel(pairs, sizes, *refs):
+    sums, refs = refs[: 2 * pairs], refs[2 * pairs :]
+    (gate_ref, up_ref, act_ref, gd_ref, ud_ref), backs = refs[:5], refs[5:]
+    n, w = act_ref.shape[0] // 2, backs[0].shape[1]
+    totals = [
+        sums[2 * i][...].astype(F32) + sums[2 * i + 1][...].astype(F32) for i in range(pairs)
+    ]
+    gu, h = totals if pairs == 2 else (totals[0][: 2 * n], totals[0][2 * n :])
     first = upper(*gu.shape)
     half = upper(*h.shape)
     gu_t, h_t = swapped(gu, first), swapped(h, half)
@@ -163,57 +177,83 @@
     act_ref[...] = (gate * sig * up).astype(BF16)
     gate_delta = hidden * up * sig * (1.0 + gate * (1.0 - sig))
     up_delta = hidden * gate * sig
-    d = jnp.where(first, gate_delta, up_delta).astype(BF16)
-    dt = jnp.where(first, up_delta, gate_delta).astype(BF16)
-    d_ref[...] = d
-    dt_ref[...] = dt
-    low = dot(d, gate_ref[0, :w], OVER_COLUMNS) + dot(dt, up_ref[0, :w], OVER_COLUMNS)
-    high = dot(dt, gate_ref[0, w:], OVER_COLUMNS) + dot(d, up_ref[0, w:], OVER_COLUMNS)
-    back = jnp.where(upper(*low.shape), low, high).astype(BF16)
-    own_ref[...] = back[:n]
-    other_ref[...] = back[n:]
+    gate_delta, up_delta = gate_delta.astype(BF16), up_delta.astype(BF16)
+    gd_ref[...] = gate_delta
+    ud_ref[...] = up_delta
+    back = dot(gate_delta, gate_ref[0], OVER_COLUMNS) + dot(up_delta, up_ref[0], OVER_COLUMNS)
+    back = jnp.where(upper(2 * n, w), back[:, :w], back[:, w:]).astype(BF16)
+    for i, (start, size) in enumerate(sizes):
+        backs[2 * i][...] = back[start : start + size]
+        backs[2 * i + 1][...] = back[n + start : n + start + size]
+
+
+def all_received(counts, refs, part):
+    blocks, at = [], 0
+    for count in counts:
+        blocks.append(received(refs[at : at + count], refs[at + count], part))
+        at += count + 1
+    return jnp.concatenate(blocks, axis=0), refs[at:]
 
 
 def gate_up_grad_kernel(counts, *refs):
-    gate_ref, up_ref = refs[-2:]
-    low = pl.program_id(0) == 0
-    rows, d, dt, at = [], [], [], 0
-    for count in counts:
-        rows.append(received(refs[at : at + count], refs[at + count], 0))
-        at += count + 1
-    for i in range(len(counts)):
-        d.append(refs[at + 2 * i][...].astype(F32))
-        dt.append(refs[at + 2 * i + 1][...].astype(F32))
-    rows, d, dt = (jnp.concatenate(v, axis=0) for v in (rows, d, dt))
-    rows = rows.astype(BF16)
-    keep = jnp.logical_xor(upper(*d.shape), jnp.logical_not(low))
-    gate = jnp.where(keep, jnp.where(low, d, dt), 0.0).astype(BF16)
-    up = jnp.where(keep, jnp.where(low, dt, d), 0.0).astype(BF16)
-    gate_ref[0] = dot(rows, gate, OVER_ROWS).astype(BF16)
-    up_ref[0] = dot(rows, up, OVER_ROWS).astype(BF16)
+    rows, refs = all_received(counts, refs, 0)
+    k = len(counts)
+    deltas = [jnp.concatenate([r[...].astype(F32) for r in refs[i * k : i * k + k]], axis=0) for i in (0, 1)]
+    outs, (held, sems) = refs[2 * k : -2], refs[-2:]
+    w = rows.shape[1]
+    first = upper(*deltas[0].shape)
+    turned = rows.T.astype(BF16)
+    copies = []
+    for half in (0, 1):
+        keep = first if half == 0 else jnp.logical_not(first)
+        for i, delta in enumerate(deltas):
+            at = 2 * half + i
+            held[at] = dot(turned, jnp.where(keep, delta, 0.0).astype(BF16)).astype(BF16)
+            copies.append(
+                pltpu.make_async_copy(
+                    held.at[at], outs[i].at[0, half * w : (half + 1) * w], sems.at[at]
+                )
+            )
+            copies[-1].start()
+    for copy in copies:
+        copy.wait()
 
 
 def down_grad_kernel(counts, *refs):
-    out_ref = refs[-1]
-    grads, act, at = [], [], 0
-    for count in counts:
-        grads.append(received(refs[at : at + count], refs[at + count], 1))
-        at += count + 1
-    for i in range(len(counts)):
-        act.append(refs[at + i][...].astype(F32))
-    grads, act = (jnp.concatenate(v, axis=0) for v in (grads, act))
-    keep = jnp.logical_xor(upper(*act.shape), pl.program_id(0) == 1)
-    act = jnp.where(keep, act, 0.0).astype(BF16)
-    out_ref[0] = dot(act, grads.astype(BF16), OVER_ROWS).astype(BF16)
+    grads, refs = all_received(counts, refs, 1)
+    k = len(counts)
+    act = jnp.concatenate([r[...].astype(F32) for r in refs[:k]], axis=0)
+    outs, (held, sems) = refs[k:-2], refs[-2:]
+    w = grads.shape[1]
+    grads = grads.astype(BF16)
+    first = upper(*act.shape)
+    copies = []
+    for half in (0, 1):
+        keep = first if half == 0 else jnp.logical_not(first)
+        held[half] = dot(jnp.where(keep, act, 0.0).astype(BF16), grads, OVER_ROWS).astype(BF16)
+        out = outs[0].at[0, :, half * w : (half + 1) * w] if len(outs) == 1 else outs[half].at[0]
+        copies.append(pltpu.make_async_copy(held.at[half], out, sems.at[half]))
+        copies[-1].start()
+    for copy in copies:
+        copy.wait()
+
+
+def early_kernel(count, *refs):
+    blocks, (p0_ref, p1_ref, total_ref) = refs[:count], refs[count:]
+    rows = joined(blocks).astype(BF16)
+    n = rows.shape[0]
+    total_ref[0] = dot(p0_ref[:n], rows, OVER_ROWS)
+    total_ref[1] = dot(p1_ref[:n], rows, OVER_ROWS)
 
 
 def combine_kernel(count, *refs):
-    blocks, p_refs = refs[:count], refs[count : count + 2]
-    outs, (held, sems) = refs[count + 2 : -2], refs[-2:]
+    blocks, (p0_ref, p1_ref, total_ref) = refs[:count], refs[count : count + 3]
+    outs, (held, sems) = refs[count + 3 : -2], refs[-2:]
     rows = joined(blocks).astype(BF16)
+    start = p0_ref.shape[0] - rows.shape[0]
     copies = []
-    for i, (p_ref, out) in enumerate(zip(p_refs, columns(outs))):
-        held[i] = dot(p_ref[...], rows, OVER_ROWS).astype(BF16)
+    for i, (p_ref, out) in enumerate(zip((p0_ref, p1_ref), columns(outs))):
+        held[i] = (total_ref[i] + dot(p_ref[start:], rows, OVER_ROWS)).astype(BF16)
         copies.append(pltpu.make_async_copy(held.at[i], out, sems.at[i]))
         copies[-1].start()
     for copy in copies:
@@ -249,9 +289,6 @@
 
     def halves(v):
         return (v,) if aligned else (v[:, :w], v[:, w:])
-
-    def whole(v):
-        return pl.BlockSpec(v.shape, lambda i: (0,) * v.ndim)
 
     space = pl.BlockSpec(memory_space=pltpu.VMEM)
     smem = pl.BlockSpec(memory_space=pltpu.SMEM)
@@ -290,59 +327,78 @@
     other = [other_half(jnp.concatenate(v, axis=0)) for v in own]
     sums = []
     for i, count in enumerate(counts):
+        n = count * PAIR
+        take = (*own[i], other[i])
+        if i == 0:
+            part = call(
+                functools.partial(product_kernel, count),
+                shape((3 * n, hidden)),
+                *take, gate_weight, up_w, down_w,
+            )
+            sums.append(reduced(part))
+            continue
         part = call(
-            functools.partial(product_kernel, count),
-            shape((3 * count * PAIR, hidden)),
-            *own[i], other[i], gate_weight, up_w, down_w,
+            functools.partial(gate_up_kernel, count),
+            shape((2 * n, hidden)),
+            *take, gate_weight, up_w,
         )
-        sums.append(reduced(part))
+        h_part = call(functools.partial(hidden_kernel, count), shape((n, hidden)), *take, down_w)
+        sums.append(reduced(part) + reduced(h_part))
     deltas, home = [], [None] * window
     for i, count in enumerate(counts):
         n = count * PAIR
-        *delta, back_own, back_other = call(
-            delta_kernel,
-            (shape((2 * n, hidden)),) * 3 + (shape((n, w)),) * 2,
+        chunk = list(chunks[i])
+        pieces = [chunk] if i == 0 else [chunk[count // 2 :], chunk[: count // 2]]
+        sizes = [((piece[0] - chunk[0]) * PAIR, len(piece) * PAIR) for piece in pieces]
+        *delta, = call(
+            functools.partial(delta_kernel, len(sums[i]) // 2, sizes),
+            (shape((2 * n, hidden)),) * 3
+            + tuple(shape((size, w)) for _, size in sizes for _ in range(2)),
             *sums[i], gate_weight, up_w,
         )
-        deltas.append(delta)
-        returned = other_half(back_other)
-        back = (back_own.astype(F32) + returned.astype(F32)).astype(BF16)
-        for k, d in enumerate(chunks[i]):
-            block = back[k * PAIR : (k + 1) * PAIR]
-            home[d] = across(block, d) if d else block
+        deltas.append(delta[:3])
+        for j, piece in enumerate(pieces):
+            back_own, back_other = delta[3 + 2 * j], delta[4 + 2 * j]
+            returned = other_half(back_other)
+            back = (back_own.astype(F32) + returned.astype(F32)).astype(BF16)
+            for k, d in enumerate(piece):
+                block = back[k * PAIR : (k + 1) * PAIR]
+                home[d] = across(block, d) if d else block
 
     blocks = tuple(v for i in range(len(chunks)) for v in (*own[i], other[i]))
-    grad_args = blocks + tuple(v for delta in deltas for v in delta[1:])
+    grad_args = blocks + tuple(delta[i] for i in (1, 2) for delta in deltas)
     gate_grad, up_grad = pl.pallas_call(
         functools.partial(gate_up_grad_kernel, counts),
-        grid=(2,),
         out_shape=(shape(gate_weight.shape),) * 2,
-        in_specs=[whole(v) for v in grad_args],
-        out_specs=(pl.BlockSpec((1, w, hidden), lambda i: (0, i, 0)),) * 2,
+        in_specs=[space] * len(grad_args),
+        out_specs=(hbm,) * 2,
+        scratch_shapes=[pltpu.VMEM((4, w, hidden), BF16), pltpu.SemaphoreType.DMA((4,))],
         compiler_params=params,
     )(*grad_args)
     down_args = blocks + tuple(delta[0] for delta in deltas)
+    out_shape = (shape(down_weight.shape),) if aligned else (shape((1, hidden, w)),) * 2
     down_grad = pl.pallas_call(
         functools.partial(down_grad_kernel, counts),
-        grid=(2,),
-        out_shape=shape(down_weight.shape if aligned else (2, hidden, w)),
-        in_specs=[whole(v) for v in down_args],
-        out_specs=pl.BlockSpec(
-            (1, hidden, w), (lambda i: (0, 0, i)) if aligned else (lambda i: (i, 0, 0))
-        ),
+        out_shape=out_shape,
+        in_specs=[space] * len(down_args),
+        out_specs=(hbm,) * len(out_shape),
+        scratch_shapes=[pltpu.VMEM((2, hidden, w), BF16), pltpu.SemaphoreType.DMA((2,))],
         compiler_params=params,
     )(*down_args)
-    if not aligned:
-        down_grad = jnp.concatenate([down_grad[:1], down_grad[1:]], axis=2)
+    down_grad = down_grad[0] if aligned else jnp.concatenate(down_grad, axis=2)
+    early, late = [home[d] for d in chunks[0]], [home[d] for d in chunks[1]]
+    total = call(
+        functools.partial(early_kernel, len(early)), shape((2, tok, w), F32), *early, p0, p1
+    )
     out_shape = (shape((tok, slab)),) if aligned else (shape((tok, w)),) * 2
     out = pl.pallas_call(
-        functools.partial(combine_kernel, len(home)),
+        functools.partial(combine_kernel, len(late)),
         out_shape=out_shape,
-        in_specs=[space] * (len(home) + 2),
+        in_specs=[space] * (len(late) + 3),
         out_specs=(hbm,) * len(out_shape),
         scratch_shapes=[pltpu.VMEM((2, tok, w), BF16), pltpu.SemaphoreType.DMA((2,))],
         compiler_params=params,
-    )(*home, p0, p1)
+    )(*late, p0, p1, total)
     token_grad = out[0] if aligned else jnp.concatenate(out, axis=1)
     return token_grad, gate_grad, up_grad, down_grad
 

time: 48.8 us -> 55 us (1.13)
  starting transfers between devices: 20.8 us -> 26.4 us
    ppermute x6, starting transfers between devices: 12.5 us -> 16 us  [across(): return lax.ppermute(v, 'expert', perm)]
    ppermute x4 -> x6, waiting for transfers between devices: 3.9 us -> 5.66 us  [reduced(): got = lax.ppermute(part, 'fsdp', [(f, f ^ bit) for f in range(fsdp_count)])]
    ppermute x4 -> x6, starting transfers between devices: 3.04 us -> 4.46 us  [reduced(): got = lax.ppermute(part, 'fsdp', [(f, f ^ bit) for f in range(fsdp_count)])]
    ppermute x4 -> x5, waiting for transfers between devices: 2.46 us -> 1.68 us  [other_half(): return lax.ppermute(v, 'expert', [(e, e ^ 1) for e in range(expert_count)])]
    ppermute x4 -> x5, starting transfers between devices: 5.32 us -> 6 us  [other_half(): return lax.ppermute(v, 'expert', [(e, e ^ 1) for e in range(expert_count)])]
    ppermute x6, waiting for transfers between devices: 5.92 us -> 5.24 us  [across(): return lax.ppermute(v, 'expert', perm)]
    pallas_call x4 -> x6, Pallas kernels: 5.08 us -> 5.58 us  [call(): pl.pallas_call(kernel, out_shape=outs, in_specs=[space] * len(args), out_...]
  transfers between devices with their start and end apart: 14 -> 17, of which waited for: 7 -> 4; matrix products, arithmetic and copies ran while one was open for 0% -> 0% of each run, Pallas kernels for 24% -> 21%
where the time goes in v2:
time: 55 us; the launch traced here: 54.8 us
  starting transfers between devices  26.4 us (48%)
  Pallas kernels  14.8 us (27%)
  waiting for transfers between devices  12.6 us (23%)
  between operations  0.81 us (1%)
    ppermute x6, starting transfers between devices, across(): return lax.ppermute(v, 'expert', perm)  16 us
    ppermute x5, starting transfers between devices, other_half(): return lax.ppermute(v, 'expert', [(e, e ^ 1) for e in range(expert_count)])  6 us
    ppermute x6, waiting for transfers between devices, reduced(): got = lax.ppermute(part, 'fsdp', [(f, f ^ bit) for f in range(fsdp_count)])  5.66 us
    pallas_call x6, Pallas kernels, call(): pl.pallas_call(kernel, out_shape=outs, in_specs=[space] * len(args), out_...  5.58 us
    ppermute x6, waiting for transfers between devices, across(): return lax.ppermute(v, 'expert', perm)  5.24 us
    ppermute x6, starting transfers between devices, reduced(): got = lax.ppermute(part, 'fsdp', [(f, f ^ bit) for f in range(fsdp_count)])  4.46 us
    pallas_call x1, Pallas kernels, body(): pl.pallas_call(functools.partial(gate_up_grad_kernel, counts), out_shape=...  2.33 us
    pallas_call x1, Pallas kernels, body(): pl.pallas_call(load_kernel, out_shape=tuple((shape(v.shape) for v in weig...  2.1 us
  transfers between devices with their start and end apart: 17, of which 4 were waited for; matrix products, arithmetic and copies ran while one was open for 0% of the time, Pallas kernels for 21%

profile of v2, /device:TPU:0, one launch (start us, length us, event | category | flops | bytes accessed | tf_op | source)
XLA Modules:
  0.0 54.8 jit_solution(12628160833626666870)
XLA Ops:
  0.6 1.9 %shard_map.102 = (bf16[48,896]{1,0:T(8,128)(2,1)S(1)}, bf16[48,896]{1,0:T(8,128)(2,1)S(1)}, bf16[48,896]{1,0:T(8,128)(2,1)S(1)}, bf16[48,896]{1,0:T(8,128)(2,1)S...) custom-call(s32[1]{0:T(128)} %bitcast.refs_0_, s32[8,256]{1,0:T(8,128)} %bitcast.3, f32[8,256]{1,0:T(8,128)} %bitcast.4, ...), custom_call_target="tpu_custom_call" | custom-call | tf_op jit(solution)/shard_map/pallas_call | solution.py:299
  2.5 4.1 %collective-permute-start = (bf16[48,896]{1,0:T(8,128)(2,1)S(1)}, bf16[48,896]{1,0:T(8,128)(2,1)S(1)}, u32[]{:S(2)}, u32[]{:S(2)}) collective-permute-start(bf16[48,896]{1,0:T(8,128)(2,1)S(1)} %get-tuple-element.26), channel_id=1, source_target_pairs={{0,16},{4,20},{8,24},{12,28},{16,0},{20,4},{24,8},{28,12},{1,17},{... | collective-permute-start | bytes 258056 | tf_op jit(solution)/shard_map/ppermute | solution.py:275
  6.6 1.3 %collective-permute-start.1 = (bf16[48,896]{1,0:T(8,128)(2,1)S(1)}, bf16[48,896]{1,0:T(8,128)(2,1)S(1)}, u32[]{:S(2)}, u32[]{:S(2)}) collective-permute-start(bf16[48,896]{1,0:T(8,128)(2,1)S(1)} %get-tuple-element.27), channel_id=1, source_target_pairs={{0,24},{4,28},{8,16},{12,20},{16,8},{20,12},{24,0},{28,4},{1,25},{... | collective-permute-start | bytes 258056 | tf_op jit(solution)/shard_map/ppermute | solution.py:275
  8.0 0.2 collective-permute-start.11
  8.2 4.7 %collective-permute-done.refs_0_.refs_3_ = bf16[48,896]{1,0:T(8,128)(2,1)S(1)} collective-permute-done((bf16[48,896]{1,0:T(8,128)(2,1)S(1)}, bf16[48,896]{1,0:T(8,128)(2,1)S(1)}, u32[]{:S(2)}, u32[]{:S(2)}) %collective-permute-start) | collective-permute-done | bytes 86048 | tf_op jit(solution)/shard_map/ppermute | solution.py:275
  12.9 0.5 collective-permute-done.1.refs_1_.refs_4_
  13.5 1.8 %collective-permute-start.2 = (bf16[96,896]{1,0:T(8,128)(2,1)S(1)}, bf16[96,896]{1,0:T(8,128)(2,1)S(1)}, u32[]{:S(2)}, u32[]{:S(2)}) collective-permute-start(bf16[96,896]{1,0:T(8,128)(2,1)S(1)} %pad_maximum_fusion), channel_id=1, source_target_pairs={{0,4},{4,0},{8,12},{12,8},{16,20},{20,16},{24,28},{28,24},{1,5},{5... | collective-permute-start | bytes 516104 | tf_op jit(solution)/shard_map/ppermute | solution.py:278
  15.3 0.0 collective-permute-done.11.refs_1_
  15.3 0.0 copy-start
  15.3 0.5 collective-permute-start.12
  15.8 2.1 %shard_map.103 = (bf16[1,1792,512]{2,1,0:T(8,128)(2,1)S(1)}, bf16[1,512,1792]{2,1,0:T(8,128)(2,1)S(1)}) custom-call(bf16[1,1792,512]{2,1,0:T(8,128)(2,1)} %refs_0_.1, bf16[1,512,1792]{2,1,0:T(8,128)(2,1)} %refs_1_.1), custom_call_target="tpu_custom_call" | custom-call | tf_op jit(solution)/shard_map/pallas_call | solution.py:315
  18.0 1.7 %collective-permute-done.2.refs_2_.refs_5_ = bf16[96,896]{1,0:T(8,128)(2,1)S(1)} collective-permute-done((bf16[96,896]{1,0:T(8,128)(2,1)S(1)}, bf16[96,896]{1,0:T(8,128)(2,1)S(1)}, u32[]{:S(2)}, u32[]{:S(2)}) %collective-permute-start.2) | collective-permute-done | bytes 172064 | tf_op jit(solution)/shard_map/ppermute | solution.py:278
  19.6 0.0 copy-done
  19.6 0.7 %shard_map.104 = bf16[96,512]{1,0:T(8,128)(2,1)S(1)} custom-call(bf16[48,896]{1,0:T(8,128)(2,1)S(1)} %collective-permute-done.refs_0_.refs_3_, bf16[48,896]{1,0:T(8,128)(2,1)S(1)} %collective-permute-done.1.refs_1_.refs_4_, bf16[96,896]{1,0:T(8,128)(2,1)S(1)} %collective-permute-done.2.refs_2_.refs_5_, bf16[1,1792,512]{2,1,0:T(8,128)(2,1)S(1)} %copy-done, ...), custom_call_target="tpu_custom_call" | custom-call | tf_op jit(solution)/shard_map/pallas_call | solution.py:36
  20.3 0.1 collective-permute-start.3
  20.4 0.7 %shard_map.105 = bf16[48,512]{1,0:T(8,128)(2,1)S(1)} custom-call(bf16[48,896]{1,0:T(8,128)(2,1)S(1)} %collective-permute-done.refs_0_.refs_3_, bf16[48,896]{1,0:T(8,128)(2,1)S(1)} %collective-permute-done.1.refs_1_.refs_4_, bf16[96,896]{1,0:T(8,128)(2,1)S(1)} %collective-permute-done.2.refs_2_.refs_5_, ...), custom_call_target="tpu_custom_call" | custom-call | tf_op jit(solution)/shard_map/pallas_call | solution.py:36
  21.1 0.6 %collective-permute-start.5 = (bf16[48,512]{1,0:T(8,128)(2,1)S(1)}, bf16[48,512]{1,0:T(8,128)(2,1)S(1)}, u32[]{:S(2)}, u32[]{:S(2)}) collective-permute-start(bf16[48,512]{1,0:T(8,128)(2,1)S(1)} %shard_map.105), channel_id=1, source_target_pairs={{0,1},{1,0},{2,3},{3,2},{4,5},{5,4},{6,7},{7,6},{8,9},{9,8},{10,11... | collective-permute-start | bytes 147464 | tf_op jit(solution)/shard_map/ppermute | solution.py:284
  21.7 0.0 collective-permute-done.12.refs_2_
  21.7 1.3 %shard_map.107 = bf16[144,512]{1,0:T(8,128)(2,1)S(1)} custom-call(bf16[48,896]{1,0:T(8,128)(2,1)S(1)} %get-tuple-element.36.refs_0_, bf16[48,896]{1,0:T(8,128)(2,1)S(1)} %collective-permute-done.11.refs_1_, bf16[96,896]{1,0:T(8,128)(2,1)S(1)} %collective-permute-done.12.refs_2_, bf16[1,1792,512]{2,1,0:T(8,128)(2,1)S(1)} %copy-done, ...), custom_call_target="tpu_custom_call" | custom-call | tf_op jit(solution)/shard_map/pallas_call | solution.py:36
  23.0 0.1 collective-permute-start.13
  23.0 0.0 collective-permute-done.3
  23.1 1.6 %collective-permute-start.4 = (bf16[96,512]{1,0:T(8,128)(2,1)S(1)}, bf16[96,512]{1,0:T(8,128)(2,1)S(1)}, u32[]{:S(2)}, u32[]{:S(2)}) collective-permute-start(bf16[96,512]{1,0:T(8,128)(2,1)S(1)} %add_convert_fusion.1.refs_0_), channel_id=1, source_target_pairs={{0,2},{1,3},{2,0},{3,1},{4,6},{5,7},{6,4},{7,5},{8,10},{9,11},{10,... | collective-permute-start | bytes 294920 | tf_op jit(solution)/shard_map/ppermute | solution.py:284
  24.7 0.0 collective-permute-done.13
  24.7 1.3 %collective-permute-start.14 = (bf16[144,512]{1,0:T(8,128)(2,1)S(1)}, bf16[144,512]{1,0:T(8,128)(2,1)S(1)}, u32[]{:S(2)}, u32[]{:S(2)}) collective-permute-start(bf16[144,512]{1,0:T(8,128)(2,1)S(1)} %add_convert_fusion.refs_0_), channel_id=1, source_target_pairs={{0,2},{1,3},{2,0},{3,1},{4,6},{5,7},{6,4},{7,5},{8,10},{9,11},{10,... | collective-permute-start | bytes 442376 | tf_op jit(solution)/shard_map/ppermute | solution.py:284
  26.0 0.0 collective-permute-done.5
  26.1 0.8 %collective-permute-start.6 = (bf16[48,512]{1,0:T(8,128)(2,1)S(1)}, bf16[48,512]{1,0:T(8,128)(2,1)S(1)}, u32[]{:S(2)}, u32[]{:S(2)}) collective-permute-start(bf16[48,512]{1,0:T(8,128)(2,1)S(1)} %add_convert_fusion.3.refs_2_), channel_id=1, source_target_pairs={{0,2},{1,3},{2,0},{3,1},{4,6},{5,7},{6,4},{7,5},{8,10},{9,11},{10,... | collective-permute-start | bytes 147464 | tf_op jit(solution)/shard_map/ppermute | solution.py:284
  26.9 5.6 %collective-permute-done.6.refs_3_ = bf16[48,512]{1,0:T(8,128)(2,1)S(1)} collective-permute-done((bf16[48,512]{1,0:T(8,128)(2,1)S(1)}, bf16[48,512]{1,0:T(8,128)(2,1)S(1)}, u32[]{:S(2)}, u32[]{:S(2)}) %collective-permute-start.6) | collective-permute-done | bytes 49184 | tf_op jit(solution)/shard_map/ppermute | solution.py:284
  32.5 0.0 collective-permute-done.4.refs_1_
  32.6 1.2 %shard_map.106 = (bf16[96,512]{1,0:T(8,128)(2,1)S(1)}, bf16[96,512]{1,0:T(8,128)(2,1)S(1)}, bf16[96,512]{1,0:T(8,128)(2,1)S(1)}, bf16[24,896]{1,0:T(8,128)(2,1)S...) custom-call(bf16[96,512]{1,0:T(8,128)(2,1)S(1)} %add_convert_fusion.1.refs_0_, ...), custom_call_target="tpu_custom_call" | custom-call | tf_op jit(solution)/shard_map/pallas_call | solution.py:36
  33.8 1.6 %collective-permute-start.7 = (bf16[24,896]{1,0:T(8,128)(2,1)S(1)}, bf16[24,896]{1,0:T(8,128)(2,1)S(1)}, u32[]{:S(2)}, u32[]{:S(2)}) collective-permute-start(bf16[24,896]{1,0:T(8,128)(2,1)S(1)} %get-tuple-element.31), channel_id=1, source_target_pairs={{0,4},{4,0},{8,12},{12,8},{16,20},{20,16},{24,28},{28,24},{1,5},{5... | collective-permute-start | bytes 129032 | tf_op jit(solution)/shard_map/ppermute | solution.py:278
  35.4 0.5 collective-permute-start.9
  35.9 0.0 collective-permute-done.14.refs_1_
  35.9 1.2 %shard_map.108 = (bf16[96,512]{1,0:T(8,128)(2,1)S(1)}, bf16[96,512]{1,0:T(8,128)(2,1)S(1)}, bf16[96,512]{1,0:T(8,128)(2,1)S(1)}, bf16[48,896]{1,0:T(8,128)(2,1)S(1)}, bf16[48,896]{1,0:T(8,128)(2,1)S(1)}) custom-call(bf16[144,512]{1,0:T(8,128)(2,1)S(1)} %add_convert_fusion.refs_0_, bf16[144,512]{1,0:T(8,128)(2,1)S(1)} %collective-permute-done.14.refs_1_, ...), custom_call_target="tpu_custom_call" | custom-call | tf_op jit(solution)/shard_map/pallas_call | solution.py:36
  37.2 1.6 %collective-permute-start.15 = (bf16[48,896]{1,0:T(8,128)(2,1)S(1)}, bf16[48,896]{1,0:T(8,128)(2,1)S(1)}, u32[]{:S(2)}, u32[]{:S(2)}) collective-permute-start(bf16[48,896]{1,0:T(8,128)(2,1)S(1)} %get-tuple-element.39), channel_id=1, source_target_pairs={{0,4},{4,0},{8,12},{12,8},{16,20},{20,16},{24,28},{28,24},{1,5},{5... | collective-permute-start | bytes 258056 | tf_op jit(solution)/shard_map/ppermute | solution.py:278
  38.7 0.0 collective-permute-done.7
  38.7 5.7 %collective-permute-start.8 = (bf16[24,896]{1,0:T(8,128)(2,1)S(1)}, bf16[24,896]{1,0:T(8,128)(2,1)S(1)}, u32[]{:S(2)}, u32[]{:S(2)}) collective-permute-start(bf16[24,896]{1,0:T(8,128)(2,1)S(1)} %add_convert_fusion.5), channel_id=1, source_target_pairs={{0,16},{4,20},{8,24},{12,28},{16,0},{20,4},{24,8},{28,12},{1,17},{... | collective-permute-start | bytes 129032 | tf_op jit(solution)/shard_map/ppermute | solution.py:275
  44.5 0.0 collective-permute-done.15
  44.5 1.1 %collective-permute-start.16 = (bf16[24,896]{1,0:T(8,128)(2,1)S(1)}, bf16[24,896]{1,0:T(8,128)(2,1)S(1)}, u32[]{:S(2)}, u32[]{:S(2)}) collective-permute-start(bf16[24,896]{1,0:T(8,128)(2,1)S(1)} %get-tuple-element.48), channel_id=1, source_target_pairs={{0,8},{4,12},{8,0},{12,4},{16,24},{20,28},{24,16},{28,20},{1,9},{5... | collective-permute-start | bytes 129032 | tf_op jit(solution)/shard_map/ppermute | solution.py:275
  45.6 0.0 collective-permute-done.9
  45.6 3.5 %collective-permute-start.10 = (bf16[24,896]{1,0:T(8,128)(2,1)S(1)}, bf16[24,896]{1,0:T(8,128)(2,1)S(1)}, u32[]{:S(2)}, u32[]{:S(2)}) collective-permute-start(bf16[24,896]{1,0:T(8,128)(2,1)S(1)} %add_convert_fusion.4), channel_id=1, source_target_pairs={{0,24},{4,28},{8,16},{12,20},{16,8},{20,12},{24,0},{28,4},{1,25},{... | collective-permute-start | bytes 129032 | tf_op jit(solution)/shard_map/ppermute | solution.py:275
  49.1 1.7 %shard_map.112 = bf16[1,512,1792]{2,1,0:T(8,128)(2,1)} custom-call(bf16[48,896]{1,0:T(8,128)(2,1)S(1)} %get-tuple-element.36.refs_0_, bf16[48,896]{1,0:T(8,128)(2,1)S(1)} %collective-permute-done.11.refs_1_, bf16[96,896]{1,0:T(8,128)(2,1)S(1)} %collective-permute-done.12.refs_2_, bf16[48,896]{1,0:T(8,128)(2,1)S(1)} %collective-permute-done.refs_0_.refs_3_, ...), custom_call_target="tpu_custom_call" | custom-call | tf_op jit(solution)/shard_map/pallas_call | solution.py:380
  50.8 2.3 %shard_map.111 = (bf16[1,1792,512]{2,1,0:T(8,128)(2,1)}, bf16[1,1792,512]{2,1,0:T(8,128)(2,1)}) custom-call(bf16[48,896]{1,0:T(8,128)(2,1)S(1)} %get-tuple-element.36.refs_0_, bf16[48,896]{1,0:T(8,128)(2,1)S(1)} %collective-permute-done.11.refs_1_, bf16[96,896]{1,0:T(8,128)(2,1)S(1)} %collective-permute-done.12.refs_2_, ...), custom_call_target="tpu_custom_call" | custom-call | tf_op jit(solution)/shard_map/pallas_call | solution.py:370
  53.1 0.0 collective-permute-done.16.refs_1_
  53.1 0.4 shard_map.109.refs_4_
  53.5 0.0 collective-permute-done.8.refs_0_
  53.6 0.0 collective-permute-done.10.refs_1_
  53.6 1.3 %shard_map.110 = bf16[256,1792]{1,0:T(8,128)(2,1)} custom-call(bf16[24,896]{1,0:T(8,128)(2,1)S(1)} %collective-permute-done.8.refs_0_, bf16[24,896]{1,0:T(8,128)(2,1)S(1)} %collective-permute-done.10.refs_1_, bf16[96,256]{1,0:T(8,128)(2,1)S(1)} %get-tuple-element.34.refs_2_, bf16[96,256]{1,0:T(8,128)(2,1)S(1)} %get-tuple-element.35.refs_3_, ...), custom_call_target="tpu_custom_call" | custom-call | tf_op jit(solution)/shard_map/pallas_call | solution.py:394
  (9 shorter events, 0.2 us)
Async XLA Ops:
  2.5 10.4 %collective-permute-start = (bf16[48,896]{1,0:T(8,128)(2,1)S(1)}, bf16[48,896]{1,0:T(8,128)(2,1)S(1)}, u32[]{:S(2)}, u32[]{:S(2)}) collective-permute-start(bf16[48,896]{1,0:T(8,128)(2,1)S(1)} %get-tuple-element.26), channel_id=1, source_target_pairs={{0,16},{4,20},{8,24},{12,28},{16,0},{20,4},{24,8},{28,12},{1,17},{... | collective-permute-start | bytes 258056 | tf_op jit(solution)/shard_map/ppermute | solution.py:275
  6.6 6.8 %collective-permute-start.1 = (bf16[48,896]{1,0:T(8,128)(2,1)S(1)}, bf16[48,896]{1,0:T(8,128)(2,1)S(1)}, u32[]{:S(2)}, u32[]{:S(2)}) collective-permute-start(bf16[48,896]{1,0:T(8,128)(2,1)S(1)} %get-tuple-element.27), channel_id=1, source_target_pairs={{0,24},{4,28},{8,16},{12,20},{16,8},{20,12},{24,0},{28,4},{1,25},{... | collective-permute-start | bytes 258056 | tf_op jit(solution)/shard_map/ppermute | solution.py:275
  8.0 7.3 %collective-permute-start.11 = (bf16[48,896]{1,0:T(8,128)(2,1)S(1)}, bf16[48,896]{1,0:T(8,128)(2,1)S(1)}, u32[]{:S(2)}, u32[]{:S(2)}) collective-permute-start(bf16[48,896]{1,0:T(8,128)(2,1)S(1)} %get-tuple-element.37), channel_id=1, source_target_pairs={{0,8},{4,12},{8,0},{12,4},{16,24},{20,28},{24,16},{28,20},{1,9},{5... | collective-permute-start | bytes 258056 | tf_op jit(solution)/shard_map/ppermute | solution.py:275
  13.5 6.2 %collective-permute-start.2 = (bf16[96,896]{1,0:T(8,128)(2,1)S(1)}, bf16[96,896]{1,0:T(8,128)(2,1)S(1)}, u32[]{:S(2)}, u32[]{:S(2)}) collective-permute-start(bf16[96,896]{1,0:T(8,128)(2,1)S(1)} %pad_maximum_fusion), channel_id=1, source_target_pairs={{0,4},{4,0},{8,12},{12,8},{16,20},{20,16},{24,28},{28,24},{1,5},{5... | collective-permute-start | bytes 516104 | tf_op jit(solution)/shard_map/ppermute | solution.py:278
  15.3 4.3 %copy-start = (bf16[1,1792,512]{2,1,0:T(8,128)(2,1)S(1)}, bf16[1,1792,512]{2,1,0:T(8,128)(2,1)}, u32[]{:S(2)}) copy-start(bf16[1,1792,512]{2,1,0:T(8,128)(2,1)} %refs_2_.1) | copy-start | bytes 5505028
  15.3 6.4 %collective-permute-start.12 = (bf16[96,896]{1,0:T(8,128)(2,1)S(1)}, bf16[96,896]{1,0:T(8,128)(2,1)S(1)}, u32[]{:S(2)}, u32[]{:S(2)}) collective-permute-start(bf16[96,896]{1,0:T(8,128)(2,1)S(1)} %pad_maximum_fusion.1), channel_id=1, source_target_pairs={{0,4},{4,0},{8,12},{12,8},{16,20},{20,16},{24,28},{28,24},{1,5},{5... | collective-permute-start | bytes 516104 | tf_op jit(solution)/shard_map/ppermute | solution.py:278
  20.3 2.7 %collective-permute-start.3 = (bf16[96,512]{1,0:T(8,128)(2,1)S(1)}, bf16[96,512]{1,0:T(8,128)(2,1)S(1)}, u32[]{:S(2)}, u32[]{:S(2)}) collective-permute-start(bf16[96,512]{1,0:T(8,128)(2,1)S(1)} %shard_map.104), channel_id=1, source_target_pairs={{0,1},{1,0},{2,3},{3,2},{4,5},{5,4},{6,7},{7,6},{8,9},{9,8},{10,11... | collective-permute-start | bytes 294920 | tf_op jit(solution)/shard_map/ppermute | solution.py:284
  21.1 4.9 %collective-permute-start.5 = (bf16[48,512]{1,0:T(8,128)(2,1)S(1)}, bf16[48,512]{1,0:T(8,128)(2,1)S(1)}, u32[]{:S(2)}, u32[]{:S(2)}) collective-permute-start(bf16[48,512]{1,0:T(8,128)(2,1)S(1)} %shard_map.105), channel_id=1, source_target_pairs={{0,1},{1,0},{2,3},{3,2},{4,5},{5,4},{6,7},{7,6},{8,9},{9,8},{10,11... | collective-permute-start | bytes 147464 | tf_op jit(solution)/shard_map/ppermute | solution.py:284
  23.0 1.7 %collective-permute-start.13 = (bf16[144,512]{1,0:T(8,128)(2,1)S(1)}, bf16[144,512]{1,0:T(8,128)(2,1)S(1)}, u32[]{:S(2)}, u32[]{:S(2)}) collective-permute-start(bf16[144,512]{1,0:T(8,128)(2,1)S(1)} %shard_map.107), channel_id=1, source_target_pairs={{0,1},{1,0},{2,3},{3,2},{4,5},{5,4},{6,7},{7,6},{8,9},{9,8},{10,11... | collective-permute-start | bytes 442376 | tf_op jit(solution)/shard_map/ppermute | solution.py:284
  23.1 9.5 %collective-permute-start.4 = (bf16[96,512]{1,0:T(8,128)(2,1)S(1)}, bf16[96,512]{1,0:T(8,128)(2,1)S(1)}, u32[]{:S(2)}, u32[]{:S(2)}) collective-permute-start(bf16[96,512]{1,0:T(8,128)(2,1)S(1)} %add_convert_fusion.1.refs_0_), channel_id=1, source_target_pairs={{0,2},{1,3},{2,0},{3,1},{4,6},{5,7},{6,4},{7,5},{8,10},{9,11},{10,... | collective-permute-start | bytes 294920 | tf_op jit(solution)/shard_map/ppermute | solution.py:284
  24.7 11.2 %collective-permute-start.14 = (bf16[144,512]{1,0:T(8,128)(2,1)S(1)}, bf16[144,512]{1,0:T(8,128)(2,1)S(1)}, u32[]{:S(2)}, u32[]{:S(2)}) collective-permute-start(bf16[144,512]{1,0:T(8,128)(2,1)S(1)} %add_convert_fusion.refs_0_), channel_id=1, source_target_pairs={{0,2},{1,3},{2,0},{3,1},{4,6},{5,7},{6,4},{7,5},{8,10},{9,11},{10,... | collective-permute-start | bytes 442376 | tf_op jit(solution)/shard_map/ppermute | solution.py:284
  26.1 6.5 %collective-permute-start.6 = (bf16[48,512]{1,0:T(8,128)(2,1)S(1)}, bf16[48,512]{1,0:T(8,128)(2,1)S(1)}, u32[]{:S(2)}, u32[]{:S(2)}) collective-permute-start(bf16[48,512]{1,0:T(8,128)(2,1)S(1)} %add_convert_fusion.3.refs_2_), channel_id=1, source_target_pairs={{0,2},{1,3},{2,0},{3,1},{4,6},{5,7},{6,4},{7,5},{8,10},{9,11},{10,... | collective-permute-start | bytes 147464 | tf_op jit(solution)/shard_map/ppermute | solution.py:284
  33.8 4.9 %collective-permute-start.7 = (bf16[24,896]{1,0:T(8,128)(2,1)S(1)}, bf16[24,896]{1,0:T(8,128)(2,1)S(1)}, u32[]{:S(2)}, u32[]{:S(2)}) collective-permute-start(bf16[24,896]{1,0:T(8,128)(2,1)S(1)} %get-tuple-element.31), channel_id=1, source_target_pairs={{0,4},{4,0},{8,12},{12,8},{16,20},{20,16},{24,28},{28,24},{1,5},{5... | collective-permute-start | bytes 129032 | tf_op jit(solution)/shard_map/ppermute | solution.py:278
  35.4 10.2 %collective-permute-start.9 = (bf16[24,896]{1,0:T(8,128)(2,1)S(1)}, bf16[24,896]{1,0:T(8,128)(2,1)S(1)}, u32[]{:S(2)}, u32[]{:S(2)}) collective-permute-start(bf16[24,896]{1,0:T(8,128)(2,1)S(1)} %get-tuple-element.33), channel_id=1, source_target_pairs={{0,4},{4,0},{8,12},{12,8},{16,20},{20,16},{24,28},{28,24},{1,5},{5... | collective-permute-start | bytes 129032 | tf_op jit(solution)/shard_map/ppermute | solution.py:278
  37.2 7.3 %collective-permute-start.15 = (bf16[48,896]{1,0:T(8,128)(2,1)S(1)}, bf16[48,896]{1,0:T(8,128)(2,1)S(1)}, u32[]{:S(2)}, u32[]{:S(2)}) collective-permute-start(bf16[48,896]{1,0:T(8,128)(2,1)S(1)} %get-tuple-element.39), channel_id=1, source_target_pairs={{0,4},{4,0},{8,12},{12,8},{16,20},{20,16},{24,28},{28,24},{1,5},{5... | collective-permute-start | bytes 258056 | tf_op jit(solution)/shard_map/ppermute | solution.py:278
  38.7 14.8 %collective-permute-start.8 = (bf16[24,896]{1,0:T(8,128)(2,1)S(1)}, bf16[24,896]{1,0:T(8,128)(2,1)S(1)}, u32[]{:S(2)}, u32[]{:S(2)}) collective-permute-start(bf16[24,896]{1,0:T(8,128)(2,1)S(1)} %add_convert_fusion.5), channel_id=1, source_target_pairs={{0,16},{4,20},{8,24},{12,28},{16,0},{20,4},{24,8},{28,12},{1,17},{... | collective-permute-start | bytes 129032 | tf_op jit(solution)/shard_map/ppermute | solution.py:275
  44.5 8.6 %collective-permute-start.16 = (bf16[24,896]{1,0:T(8,128)(2,1)S(1)}, bf16[24,896]{1,0:T(8,128)(2,1)S(1)}, u32[]{:S(2)}, u32[]{:S(2)}) collective-permute-start(bf16[24,896]{1,0:T(8,128)(2,1)S(1)} %get-tuple-element.48), channel_id=1, source_target_pairs={{0,8},{4,12},{8,0},{12,4},{16,24},{20,28},{24,16},{28,20},{1,9},{5... | collective-permute-start | bytes 129032 | tf_op jit(solution)/shard_map/ppermute | solution.py:275
  45.6 8.0 %collective-permute-start.10 = (bf16[24,896]{1,0:T(8,128)(2,1)S(1)}, bf16[24,896]{1,0:T(8,128)(2,1)S(1)}, u32[]{:S(2)}, u32[]{:S(2)}) collective-permute-start(bf16[24,896]{1,0:T(8,128)(2,1)S(1)} %add_convert_fusion.4), channel_id=1, source_target_pairs={{0,24},{4,28},{8,16},{12,20},{16,8},{20,12},{24,0},{28,4},{1,25},{... | collective-permute-start | bytes 129032 | tf_op jit(solution)/shard_map/ppermute | solution.py:275

commit v3 on v2

--- a/solution.py
+++ b/solution.py
@@ -11,7 +11,6 @@
 CAP = 12
 PAIR = 2 * CAP
 BF16, F32 = jnp.bfloat16, jnp.float32
-OVER_COLUMNS = (((1,), (1,)), ((), ()))
 OVER_ROWS = (((0,), (0,)), ((), ()))
 
 
@@ -64,9 +63,10 @@
     outs = refs[3 + 2 * halves : -4]
     held, ids_ref, w_ref, sems = refs[-4:]
     messages, (p0_ref, p1_ref) = outs[:window], outs[window:]
+    top, tok = ids_ref.shape
     copies = [pltpu.make_async_copy(src, dst, sem) for src, dst, sem in zip(
         (ids_hbm, w_hbm) + tuple(sources),
-        (ids_ref, w_ref) + tuple(held.at[i] for i in range(4)),
+        (ids_ref, w_ref) + tuple(held.at[i // 2, tok * (i % 2) : tok * (i % 2 + 1)] for i in range(4)),
         [sems.at[i] for i in range(6)],
     )]
     for copy in copies:
@@ -97,25 +97,29 @@
     p0, p1 = p0.astype(BF16), p1.astype(BF16)
     p0_ref[...] = p0
     p1_ref[...] = p1
+    both = jnp.concatenate([p0, p1], axis=1)
     copies[2].wait()
     copies[3].wait()
-    message = dot(p0, held[0]) + dot(p1, held[1])
+    message = dot(both, held[0])
     for d in range(window):
         messages[d][:PAIR] = message[d * PAIR : (d + 1) * PAIR].astype(BF16)
     copies[4].wait()
     copies[5].wait()
-    message = (dot(p0, held[2]) + dot(p1, held[3])) * scale
+    message = dot(both, held[1]) * scale
     for d in range(window):
         messages[d][PAIR:] = message[d * PAIR : (d + 1) * PAIR].astype(BF16)
 
 
-def load_kernel(*refs):
-    n = (len(refs) - 1) // 2
-    copies = [pltpu.make_async_copy(refs[i], refs[n + i], refs[-1].at[i]) for i in range(n)]
-    for copy in copies:
-        copy.start()
-    for copy in copies:
-        copy.wait()
+def load_kernel(gate_ref, up_hbm, down_hbm, up_ref, gate_t, up_t, down_t, down_ref, sems):
+    up_copy = pltpu.make_async_copy(up_hbm, up_ref, sems.at[0])
+    down_copy = pltpu.make_async_copy(down_hbm, down_ref, sems.at[1])
+    up_copy.start()
+    down_copy.start()
+    gate_t[...] = gate_ref[0].T
+    up_copy.wait()
+    up_t[...] = up_ref[0].T
+    down_copy.wait()
+    down_t[...] = down_ref[0].T
 
 
 def joined(refs):
@@ -149,7 +153,7 @@
     own, other, (down_ref, out_ref) = refs[:count], refs[count], refs[count + 1 :]
     n = count * PAIR
     grads = unfolded(received(own, other, 1))
-    part = dot(grads, down_ref[0], OVER_COLUMNS)
+    part = dot(grads, down_ref[...])
     start = out_ref.shape[0] - n
     out_ref[start:] = jnp.where(upper(n, part.shape[1]), part[:n], part[n:]).astype(BF16)
 
@@ -180,7 +184,7 @@
     gate_delta, up_delta = gate_delta.astype(BF16), up_delta.astype(BF16)
     gd_ref[...] = gate_delta
     ud_ref[...] = up_delta
-    back = dot(gate_delta, gate_ref[0], OVER_COLUMNS) + dot(up_delta, up_ref[0], OVER_COLUMNS)
+    back = dot(gate_delta, gate_ref[...]) + dot(up_delta, up_ref[...])
     back = jnp.where(upper(2 * n, w), back[:, :w], back[:, w:]).astype(BF16)
     for i, (start, size) in enumerate(sizes):
         backs[2 * i][...] = back[start : start + size]
@@ -238,24 +242,20 @@
         copy.wait()
 
 
-def early_kernel(count, *refs):
-    blocks, (p0_ref, p1_ref, total_ref) = refs[:count], refs[count:]
+def combine_kernel(count, *refs):
+    blocks, (p0_ref, p1_ref) = refs[:count], refs[count : count + 2]
+    outs, (held, sems) = refs[count + 2 : -2], refs[-2:]
     rows = joined(blocks).astype(BF16)
-    n = rows.shape[0]
-    total_ref[0] = dot(p0_ref[:n], rows, OVER_ROWS)
-    total_ref[1] = dot(p1_ref[:n], rows, OVER_ROWS)
-
-
-def combine_kernel(count, *refs):
-    blocks, (p0_ref, p1_ref, total_ref) = refs[:count], refs[count : count + 3]
-    outs, (held, sems) = refs[count + 3 : -2], refs[-2:]
-    rows = joined(blocks).astype(BF16)
-    start = p0_ref.shape[0] - rows.shape[0]
     copies = []
-    for i, (p_ref, out) in enumerate(zip((p0_ref, p1_ref), columns(outs))):
-        held[i] = (total_ref[i] + dot(p_ref[start:], rows, OVER_ROWS)).astype(BF16)
-        copies.append(pltpu.make_async_copy(held.at[i], out, sems.at[i]))
-        copies[-1].start()
+    tok = p0_ref.shape[1]
+    for k in range(2):
+        here = slice(k * tok // 2, (k + 1) * tok // 2)
+        for i, (p_ref, out) in enumerate(zip((p0_ref, p1_ref), columns(outs))):
+            held[i, here] = dot(p_ref[:, here], rows, OVER_ROWS).astype(BF16)
+            copies.append(
+                pltpu.make_async_copy(held.at[i, here], out.at[here], sems.at[2 * k + i])
+            )
+            copies[-1].start()
     for copy in copies:
         copy.wait()
 
@@ -302,7 +302,7 @@
         in_specs=[smem] + [hbm] * (2 + len(far)),
         out_specs=(space,) * (window + 2),
         scratch_shapes=[
-            pltpu.VMEM((4, tok, w), BF16),
+            pltpu.VMEM((2, 2 * tok, w), BF16),
             pltpu.VMEM(expert_ids.shape[::-1], jnp.int32),
             pltpu.VMEM(route_weight.shape[::-1], F32),
             pltpu.SemaphoreType.DMA((6,)),
@@ -311,15 +311,16 @@
     )(first_expert, *(in_hbm(v) for v in (expert_ids.T, route_weight.T, *far)))
     p0, p1 = placed[window:]
     arrived = [placed[0]] + [across(placed[k], k) for k in range(1, window)]
-    weights = (up_weight, down_weight)
-    up_w, down_w = pl.pallas_call(
+    up_w, gate_t, up_t, down_t = pl.pallas_call(
         load_kernel,
-        out_shape=tuple(shape(v.shape) for v in weights),
-        in_specs=[hbm] * 2,
-        out_specs=(space,) * 2,
-        scratch_shapes=[pltpu.SemaphoreType.DMA((2,))],
+        out_shape=(shape(up_weight.shape),)
+        + (shape((hidden, slab)),) * 2
+        + (shape((slab, hidden)),),
+        in_specs=[space, hbm, hbm],
+        out_specs=(space,) * 4,
+        scratch_shapes=[pltpu.VMEM(down_weight.shape, BF16), pltpu.SemaphoreType.DMA((2,))],
         compiler_params=params,
-    )(*(in_hbm(v) for v in weights))
+    )(gate_weight, in_hbm(up_weight), in_hbm(down_weight))
 
     chunks = [range(window // 2), range(window // 2, window)]
     counts = tuple(len(chunk) for chunk in chunks)
@@ -333,7 +334,7 @@
             part = call(
                 functools.partial(product_kernel, count),
                 shape((3 * n, hidden)),
-                *take, gate_weight, up_w, down_w,
+                *take, gate_weight, up_w, down_t,
             )
             sums.append(reduced(part))
             continue
@@ -342,7 +343,7 @@
             shape((2 * n, hidden)),
             *take, gate_weight, up_w,
         )
-        h_part = call(functools.partial(hidden_kernel, count), shape((n, hidden)), *take, down_w)
+        h_part = call(functools.partial(hidden_kernel, count), shape((n, hidden)), *take, down_t)
         sums.append(reduced(part) + reduced(h_part))
     deltas, home = [], [None] * window
     for i, count in enumerate(counts):
@@ -354,7 +355,7 @@
             functools.partial(delta_kernel, len(sums[i]) // 2, sizes),
             (shape((2 * n, hidden)),) * 3
             + tuple(shape((size, w)) for _, size in sizes for _ in range(2)),
-            *sums[i], gate_weight, up_w,
+            *sums[i], gate_t, up_t,
         )
         deltas.append(delta[:3])
         for j, piece in enumerate(pieces):
@@ -386,19 +387,15 @@
         compiler_params=params,
     )(*down_args)
     down_grad = down_grad[0] if aligned else jnp.concatenate(down_grad, axis=2)
-    early, late = [home[d] for d in chunks[0]], [home[d] for d in chunks[1]]
-    total = call(
-        functools.partial(early_kernel, len(early)), shape((2, tok, w), F32), *early, p0, p1
-    )
     out_shape = (shape((tok, slab)),) if aligned else (shape((tok, w)),) * 2
     out = pl.pallas_call(
-        functools.partial(combine_kernel, len(late)),
+        functools.partial(combine_kernel, len(home)),
         out_shape=out_shape,
-        in_specs=[space] * (len(late) + 3),
+        in_specs=[space] * (len(home) + 2),
         out_specs=(hbm,) * len(out_shape),
-        scratch_shapes=[pltpu.VMEM((2, tok, w), BF16), pltpu.SemaphoreType.DMA((2,))],
+        scratch_shapes=[pltpu.VMEM((2, tok, w), BF16), pltpu.SemaphoreType.DMA((4,))],
         compiler_params=params,
-    )(*late, p0, p1, total)
+    )(*home, p0, p1)
     token_grad = out[0] if aligned else jnp.concatenate(out, axis=1)
     return token_grad, gate_grad, up_grad, down_grad
 

time: 55 us -> 51.5 us (0.936)
  starting transfers between devices: 26.4 us -> 23.7 us
  Pallas kernels: 14.8 us -> 13.5 us
    ppermute x6, starting transfers between devices: 16 us -> 13.1 us  [across(): return lax.ppermute(v, 'expert', perm)]
    ppermute x5, waiting for transfers between devices: 1.68 us -> 3.76 us  [other_half(): return lax.ppermute(v, 'expert', [(e, e ^ 1) for e in range(expert_count)])]
    pallas_call x6 -> x5, Pallas kernels: 5.58 us -> 3.66 us  [call(): pl.pallas_call(kernel, out_shape=outs, in_specs=[space] * len(args), out_...]
    ppermute x6, waiting for transfers between devices: 5.66 us -> 4.14 us  [reduced(): got = lax.ppermute(part, 'fsdp', [(f, f ^ bit) for f in range(fsdp_count)])]
  transfers between devices with their start and end apart: 17 -> 17, of which waited for: 4 -> 7; matrix products, arithmetic and copies ran while one was open for 0% -> 0% of each run, Pallas kernels for 21% -> 20%
where the time goes in v3:
time: 51.5 us; the launch traced here: 51.3 us
  starting transfers between devices  23.7 us (46%)
  Pallas kernels  13.5 us (26%)
  waiting for transfers between devices  13.1 us (25%)
  between operations  0.8 us (2%)
    ppermute x6, starting transfers between devices, across(): return lax.ppermute(v, 'expert', perm)  13.1 us
    ppermute x5, starting transfers between devices, other_half(): return lax.ppermute(v, 'expert', [(e, e ^ 1) for e in range(expert_count)])  6.21 us
    ppermute x6, waiting for transfers between devices, across(): return lax.ppermute(v, 'expert', perm)  5.24 us
    ppermute x6, starting transfers between devices, reduced(): got = lax.ppermute(part, 'fsdp', [(f, f ^ bit) for f in range(fsdp_count)])  4.44 us
    ppermute x6, waiting for transfers between devices, reduced(): got = lax.ppermute(part, 'fsdp', [(f, f ^ bit) for f in range(fsdp_count)])  4.14 us
    ppermute x5, waiting for transfers between devices, other_half(): return lax.ppermute(v, 'expert', [(e, e ^ 1) for e in range(expert_count)])  3.76 us
    pallas_call x5, Pallas kernels, call(): pl.pallas_call(kernel, out_shape=outs, in_specs=[space] * len(args), out_...  3.66 us
    pallas_call x1, Pallas kernels, body(): pl.pallas_call(load_kernel, out_shape=(shape(up_weight.shape),) + (shape(...  2.6 us
  transfers between devices with their start and end apart: 17, of which 7 were waited for; matrix products, arithmetic and copies ran while one was open for 0% of the time, Pallas kernels for 20%

profile of v3, /device:TPU:0, one launch (start us, length us, event | category | flops | bytes accessed | tf_op | source)
XLA Modules:
  0.0 51.3 jit_solution(6852886399738875691)
XLA Ops:
  0.6 0.0 copy-start
  0.6 2.0 %shard_map.102 = (bf16[48,896]{1,0:T(8,128)(2,1)S(1)}, bf16[48,896]{1,0:T(8,128)(2,1)S(1)}, bf16[48,896]{1,0:T(8,128)(2,1)S(1)}, bf16[48,896]{1,0:T(8,128)(2,1)S...) custom-call(s32[1]{0:T(128)} %bitcast.refs_0_, s32[8,256]{1,0:T(8,128)} %bitcast.3, f32[8,256]{1,0:T(8,128)} %bitcast.4, ...), custom_call_target="tpu_custom_call" | custom-call | tf_op jit(solution)/shard_map/pallas_call | solution.py:299
  2.6 4.1 %collective-permute-start.6 = (bf16[48,896]{1,0:T(8,128)(2,1)S(1)}, bf16[48,896]{1,0:T(8,128)(2,1)S(1)}, u32[]{:S(2)}, u32[]{:S(2)}) collective-permute-start(bf16[48,896]{1,0:T(8,128)(2,1)S(1)} %get-tuple-element.36), channel_id=1, source_target_pairs={{0,16},{4,20},{8,24},{12,28},{16,0},{20,4},{24,8},{28,12},{1,17},{... | collective-permute-start | bytes 258056 | tf_op jit(solution)/shard_map/ppermute | solution.py:275
  6.8 1.3 %collective-permute-start.7 = (bf16[48,896]{1,0:T(8,128)(2,1)S(1)}, bf16[48,896]{1,0:T(8,128)(2,1)S(1)}, u32[]{:S(2)}, u32[]{:S(2)}) collective-permute-start(bf16[48,896]{1,0:T(8,128)(2,1)S(1)} %get-tuple-element.37), channel_id=1, source_target_pairs={{0,24},{4,28},{8,16},{12,20},{16,8},{20,12},{24,0},{28,4},{1,25},{... | collective-permute-start | bytes 258056 | tf_op jit(solution)/shard_map/ppermute | solution.py:275
  8.1 0.2 collective-permute-start
  8.3 4.7 %collective-permute-done.6.refs_0_.refs_3_ = bf16[48,896]{1,0:T(8,128)(2,1)S(1)} collective-permute-done((bf16[48,896]{1,0:T(8,128)(2,1)S(1)}, bf16[48,896]{1,0:T(8,128)(2,1)S(1)}, u32[]{:S(2)}, u32[]{:S(2)}) %collective-permute-start.6) | collective-permute-done | bytes 86048 | tf_op jit(solution)/shard_map/ppermute | solution.py:275
  13.1 0.5 collective-permute-done.7.refs_1_.refs_4_
  13.6 1.8 %collective-permute-start.8 = (bf16[96,896]{1,0:T(8,128)(2,1)S(1)}, bf16[96,896]{1,0:T(8,128)(2,1)S(1)}, u32[]{:S(2)}, u32[]{:S(2)}) collective-permute-start(bf16[96,896]{1,0:T(8,128)(2,1)S(1)} %pad_maximum_fusion.1), channel_id=1, source_target_pairs={{0,4},{4,0},{8,12},{12,8},{16,20},{20,16},{24,28},{28,24},{1,5},{5... | collective-permute-start | bytes 516104 | tf_op jit(solution)/shard_map/ppermute | solution.py:278
  15.4 0.0 collective-permute-done.refs_1_
  15.4 0.5 %collective-permute-start.1 = (bf16[96,896]{1,0:T(8,128)(2,1)S(1)}, bf16[96,896]{1,0:T(8,128)(2,1)S(1)}, u32[]{:S(2)}, u32[]{:S(2)}) collective-permute-start(bf16[96,896]{1,0:T(8,128)(2,1)S(1)} %pad_maximum_fusion), channel_id=1, source_target_pairs={{0,4},{4,0},{8,12},{12,8},{16,20},{20,16},{24,28},{28,24},{1,5},{5... | collective-permute-start | bytes 516104 | tf_op jit(solution)/shard_map/ppermute | solution.py:278
  16.0 0.0 copy-done
  16.0 2.6 %shard_map.103 = (bf16[1,1792,512]{2,1,0:T(8,128)(2,1)S(1)}, bf16[512,1792]{1,0:T(8,128)(2,1)S(1)}, bf16[512,1792]{1,0:T(8,128)(2,1)S(1)}, bf16[1792,512]{1,0:T(8,128)(2,1)S(1)}) custom-call(bf16[1,1792,512]{2,1,0:T(8,128)(2,1)S(1)} %copy-done, bf16[1,1792,512]{2,1,0:T(8,128)(2,1)} %up_hbm.1, bf16[1,512,1792]{2,1,0:T(8,128)(2,1)} %down_hbm.1), custom_call_target="tpu_custom_call" | custom-call | tf_op jit(solution)/shard_map/pallas_call | solution.py:314
  18.6 1.2 %collective-permute-done.8.refs_2_.refs_5_ = bf16[96,896]{1,0:T(8,128)(2,1)S(1)} collective-permute-done((bf16[96,896]{1,0:T(8,128)(2,1)S(1)}, bf16[96,896]{1,0:T(8,128)(2,1)S(1)}, u32[]{:S(2)}, u32[]{:S(2)}) %collective-permute-start.8) | collective-permute-done | bytes 172064 | tf_op jit(solution)/shard_map/ppermute | solution.py:278
  19.8 0.7 %shard_map.106 = bf16[96,512]{1,0:T(8,128)(2,1)S(1)} custom-call(bf16[48,896]{1,0:T(8,128)(2,1)S(1)} %collective-permute-done.6.refs_0_.refs_3_, bf16[48,896]{1,0:T(8,128)(2,1)S(1)} %collective-permute-done.7.refs_1_.refs_4_, bf16[96,896]{1,0:T(8,128)(2,1)S(1)} %collective-permute-done.8.refs_2_.refs_5_, bf16[1,1792,512]{2,1,0:T(8,128)(2,1)S(1)} %copy-done, ...), custom_call_target="tpu_custom_call" | custom-call | tf_op jit(solution)/shard_map/pallas_call | solution.py:35
  20.5 0.1 collective-permute-start.9
  20.6 0.4 shard_map.107
  21.0 0.6 %collective-permute-start.11 = (bf16[48,512]{1,0:T(8,128)(2,1)S(1)}, bf16[48,512]{1,0:T(8,128)(2,1)S(1)}, u32[]{:S(2)}, u32[]{:S(2)}) collective-permute-start(bf16[48,512]{1,0:T(8,128)(2,1)S(1)} %shard_map.107), channel_id=1, source_target_pairs={{0,1},{1,0},{2,3},{3,2},{4,5},{5,4},{6,7},{7,6},{8,9},{9,8},{10,11... | collective-permute-start | bytes 147464 | tf_op jit(solution)/shard_map/ppermute | solution.py:284
  21.6 0.1 collective-permute-done.1.refs_2_
  21.6 1.0 %shard_map.104 = bf16[144,512]{1,0:T(8,128)(2,1)S(1)} custom-call(bf16[48,896]{1,0:T(8,128)(2,1)S(1)} %get-tuple-element.28.refs_0_, bf16[48,896]{1,0:T(8,128)(2,1)S(1)} %collective-permute-done.refs_1_, bf16[96,896]{1,0:T(8,128)(2,1)S(1)} %collective-permute-done.1.refs_2_, bf16[1,1792,512]{2,1,0:T(8,128)(2,1)S(1)} %copy-done, ...), custom_call_target="tpu_custom_call" | custom-call | tf_op jit(solution)/shard_map/pallas_call | solution.py:35
  22.6 0.1 collective-permute-start.2
  22.7 0.0 collective-permute-done.9
  22.7 1.6 %collective-permute-start.10 = (bf16[96,512]{1,0:T(8,128)(2,1)S(1)}, bf16[96,512]{1,0:T(8,128)(2,1)S(1)}, u32[]{:S(2)}, u32[]{:S(2)}) collective-permute-start(bf16[96,512]{1,0:T(8,128)(2,1)S(1)} %add_convert_fusion.1.refs_0_), channel_id=1, source_target_pairs={{0,2},{1,3},{2,0},{3,1},{4,6},{5,7},{6,4},{7,5},{8,10},{9,11},{10,... | collective-permute-start | bytes 294920 | tf_op jit(solution)/shard_map/ppermute | solution.py:284
  24.3 0.0 collective-permute-done.11
  24.3 0.6 %collective-permute-start.12 = (bf16[48,512]{1,0:T(8,128)(2,1)S(1)}, bf16[48,512]{1,0:T(8,128)(2,1)S(1)}, u32[]{:S(2)}, u32[]{:S(2)}) collective-permute-start(bf16[48,512]{1,0:T(8,128)(2,1)S(1)} %add_convert_fusion.3.refs_2_), channel_id=1, source_target_pairs={{0,2},{1,3},{2,0},{3,1},{4,6},{5,7},{6,4},{7,5},{8,10},{9,11},{10,... | collective-permute-start | bytes 147464 | tf_op jit(solution)/shard_map/ppermute | solution.py:284
  24.9 4.1 %collective-permute-done.12.refs_3_ = bf16[48,512]{1,0:T(8,128)(2,1)S(1)} collective-permute-done((bf16[48,512]{1,0:T(8,128)(2,1)S(1)}, bf16[48,512]{1,0:T(8,128)(2,1)S(1)}, u32[]{:S(2)}, u32[]{:S(2)}) %collective-permute-start.12) | collective-permute-done | bytes 49184 | tf_op jit(solution)/shard_map/ppermute | solution.py:284
  29.0 0.0 collective-permute-done.10.refs_1_
  29.0 0.8 %shard_map.108 = (bf16[96,512]{1,0:T(8,128)(2,1)S(1)}, bf16[96,512]{1,0:T(8,128)(2,1)S(1)}, bf16[96,512]{1,0:T(8,128)(2,1)S(1)}, bf16[24,896]{1,0:T(8,128)(2,1)S...) custom-call(bf16[96,512]{1,0:T(8,128)(2,1)S(1)} %add_convert_fusion.1.refs_0_, ...), custom_call_target="tpu_custom_call" | custom-call | tf_op jit(solution)/shard_map/pallas_call | solution.py:35
  29.8 1.6 %collective-permute-start.13 = (bf16[24,896]{1,0:T(8,128)(2,1)S(1)}, bf16[24,896]{1,0:T(8,128)(2,1)S(1)}, u32[]{:S(2)}, u32[]{:S(2)}) collective-permute-start(bf16[24,896]{1,0:T(8,128)(2,1)S(1)} %get-tuple-element.39), channel_id=1, source_target_pairs={{0,4},{4,0},{8,12},{12,8},{16,20},{20,16},{24,28},{28,24},{1,5},{5... | collective-permute-start | bytes 129032 | tf_op jit(solution)/shard_map/ppermute | solution.py:278
  31.4 0.0 collective-permute-done.2
  31.4 1.6 %collective-permute-start.3 = (bf16[144,512]{1,0:T(8,128)(2,1)S(1)}, bf16[144,512]{1,0:T(8,128)(2,1)S(1)}, u32[]{:S(2)}, u32[]{:S(2)}) collective-permute-start(bf16[144,512]{1,0:T(8,128)(2,1)S(1)} %add_convert_fusion.refs_0_), channel_id=1, source_target_pairs={{0,2},{1,3},{2,0},{3,1},{4,6},{5,7},{6,4},{7,5},{8,10},{9,11},{10,... | collective-permute-start | bytes 442376 | tf_op jit(solution)/shard_map/ppermute | solution.py:284
  33.0 0.5 %collective-permute-start.15 = (bf16[24,896]{1,0:T(8,128)(2,1)S(1)}, bf16[24,896]{1,0:T(8,128)(2,1)S(1)}, u32[]{:S(2)}, u32[]{:S(2)}) collective-permute-start(bf16[24,896]{1,0:T(8,128)(2,1)S(1)} %get-tuple-element.41), channel_id=1, source_target_pairs={{0,4},{4,0},{8,12},{12,8},{16,20},{20,16},{24,28},{28,24},{1,5},{5... | collective-permute-start | bytes 129032 | tf_op jit(solution)/shard_map/ppermute | solution.py:278
  33.5 0.4 collective-permute-done.13
  33.9 6.0 %collective-permute-start.14 = (bf16[24,896]{1,0:T(8,128)(2,1)S(1)}, bf16[24,896]{1,0:T(8,128)(2,1)S(1)}, u32[]{:S(2)}, u32[]{:S(2)}) collective-permute-start(bf16[24,896]{1,0:T(8,128)(2,1)S(1)} %add_convert_fusion.5), channel_id=1, source_target_pairs={{0,16},{4,20},{8,24},{12,28},{16,0},{20,4},{24,8},{28,12},{1,17},{... | collective-permute-start | bytes 129032 | tf_op jit(solution)/shard_map/ppermute | solution.py:275
  39.9 0.0 collective-permute-done.3.refs_1_
  39.9 0.8 %shard_map.105 = (bf16[96,512]{1,0:T(8,128)(2,1)S(1)}, bf16[96,512]{1,0:T(8,128)(2,1)S(1)}, bf16[96,512]{1,0:T(8,128)(2,1)S(1)}, bf16[48,896]{1,0:T(8,128)(2,1)S(1)}, bf16[48,896]{1,0:T(8,128)(2,1)S(1)}) custom-call(bf16[144,512]{1,0:T(8,128)(2,1)S(1)} %add_convert_fusion.refs_0_, bf16[144,512]{1,0:T(8,128)(2,1)S(1)} %collective-permute-done.3.refs_1_, ...), custom_call_target="tpu_custom_call" | custom-call | tf_op jit(solution)/shard_map/pallas_call | solution.py:35
  40.6 1.8 %collective-permute-start.4 = (bf16[48,896]{1,0:T(8,128)(2,1)S(1)}, bf16[48,896]{1,0:T(8,128)(2,1)S(1)}, u32[]{:S(2)}, u32[]{:S(2)}) collective-permute-start(bf16[48,896]{1,0:T(8,128)(2,1)S(1)} %get-tuple-element.35), channel_id=1, source_target_pairs={{0,4},{4,0},{8,12},{12,8},{16,20},{20,16},{24,28},{28,24},{1,5},{5... | collective-permute-start | bytes 258056 | tf_op jit(solution)/shard_map/ppermute | solution.py:278
  42.4 0.0 collective-permute-done.15
  42.4 0.6 %collective-permute-start.16 = (bf16[24,896]{1,0:T(8,128)(2,1)S(1)}, bf16[24,896]{1,0:T(8,128)(2,1)S(1)}, u32[]{:S(2)}, u32[]{:S(2)}) collective-permute-start(bf16[24,896]{1,0:T(8,128)(2,1)S(1)} %add_convert_fusion.4), channel_id=1, source_target_pairs={{0,24},{4,28},{8,16},{12,20},{16,8},{20,12},{24,0},{28,4},{1,25},{... | collective-permute-start | bytes 129032 | tf_op jit(solution)/shard_map/ppermute | solution.py:275
  43.0 2.2 %collective-permute-done.4 = bf16[48,896]{1,0:T(8,128)(2,1)S(1)} collective-permute-done((bf16[48,896]{1,0:T(8,128)(2,1)S(1)}, bf16[48,896]{1,0:T(8,128)(2,1)S(1)}, u32[]{:S(2)}, u32[]{:S(2)}) %collective-permute-start.4) | collective-permute-done | bytes 86048 | tf_op jit(solution)/shard_map/ppermute | solution.py:278
  45.2 0.8 %collective-permute-start.5 = (bf16[24,896]{1,0:T(8,128)(2,1)S(1)}, bf16[24,896]{1,0:T(8,128)(2,1)S(1)}, u32[]{:S(2)}, u32[]{:S(2)}) collective-permute-start(bf16[24,896]{1,0:T(8,128)(2,1)S(1)} %get-tuple-element.52), channel_id=1, source_target_pairs={{0,8},{4,12},{8,0},{12,4},{16,24},{20,28},{24,16},{28,20},{1,9},{5... | collective-permute-start | bytes 129032 | tf_op jit(solution)/shard_map/ppermute | solution.py:275
  46.0 1.7 %shard_map.111 = bf16[1,512,1792]{2,1,0:T(8,128)(2,1)} custom-call(bf16[48,896]{1,0:T(8,128)(2,1)S(1)} %get-tuple-element.28.refs_0_, bf16[48,896]{1,0:T(8,128)(2,1)S(1)} %collective-permute-done.refs_1_, bf16[96,896]{1,0:T(8,128)(2,1)S(1)} %collective-permute-done.1.refs_2_, bf16[48,896]{1,0:T(8,128)(2,1)S(1)} %collective-permute-done.6.refs_0_.refs_3_, ...), custom_call_target="tpu_custom_call" | custom-call | tf_op jit(solution)/shard_map/pallas_call | solution.py:381
  47.7 2.3 %shard_map.110 = (bf16[1,1792,512]{2,1,0:T(8,128)(2,1)}, bf16[1,1792,512]{2,1,0:T(8,128)(2,1)}) custom-call(bf16[48,896]{1,0:T(8,128)(2,1)S(1)} %get-tuple-element.28.refs_0_, bf16[48,896]{1,0:T(8,128)(2,1)S(1)} %collective-permute-done.refs_1_, bf16[96,896]{1,0:T(8,128)(2,1)S(1)} %collective-permute-done.1.refs_2_, ...), custom_call_target="tpu_custom_call" | custom-call | tf_op jit(solution)/shard_map/pallas_call | solution.py:371
  50.1 0.0 collective-permute-done.14.refs_2_
  50.1 0.0 collective-permute-done.16.refs_3_
  50.1 0.0 collective-permute-done.5.refs_1_
  50.1 1.2 %shard_map.109 = bf16[256,1792]{1,0:T(8,128)(2,1)} custom-call(bf16[24,896]{1,0:T(8,128)(2,1)S(1)} %get-tuple-element.53.refs_0_, bf16[24,896]{1,0:T(8,128)(2,1)S(1)} %collective-permute-done.5.refs_1_, bf16[24,896]{1,0:T(8,128)(2,1)S(1)} %collective-permute-done.14.refs_2_, bf16[24,896]{1,0:T(8,128)(2,1)S(1)} %collective-permute-done.16.refs_3_, ...), custom_call_target="tpu_custom_call" | custom-call | tf_op jit(solution)/shard_map/pallas_call | solution.py:391
  (9 shorter events, 0.2 us)
Async XLA Ops:
  0.6 15.3 %copy-start = (bf16[1,1792,512]{2,1,0:T(8,128)(2,1)S(1)}, bf16[1,1792,512]{2,1,0:T(8,128)(2,1)}, u32[]{:S(2)}) copy-start(bf16[1,1792,512]{2,1,0:T(8,128)(2,1)} %refs_3_.5) | copy-start | bytes 5505028
  2.6 10.4 %collective-permute-start.6 = (bf16[48,896]{1,0:T(8,128)(2,1)S(1)}, bf16[48,896]{1,0:T(8,128)(2,1)S(1)}, u32[]{:S(2)}, u32[]{:S(2)}) collective-permute-start(bf16[48,896]{1,0:T(8,128)(2,1)S(1)} %get-tuple-element.36), channel_id=1, source_target_pairs={{0,16},{4,20},{8,24},{12,28},{16,0},{20,4},{24,8},{28,12},{1,17},{... | collective-permute-start | bytes 258056 | tf_op jit(solution)/shard_map/ppermute | solution.py:275
  6.8 6.8 %collective-permute-start.7 = (bf16[48,896]{1,0:T(8,128)(2,1)S(1)}, bf16[48,896]{1,0:T(8,128)(2,1)S(1)}, u32[]{:S(2)}, u32[]{:S(2)}) collective-permute-start(bf16[48,896]{1,0:T(8,128)(2,1)S(1)} %get-tuple-element.37), channel_id=1, source_target_pairs={{0,24},{4,28},{8,16},{12,20},{16,8},{20,12},{24,0},{28,4},{1,25},{... | collective-permute-start | bytes 258056 | tf_op jit(solution)/shard_map/ppermute | solution.py:275
  8.1 7.3 %collective-permute-start = (bf16[48,896]{1,0:T(8,128)(2,1)S(1)}, bf16[48,896]{1,0:T(8,128)(2,1)S(1)}, u32[]{:S(2)}, u32[]{:S(2)}) collective-permute-start(bf16[48,896]{1,0:T(8,128)(2,1)S(1)} %get-tuple-element.29), channel_id=1, source_target_pairs={{0,8},{4,12},{8,0},{12,4},{16,24},{20,28},{24,16},{28,20},{1,9},{5... | collective-permute-start | bytes 258056 | tf_op jit(solution)/shard_map/ppermute | solution.py:275
  13.6 6.2 %collective-permute-start.8 = (bf16[96,896]{1,0:T(8,128)(2,1)S(1)}, bf16[96,896]{1,0:T(8,128)(2,1)S(1)}, u32[]{:S(2)}, u32[]{:S(2)}) collective-permute-start(bf16[96,896]{1,0:T(8,128)(2,1)S(1)} %pad_maximum_fusion.1), channel_id=1, source_target_pairs={{0,4},{4,0},{8,12},{12,8},{16,20},{20,16},{24,28},{28,24},{1,5},{5... | collective-permute-start | bytes 516104 | tf_op jit(solution)/shard_map/ppermute | solution.py:278
  15.4 6.2 %collective-permute-start.1 = (bf16[96,896]{1,0:T(8,128)(2,1)S(1)}, bf16[96,896]{1,0:T(8,128)(2,1)S(1)}, u32[]{:S(2)}, u32[]{:S(2)}) collective-permute-start(bf16[96,896]{1,0:T(8,128)(2,1)S(1)} %pad_maximum_fusion), channel_id=1, source_target_pairs={{0,4},{4,0},{8,12},{12,8},{16,20},{20,16},{24,28},{28,24},{1,5},{5... | collective-permute-start | bytes 516104 | tf_op jit(solution)/shard_map/ppermute | solution.py:278
  20.5 2.2 %collective-permute-start.9 = (bf16[96,512]{1,0:T(8,128)(2,1)S(1)}, bf16[96,512]{1,0:T(8,128)(2,1)S(1)}, u32[]{:S(2)}, u32[]{:S(2)}) collective-permute-start(bf16[96,512]{1,0:T(8,128)(2,1)S(1)} %shard_map.106), channel_id=1, source_target_pairs={{0,1},{1,0},{2,3},{3,2},{4,5},{5,4},{6,7},{7,6},{8,9},{9,8},{10,11... | collective-permute-start | bytes 294920 | tf_op jit(solution)/shard_map/ppermute | solution.py:284
  21.0 3.3 %collective-permute-start.11 = (bf16[48,512]{1,0:T(8,128)(2,1)S(1)}, bf16[48,512]{1,0:T(8,128)(2,1)S(1)}, u32[]{:S(2)}, u32[]{:S(2)}) collective-permute-start(bf16[48,512]{1,0:T(8,128)(2,1)S(1)} %shard_map.107), channel_id=1, source_target_pairs={{0,1},{1,0},{2,3},{3,2},{4,5},{5,4},{6,7},{7,6},{8,9},{9,8},{10,11... | collective-permute-start | bytes 147464 | tf_op jit(solution)/shard_map/ppermute | solution.py:284
  22.6 8.7 %collective-permute-start.2 = (bf16[144,512]{1,0:T(8,128)(2,1)S(1)}, bf16[144,512]{1,0:T(8,128)(2,1)S(1)}, u32[]{:S(2)}, u32[]{:S(2)}) collective-permute-start(bf16[144,512]{1,0:T(8,128)(2,1)S(1)} %shard_map.104), channel_id=1, source_target_pairs={{0,1},{1,0},{2,3},{3,2},{4,5},{5,4},{6,7},{7,6},{8,9},{9,8},{10,11... | collective-permute-start | bytes 442376 | tf_op jit(solution)/shard_map/ppermute | solution.py:284
  22.7 6.3 %collective-permute-start.10 = (bf16[96,512]{1,0:T(8,128)(2,1)S(1)}, bf16[96,512]{1,0:T(8,128)(2,1)S(1)}, u32[]{:S(2)}, u32[]{:S(2)}) collective-permute-start(bf16[96,512]{1,0:T(8,128)(2,1)S(1)} %add_convert_fusion.1.refs_0_), channel_id=1, source_target_pairs={{0,2},{1,3},{2,0},{3,1},{4,6},{5,7},{6,4},{7,5},{8,10},{9,11},{10,... | collective-permute-start | bytes 294920 | tf_op jit(solution)/shard_map/ppermute | solution.py:284
  24.3 4.7 %collective-permute-start.12 = (bf16[48,512]{1,0:T(8,128)(2,1)S(1)}, bf16[48,512]{1,0:T(8,128)(2,1)S(1)}, u32[]{:S(2)}, u32[]{:S(2)}) collective-permute-start(bf16[48,512]{1,0:T(8,128)(2,1)S(1)} %add_convert_fusion.3.refs_2_), channel_id=1, source_target_pairs={{0,2},{1,3},{2,0},{3,1},{4,6},{5,7},{6,4},{7,5},{8,10},{9,11},{10,... | collective-permute-start | bytes 147464 | tf_op jit(solution)/shard_map/ppermute | solution.py:284
  29.8 4.1 %collective-permute-start.13 = (bf16[24,896]{1,0:T(8,128)(2,1)S(1)}, bf16[24,896]{1,0:T(8,128)(2,1)S(1)}, u32[]{:S(2)}, u32[]{:S(2)}) collective-permute-start(bf16[24,896]{1,0:T(8,128)(2,1)S(1)} %get-tuple-element.39), channel_id=1, source_target_pairs={{0,4},{4,0},{8,12},{12,8},{16,20},{20,16},{24,28},{28,24},{1,5},{5... | collective-permute-start | bytes 129032 | tf_op jit(solution)/shard_map/ppermute | solution.py:278
  31.4 8.5 %collective-permute-start.3 = (bf16[144,512]{1,0:T(8,128)(2,1)S(1)}, bf16[144,512]{1,0:T(8,128)(2,1)S(1)}, u32[]{:S(2)}, u32[]{:S(2)}) collective-permute-start(bf16[144,512]{1,0:T(8,128)(2,1)S(1)} %add_convert_fusion.refs_0_), channel_id=1, source_target_pairs={{0,2},{1,3},{2,0},{3,1},{4,6},{5,7},{6,4},{7,5},{8,10},{9,11},{10,... | collective-permute-start | bytes 442376 | tf_op jit(solution)/shard_map/ppermute | solution.py:284
  33.0 9.4 %collective-permute-start.15 = (bf16[24,896]{1,0:T(8,128)(2,1)S(1)}, bf16[24,896]{1,0:T(8,128)(2,1)S(1)}, u32[]{:S(2)}, u32[]{:S(2)}) collective-permute-start(bf16[24,896]{1,0:T(8,128)(2,1)S(1)} %get-tuple-element.41), channel_id=1, source_target_pairs={{0,4},{4,0},{8,12},{12,8},{16,20},{20,16},{24,28},{28,24},{1,5},{5... | collective-permute-start | bytes 129032 | tf_op jit(solution)/shard_map/ppermute | solution.py:278
  33.9 16.2 %collective-permute-start.14 = (bf16[24,896]{1,0:T(8,128)(2,1)S(1)}, bf16[24,896]{1,0:T(8,128)(2,1)S(1)}, u32[]{:S(2)}, u32[]{:S(2)}) collective-permute-start(bf16[24,896]{1,0:T(8,128)(2,1)S(1)} %add_convert_fusion.5), channel_id=1, source_target_pairs={{0,16},{4,20},{8,24},{12,28},{16,0},{20,4},{24,8},{28,12},{1,17},{... | collective-permute-start | bytes 129032 | tf_op jit(solution)/shard_map/ppermute | solution.py:275
  40.6 4.5 %collective-permute-start.4 = (bf16[48,896]{1,0:T(8,128)(2,1)S(1)}, bf16[48,896]{1,0:T(8,128)(2,1)S(1)}, u32[]{:S(2)}, u32[]{:S(2)}) collective-permute-start(bf16[48,896]{1,0:T(8,128)(2,1)S(1)} %get-tuple-element.35), channel_id=1, source_target_pairs={{0,4},{4,0},{8,12},{12,8},{16,20},{20,16},{24,28},{28,24},{1,5},{5... | collective-permute-start | bytes 258056 | tf_op jit(solution)/shard_map/ppermute | solution.py:278
  42.4 7.7 %collective-permute-start.16 = (bf16[24,896]{1,0:T(8,128)(2,1)S(1)}, bf16[24,896]{1,0:T(8,128)(2,1)S(1)}, u32[]{:S(2)}, u32[]{:S(2)}) collective-permute-start(bf16[24,896]{1,0:T(8,128)(2,1)S(1)} %add_convert_fusion.4), channel_id=1, source_target_pairs={{0,24},{4,28},{8,16},{12,20},{16,8},{20,12},{24,0},{28,4},{1,25},{... | collective-permute-start | bytes 129032 | tf_op jit(solution)/shard_map/ppermute | solution.py:275
  45.2 4.9 %collective-permute-start.5 = (bf16[24,896]{1,0:T(8,128)(2,1)S(1)}, bf16[24,896]{1,0:T(8,128)(2,1)S(1)}, u32[]{:S(2)}, u32[]{:S(2)}) collective-permute-start(bf16[24,896]{1,0:T(8,128)(2,1)S(1)} %get-tuple-element.52), channel_id=1, source_target_pairs={{0,8},{4,12},{8,0},{12,4},{16,24},{20,28},{24,16},{28,20},{1,9},{5... | collective-permute-start | bytes 129032 | tf_op jit(solution)/shard_map/ppermute | solution.py:275

commit v4 on v3

--- a/solution.py
+++ b/solution.py
@@ -110,16 +110,15 @@
         messages[d][PAIR:] = message[d * PAIR : (d + 1) * PAIR].astype(BF16)
 
 
-def load_kernel(gate_ref, up_hbm, down_hbm, up_ref, gate_t, up_t, down_t, down_ref, sems):
-    up_copy = pltpu.make_async_copy(up_hbm, up_ref, sems.at[0])
-    down_copy = pltpu.make_async_copy(down_hbm, down_ref, sems.at[1])
-    up_copy.start()
-    down_copy.start()
-    gate_t[...] = gate_ref[0].T
-    up_copy.wait()
-    up_t[...] = up_ref[0].T
-    down_copy.wait()
-    down_t[...] = down_ref[0].T
+def load_kernel(*refs):
+    sources, held = refs[:3], refs[3:5] + refs[8:9]
+    turned, sems = refs[5:8], refs[9]
+    copies = [pltpu.make_async_copy(sources[i], held[i], sems.at[i]) for i in range(3)]
+    for copy in copies:
+        copy.start()
+    for copy, ref, out in zip(copies, held, turned):
+        copy.wait()
+        out[...] = ref[0].T
 
 
 def joined(refs):
@@ -248,8 +247,8 @@
     rows = joined(blocks).astype(BF16)
     copies = []
     tok = p0_ref.shape[1]
-    for k in range(2):
-        here = slice(k * tok // 2, (k + 1) * tok // 2)
+    for k in range(4):
+        here = slice(k * tok // 4, (k + 1) * tok // 4)
         for i, (p_ref, out) in enumerate(zip((p0_ref, p1_ref), columns(outs))):
             held[i, here] = dot(p_ref[:, here], rows, OVER_ROWS).astype(BF16)
             copies.append(
@@ -311,16 +310,16 @@
     )(first_expert, *(in_hbm(v) for v in (expert_ids.T, route_weight.T, *far)))
     p0, p1 = placed[window:]
     arrived = [placed[0]] + [across(placed[k], k) for k in range(1, window)]
-    up_w, gate_t, up_t, down_t = pl.pallas_call(
+    gate_w, up_w, gate_t, up_t, down_t = pl.pallas_call(
         load_kernel,
-        out_shape=(shape(up_weight.shape),)
+        out_shape=(shape(gate_weight.shape),) * 2
         + (shape((hidden, slab)),) * 2
         + (shape((slab, hidden)),),
-        in_specs=[space, hbm, hbm],
-        out_specs=(space,) * 4,
-        scratch_shapes=[pltpu.VMEM(down_weight.shape, BF16), pltpu.SemaphoreType.DMA((2,))],
+        in_specs=[hbm] * 3,
+        out_specs=(space,) * 5,
+        scratch_shapes=[pltpu.VMEM(down_weight.shape, BF16), pltpu.SemaphoreType.DMA((3,))],
         compiler_params=params,
-    )(gate_weight, in_hbm(up_weight), in_hbm(down_weight))
+    )(in_hbm(gate_weight), in_hbm(up_weight), in_hbm(down_weight))
 
     chunks = [range(window // 2), range(window // 2, window)]
     counts = tuple(len(chunk) for chunk in chunks)
@@ -334,14 +333,14 @@
             part = call(
                 functools.partial(product_kernel, count),
                 shape((3 * n, hidden)),
-                *take, gate_weight, up_w, down_t,
+                *take, gate_w, up_w, down_t,
             )
             sums.append(reduced(part))
             continue
         part = call(
             functools.partial(gate_up_kernel, count),
             shape((2 * n, hidden)),
-            *take, gate_weight, up_w,
+            *take, gate_w, up_w,
         )
         h_part = call(functools.partial(hidden_kernel, count), shape((n, hidden)), *take, down_t)
         sums.append(reduced(part) + reduced(h_part))
@@ -393,7 +392,7 @@
         out_shape=out_shape,
         in_specs=[space] * (len(home) + 2),
         out_specs=(hbm,) * len(out_shape),
-        scratch_shapes=[pltpu.VMEM((2, tok, w), BF16), pltpu.SemaphoreType.DMA((4,))],
+        scratch_shapes=[pltpu.VMEM((2, tok, w), BF16), pltpu.SemaphoreType.DMA((8,))],
         compiler_params=params,
     )(*home, p0, p1)
     token_grad = out[0] if aligned else jnp.concatenate(out, axis=1)

time: 51.5 us -> 51.4 us (level)
    pallas_call x1, Pallas kernels: 2.6 us -> 3.16 us  [body(): pl.pallas_call(load_kernel, out_shape=(shape(gate_weight.shape),) * 2 + (...]
    ppermute x5, waiting for transfers between devices: 3.76 us -> 3.21 us  [other_half(): return lax.ppermute(v, 'expert', [(e, e ^ 1) for e in range(expert_count)])]
  transfers between devices with their start and end apart: 17 -> 17, of which waited for: 7 -> 7; matrix products, arithmetic and copies ran while one was open for 0% -> 0% of each run, Pallas kernels for 20% -> 21%
where the time goes in v4:
time: 51.4 us; the launch traced here: 51.2 us
  starting transfers between devices  23.7 us (46%)
  Pallas kernels  13.9 us (27%)
  waiting for transfers between devices  12.6 us (25%)
  between operations  0.79 us (2%)
    ppermute x6, starting transfers between devices, across(): return lax.ppermute(v, 'expert', perm)  13.1 us
    ppermute x5, starting transfers between devices, other_half(): return lax.ppermute(v, 'expert', [(e, e ^ 1) for e in range(expert_count)])  6.2 us
    ppermute x6, waiting for transfers between devices, across(): return lax.ppermute(v, 'expert', perm)  5.24 us
    ppermute x6, starting transfers between devices, reduced(): got = lax.ppermute(part, 'fsdp', [(f, f ^ bit) for f in range(fsdp_count)])  4.45 us
    ppermute x6, waiting for transfers between devices, reduced(): got = lax.ppermute(part, 'fsdp', [(f, f ^ bit) for f in range(fsdp_count)])  4.14 us
    pallas_call x5, Pallas kernels, call(): pl.pallas_call(kernel, out_shape=outs, in_specs=[space] * len(args), out_...  3.66 us
    ppermute x5, waiting for transfers between devices, other_half(): return lax.ppermute(v, 'expert', [(e, e ^ 1) for e in range(expert_count)])  3.21 us
    pallas_call x1, Pallas kernels, body(): pl.pallas_call(load_kernel, out_shape=(shape(gate_weight.shape),) * 2 + (...  3.16 us
  transfers between devices with their start and end apart: 17, of which 7 were waited for; matrix products, arithmetic and copies ran while one was open for 0% of the time, Pallas kernels for 21%

profile of v4, /device:TPU:0, one launch (start us, length us, event | category | flops | bytes accessed | tf_op | source)
XLA Modules:
  0.0 51.2 jit_solution(6757184414210618660)
XLA Ops:
  0.6 1.9 %shard_map.102 = (bf16[48,896]{1,0:T(8,128)(2,1)S(1)}, bf16[48,896]{1,0:T(8,128)(2,1)S(1)}, bf16[48,896]{1,0:T(8,128)(2,1)S(1)}, bf16[48,896]{1,0:T(8,128)(2,1)S...) custom-call(s32[1]{0:T(128)} %bitcast.refs_0_, s32[8,256]{1,0:T(8,128)} %bitcast.3, f32[8,256]{1,0:T(8,128)} %bitcast.4, ...), custom_call_target="tpu_custom_call" | custom-call | tf_op jit(solution)/shard_map/pallas_call | solution.py:298
  2.5 4.1 %collective-permute-start.6 = (bf16[48,896]{1,0:T(8,128)(2,1)S(1)}, bf16[48,896]{1,0:T(8,128)(2,1)S(1)}, u32[]{:S(2)}, u32[]{:S(2)}) collective-permute-start(bf16[48,896]{1,0:T(8,128)(2,1)S(1)} %get-tuple-element.38), channel_id=1, source_target_pairs={{0,16},{4,20},{8,24},{12,28},{16,0},{20,4},{24,8},{28,12},{1,17},{... | collective-permute-start | bytes 258056 | tf_op jit(solution)/shard_map/ppermute | solution.py:274
  6.6 1.3 %collective-permute-start.7 = (bf16[48,896]{1,0:T(8,128)(2,1)S(1)}, bf16[48,896]{1,0:T(8,128)(2,1)S(1)}, u32[]{:S(2)}, u32[]{:S(2)}) collective-permute-start(bf16[48,896]{1,0:T(8,128)(2,1)S(1)} %get-tuple-element.39), channel_id=1, source_target_pairs={{0,24},{4,28},{8,16},{12,20},{16,8},{20,12},{24,0},{28,4},{1,25},{... | collective-permute-start | bytes 258056 | tf_op jit(solution)/shard_map/ppermute | solution.py:274
  8.0 0.2 collective-permute-start
  8.2 4.7 %collective-permute-done.6.refs_0_.refs_3_ = bf16[48,896]{1,0:T(8,128)(2,1)S(1)} collective-permute-done((bf16[48,896]{1,0:T(8,128)(2,1)S(1)}, bf16[48,896]{1,0:T(8,128)(2,1)S(1)}, u32[]{:S(2)}, u32[]{:S(2)}) %collective-permute-start.6) | collective-permute-done | bytes 86048 | tf_op jit(solution)/shard_map/ppermute | solution.py:274
  12.9 0.5 collective-permute-done.7.refs_1_.refs_4_
  13.5 1.8 %collective-permute-start.8 = (bf16[96,896]{1,0:T(8,128)(2,1)S(1)}, bf16[96,896]{1,0:T(8,128)(2,1)S(1)}, u32[]{:S(2)}, u32[]{:S(2)}) collective-permute-start(bf16[96,896]{1,0:T(8,128)(2,1)S(1)} %pad_maximum_fusion.1), channel_id=1, source_target_pairs={{0,4},{4,0},{8,12},{12,8},{16,20},{20,16},{24,28},{28,24},{1,5},{5... | collective-permute-start | bytes 516104 | tf_op jit(solution)/shard_map/ppermute | solution.py:277
  15.3 0.0 collective-permute-done.refs_1_
  15.3 0.5 %collective-permute-start.1 = (bf16[96,896]{1,0:T(8,128)(2,1)S(1)}, bf16[96,896]{1,0:T(8,128)(2,1)S(1)}, u32[]{:S(2)}, u32[]{:S(2)}) collective-permute-start(bf16[96,896]{1,0:T(8,128)(2,1)S(1)} %pad_maximum_fusion), channel_id=1, source_target_pairs={{0,4},{4,0},{8,12},{12,8},{16,20},{20,16},{24,28},{28,24},{1,5},{5... | collective-permute-start | bytes 516104 | tf_op jit(solution)/shard_map/ppermute | solution.py:277
  15.8 3.2 %shard_map.103 = (bf16[1,1792,512]{2,1,0:T(8,128)(2,1)S(1)}, bf16[1,1792,512]{2,1,0:T(8,128)(2,1)S(1)}, bf16[512,1792]{1,0:T(8,128)(2,1)S(1)}, bf16[512,1792]{1,0:T(8,128)(2,1)S(1)}, bf16[1792,512]{1,0:T(8,128)(2,1)S(1)}) custom-call(bf16[1,1792,512]{2,1,0:T(8,128)(2,1)} %refs_0_.1, bf16[1,1792,512]{2,1,0:T(8,128)(2,1)} %refs_1_.1, bf16[1,512,1792]{2,1,0:T(8,128)(2,1)} %refs_2_.1), custom_call_target="tpu_custom_call" | custom-call | tf_op jit(solution)/shard_map/pallas_call | solution.py:313
  19.0 0.6 %collective-permute-done.8.refs_2_.refs_5_ = bf16[96,896]{1,0:T(8,128)(2,1)S(1)} collective-permute-done((bf16[96,896]{1,0:T(8,128)(2,1)S(1)}, bf16[96,896]{1,0:T(8,128)(2,1)S(1)}, u32[]{:S(2)}, u32[]{:S(2)}) %collective-permute-start.8) | collective-permute-done | bytes 172064 | tf_op jit(solution)/shard_map/ppermute | solution.py:277
  19.6 0.7 %shard_map.106 = bf16[96,512]{1,0:T(8,128)(2,1)S(1)} custom-call(bf16[48,896]{1,0:T(8,128)(2,1)S(1)} %collective-permute-done.6.refs_0_.refs_3_, bf16[48,896]{1,0:T(8,128)(2,1)S(1)} %collective-permute-done.7.refs_1_.refs_4_, bf16[96,896]{1,0:T(8,128)(2,1)S(1)} %collective-permute-done.8.refs_2_.refs_5_, ...), custom_call_target="tpu_custom_call" | custom-call | tf_op jit(solution)/shard_map/pallas_call | solution.py:35
  20.3 0.1 collective-permute-start.9
  20.4 0.4 shard_map.107
  20.9 0.6 %collective-permute-start.11 = (bf16[48,512]{1,0:T(8,128)(2,1)S(1)}, bf16[48,512]{1,0:T(8,128)(2,1)S(1)}, u32[]{:S(2)}, u32[]{:S(2)}) collective-permute-start(bf16[48,512]{1,0:T(8,128)(2,1)S(1)} %shard_map.107), channel_id=1, source_target_pairs={{0,1},{1,0},{2,3},{3,2},{4,5},{5,4},{6,7},{7,6},{8,9},{9,8},{10,11... | collective-permute-start | bytes 147464 | tf_op jit(solution)/shard_map/ppermute | solution.py:283
  21.4 0.1 collective-permute-done.1.refs_2_
  21.5 1.0 %shard_map.104 = bf16[144,512]{1,0:T(8,128)(2,1)S(1)} custom-call(bf16[48,896]{1,0:T(8,128)(2,1)S(1)} %get-tuple-element.29.refs_0_, bf16[48,896]{1,0:T(8,128)(2,1)S(1)} %collective-permute-done.refs_1_, bf16[96,896]{1,0:T(8,128)(2,1)S(1)} %collective-permute-done.1.refs_2_, bf16[1,1792,512]{2,1,0:T(8,128)(2,1)S(1)} %get-tuple-element.31.refs_3_, ...), custom_call_target="tpu_custom_call" | custom-call | tf_op jit(solution)/shard_map/pallas_call | solution.py:35
  22.5 0.1 collective-permute-start.2
  22.5 0.0 collective-permute-done.9
  22.6 1.6 %collective-permute-start.10 = (bf16[96,512]{1,0:T(8,128)(2,1)S(1)}, bf16[96,512]{1,0:T(8,128)(2,1)S(1)}, u32[]{:S(2)}, u32[]{:S(2)}) collective-permute-start(bf16[96,512]{1,0:T(8,128)(2,1)S(1)} %add_convert_fusion.1.refs_0_), channel_id=1, source_target_pairs={{0,2},{1,3},{2,0},{3,1},{4,6},{5,7},{6,4},{7,5},{8,10},{9,11},{10,... | collective-permute-start | bytes 294920 | tf_op jit(solution)/shard_map/ppermute | solution.py:283
  24.2 0.0 collective-permute-done.11
  24.2 0.6 %collective-permute-start.12 = (bf16[48,512]{1,0:T(8,128)(2,1)S(1)}, bf16[48,512]{1,0:T(8,128)(2,1)S(1)}, u32[]{:S(2)}, u32[]{:S(2)}) collective-permute-start(bf16[48,512]{1,0:T(8,128)(2,1)S(1)} %add_convert_fusion.3.refs_2_), channel_id=1, source_target_pairs={{0,2},{1,3},{2,0},{3,1},{4,6},{5,7},{6,4},{7,5},{8,10},{9,11},{10,... | collective-permute-start | bytes 147464 | tf_op jit(solution)/shard_map/ppermute | solution.py:283
  24.8 4.1 %collective-permute-done.12.refs_3_ = bf16[48,512]{1,0:T(8,128)(2,1)S(1)} collective-permute-done((bf16[48,512]{1,0:T(8,128)(2,1)S(1)}, bf16[48,512]{1,0:T(8,128)(2,1)S(1)}, u32[]{:S(2)}, u32[]{:S(2)}) %collective-permute-start.12) | collective-permute-done | bytes 49184 | tf_op jit(solution)/shard_map/ppermute | solution.py:283
  28.9 0.0 collective-permute-done.10.refs_1_
  28.9 0.8 %shard_map.108 = (bf16[96,512]{1,0:T(8,128)(2,1)S(1)}, bf16[96,512]{1,0:T(8,128)(2,1)S(1)}, bf16[96,512]{1,0:T(8,128)(2,1)S(1)}, bf16[24,896]{1,0:T(8,128)(2,1)S...) custom-call(bf16[96,512]{1,0:T(8,128)(2,1)S(1)} %add_convert_fusion.1.refs_0_, ...), custom_call_target="tpu_custom_call" | custom-call | tf_op jit(solution)/shard_map/pallas_call | solution.py:35
  29.7 1.6 %collective-permute-start.13 = (bf16[24,896]{1,0:T(8,128)(2,1)S(1)}, bf16[24,896]{1,0:T(8,128)(2,1)S(1)}, u32[]{:S(2)}, u32[]{:S(2)}) collective-permute-start(bf16[24,896]{1,0:T(8,128)(2,1)S(1)} %get-tuple-element.41), channel_id=1, source_target_pairs={{0,4},{4,0},{8,12},{12,8},{16,20},{20,16},{24,28},{28,24},{1,5},{5... | collective-permute-start | bytes 129032 | tf_op jit(solution)/shard_map/ppermute | solution.py:277
  31.2 0.0 collective-permute-done.2
  31.3 1.6 %collective-permute-start.3 = (bf16[144,512]{1,0:T(8,128)(2,1)S(1)}, bf16[144,512]{1,0:T(8,128)(2,1)S(1)}, u32[]{:S(2)}, u32[]{:S(2)}) collective-permute-start(bf16[144,512]{1,0:T(8,128)(2,1)S(1)} %add_convert_fusion.refs_0_), channel_id=1, source_target_pairs={{0,2},{1,3},{2,0},{3,1},{4,6},{5,7},{6,4},{7,5},{8,10},{9,11},{10,... | collective-permute-start | bytes 442376 | tf_op jit(solution)/shard_map/ppermute | solution.py:283
  32.8 0.5 %collective-permute-start.15 = (bf16[24,896]{1,0:T(8,128)(2,1)S(1)}, bf16[24,896]{1,0:T(8,128)(2,1)S(1)}, u32[]{:S(2)}, u32[]{:S(2)}) collective-permute-start(bf16[24,896]{1,0:T(8,128)(2,1)S(1)} %get-tuple-element.43), channel_id=1, source_target_pairs={{0,4},{4,0},{8,12},{12,8},{16,20},{20,16},{24,28},{28,24},{1,5},{5... | collective-permute-start | bytes 129032 | tf_op jit(solution)/shard_map/ppermute | solution.py:277
  33.4 0.4 collective-permute-done.13
  33.8 6.0 %collective-permute-start.14 = (bf16[24,896]{1,0:T(8,128)(2,1)S(1)}, bf16[24,896]{1,0:T(8,128)(2,1)S(1)}, u32[]{:S(2)}, u32[]{:S(2)}) collective-permute-start(bf16[24,896]{1,0:T(8,128)(2,1)S(1)} %add_convert_fusion.5), channel_id=1, source_target_pairs={{0,16},{4,20},{8,24},{12,28},{16,0},{20,4},{24,8},{28,12},{1,17},{... | collective-permute-start | bytes 129032 | tf_op jit(solution)/shard_map/ppermute | solution.py:274
  39.7 0.0 collective-permute-done.3.refs_1_
  39.7 0.8 %shard_map.105 = (bf16[96,512]{1,0:T(8,128)(2,1)S(1)}, bf16[96,512]{1,0:T(8,128)(2,1)S(1)}, bf16[96,512]{1,0:T(8,128)(2,1)S(1)}, bf16[48,896]{1,0:T(8,128)(2,1)S(1)}, bf16[48,896]{1,0:T(8,128)(2,1)S(1)}) custom-call(bf16[144,512]{1,0:T(8,128)(2,1)S(1)} %add_convert_fusion.refs_0_, bf16[144,512]{1,0:T(8,128)(2,1)S(1)} %collective-permute-done.3.refs_1_, ...), custom_call_target="tpu_custom_call" | custom-call | tf_op jit(solution)/shard_map/pallas_call | solution.py:35
  40.5 1.7 %collective-permute-start.4 = (bf16[48,896]{1,0:T(8,128)(2,1)S(1)}, bf16[48,896]{1,0:T(8,128)(2,1)S(1)}, u32[]{:S(2)}, u32[]{:S(2)}) collective-permute-start(bf16[48,896]{1,0:T(8,128)(2,1)S(1)} %get-tuple-element.37), channel_id=1, source_target_pairs={{0,4},{4,0},{8,12},{12,8},{16,20},{20,16},{24,28},{28,24},{1,5},{5... | collective-permute-start | bytes 258056 | tf_op jit(solution)/shard_map/ppermute | solution.py:277
  42.2 0.0 collective-permute-done.15
  42.3 0.6 %collective-permute-start.16 = (bf16[24,896]{1,0:T(8,128)(2,1)S(1)}, bf16[24,896]{1,0:T(8,128)(2,1)S(1)}, u32[]{:S(2)}, u32[]{:S(2)}) collective-permute-start(bf16[24,896]{1,0:T(8,128)(2,1)S(1)} %add_convert_fusion.4), channel_id=1, source_target_pairs={{0,24},{4,28},{8,16},{12,20},{16,8},{20,12},{24,0},{28,4},{1,25},{... | collective-permute-start | bytes 129032 | tf_op jit(solution)/shard_map/ppermute | solution.py:274
  42.9 2.2 %collective-permute-done.4 = bf16[48,896]{1,0:T(8,128)(2,1)S(1)} collective-permute-done((bf16[48,896]{1,0:T(8,128)(2,1)S(1)}, bf16[48,896]{1,0:T(8,128)(2,1)S(1)}, u32[]{:S(2)}, u32[]{:S(2)}) %collective-permute-start.4) | collective-permute-done | bytes 86048 | tf_op jit(solution)/shard_map/ppermute | solution.py:277
  45.1 0.8 %collective-permute-start.5 = (bf16[24,896]{1,0:T(8,128)(2,1)S(1)}, bf16[24,896]{1,0:T(8,128)(2,1)S(1)}, u32[]{:S(2)}, u32[]{:S(2)}) collective-permute-start(bf16[24,896]{1,0:T(8,128)(2,1)S(1)} %get-tuple-element.54), channel_id=1, source_target_pairs={{0,8},{4,12},{8,0},{12,4},{16,24},{20,28},{24,16},{28,20},{1,9},{5... | collective-permute-start | bytes 129032 | tf_op jit(solution)/shard_map/ppermute | solution.py:274
  45.9 1.7 %shard_map.111 = bf16[1,512,1792]{2,1,0:T(8,128)(2,1)} custom-call(bf16[48,896]{1,0:T(8,128)(2,1)S(1)} %get-tuple-element.29.refs_0_, bf16[48,896]{1,0:T(8,128)(2,1)S(1)} %collective-permute-done.refs_1_, bf16[96,896]{1,0:T(8,128)(2,1)S(1)} %collective-permute-done.1.refs_2_, bf16[48,896]{1,0:T(8,128)(2,1)S(1)} %collective-permute-done.6.refs_0_.refs_3_, ...), custom_call_target="tpu_custom_call" | custom-call | tf_op jit(solution)/shard_map/pallas_call | solution.py:380
  47.6 2.3 %shard_map.110 = (bf16[1,1792,512]{2,1,0:T(8,128)(2,1)}, bf16[1,1792,512]{2,1,0:T(8,128)(2,1)}) custom-call(bf16[48,896]{1,0:T(8,128)(2,1)S(1)} %get-tuple-element.29.refs_0_, bf16[48,896]{1,0:T(8,128)(2,1)S(1)} %collective-permute-done.refs_1_, bf16[96,896]{1,0:T(8,128)(2,1)S(1)} %collective-permute-done.1.refs_2_, ...), custom_call_target="tpu_custom_call" | custom-call | tf_op jit(solution)/shard_map/pallas_call | solution.py:370
  49.9 0.0 collective-permute-done.14.refs_2_
  49.9 0.0 collective-permute-done.16.refs_3_
  50.0 0.0 collective-permute-done.5.refs_1_
  50.0 1.2 %shard_map.109 = bf16[256,1792]{1,0:T(8,128)(2,1)} custom-call(bf16[24,896]{1,0:T(8,128)(2,1)S(1)} %get-tuple-element.55.refs_0_, bf16[24,896]{1,0:T(8,128)(2,1)S(1)} %collective-permute-done.5.refs_1_, bf16[24,896]{1,0:T(8,128)(2,1)S(1)} %collective-permute-done.14.refs_2_, bf16[24,896]{1,0:T(8,128)(2,1)S(1)} %collective-permute-done.16.refs_3_, ...), custom_call_target="tpu_custom_call" | custom-call | tf_op jit(solution)/shard_map/pallas_call | solution.py:390
  (9 shorter events, 0.2 us)
Async XLA Ops:
  2.5 10.4 %collective-permute-start.6 = (bf16[48,896]{1,0:T(8,128)(2,1)S(1)}, bf16[48,896]{1,0:T(8,128)(2,1)S(1)}, u32[]{:S(2)}, u32[]{:S(2)}) collective-permute-start(bf16[48,896]{1,0:T(8,128)(2,1)S(1)} %get-tuple-element.38), channel_id=1, source_target_pairs={{0,16},{4,20},{8,24},{12,28},{16,0},{20,4},{24,8},{28,12},{1,17},{... | collective-permute-start | bytes 258056 | tf_op jit(solution)/shard_map/ppermute | solution.py:274
  6.6 6.8 %collective-permute-start.7 = (bf16[48,896]{1,0:T(8,128)(2,1)S(1)}, bf16[48,896]{1,0:T(8,128)(2,1)S(1)}, u32[]{:S(2)}, u32[]{:S(2)}) collective-permute-start(bf16[48,896]{1,0:T(8,128)(2,1)S(1)} %get-tuple-element.39), channel_id=1, source_target_pairs={{0,24},{4,28},{8,16},{12,20},{16,8},{20,12},{24,0},{28,4},{1,25},{... | collective-permute-start | bytes 258056 | tf_op jit(solution)/shard_map/ppermute | solution.py:274
  8.0 7.3 %collective-permute-start = (bf16[48,896]{1,0:T(8,128)(2,1)S(1)}, bf16[48,896]{1,0:T(8,128)(2,1)S(1)}, u32[]{:S(2)}, u32[]{:S(2)}) collective-permute-start(bf16[48,896]{1,0:T(8,128)(2,1)S(1)} %get-tuple-element.30), channel_id=1, source_target_pairs={{0,8},{4,12},{8,0},{12,4},{16,24},{20,28},{24,16},{28,20},{1,9},{5... | collective-permute-start | bytes 258056 | tf_op jit(solution)/shard_map/ppermute | solution.py:274
  13.5 6.2 %collective-permute-start.8 = (bf16[96,896]{1,0:T(8,128)(2,1)S(1)}, bf16[96,896]{1,0:T(8,128)(2,1)S(1)}, u32[]{:S(2)}, u32[]{:S(2)}) collective-permute-start(bf16[96,896]{1,0:T(8,128)(2,1)S(1)} %pad_maximum_fusion.1), channel_id=1, source_target_pairs={{0,4},{4,0},{8,12},{12,8},{16,20},{20,16},{24,28},{28,24},{1,5},{5... | collective-permute-start | bytes 516104 | tf_op jit(solution)/shard_map/ppermute | solution.py:277
  15.3 6.2 %collective-permute-start.1 = (bf16[96,896]{1,0:T(8,128)(2,1)S(1)}, bf16[96,896]{1,0:T(8,128)(2,1)S(1)}, u32[]{:S(2)}, u32[]{:S(2)}) collective-permute-start(bf16[96,896]{1,0:T(8,128)(2,1)S(1)} %pad_maximum_fusion), channel_id=1, source_target_pairs={{0,4},{4,0},{8,12},{12,8},{16,20},{20,16},{24,28},{28,24},{1,5},{5... | collective-permute-start | bytes 516104 | tf_op jit(solution)/shard_map/ppermute | solution.py:277
  20.3 2.2 %collective-permute-start.9 = (bf16[96,512]{1,0:T(8,128)(2,1)S(1)}, bf16[96,512]{1,0:T(8,128)(2,1)S(1)}, u32[]{:S(2)}, u32[]{:S(2)}) collective-permute-start(bf16[96,512]{1,0:T(8,128)(2,1)S(1)} %shard_map.106), channel_id=1, source_target_pairs={{0,1},{1,0},{2,3},{3,2},{4,5},{5,4},{6,7},{7,6},{8,9},{9,8},{10,11... | collective-permute-start | bytes 294920 | tf_op jit(solution)/shard_map/ppermute | solution.py:283
  20.9 3.3 %collective-permute-start.11 = (bf16[48,512]{1,0:T(8,128)(2,1)S(1)}, bf16[48,512]{1,0:T(8,128)(2,1)S(1)}, u32[]{:S(2)}, u32[]{:S(2)}) collective-permute-start(bf16[48,512]{1,0:T(8,128)(2,1)S(1)} %shard_map.107), channel_id=1, source_target_pairs={{0,1},{1,0},{2,3},{3,2},{4,5},{5,4},{6,7},{7,6},{8,9},{9,8},{10,11... | collective-permute-start | bytes 147464 | tf_op jit(solution)/shard_map/ppermute | solution.py:283
  22.5 8.7 %collective-permute-start.2 = (bf16[144,512]{1,0:T(8,128)(2,1)S(1)}, bf16[144,512]{1,0:T(8,128)(2,1)S(1)}, u32[]{:S(2)}, u32[]{:S(2)}) collective-permute-start(bf16[144,512]{1,0:T(8,128)(2,1)S(1)} %shard_map.104), channel_id=1, source_target_pairs={{0,1},{1,0},{2,3},{3,2},{4,5},{5,4},{6,7},{7,6},{8,9},{9,8},{10,11... | collective-permute-start | bytes 442376 | tf_op jit(solution)/shard_map/ppermute | solution.py:283
  22.6 6.3 %collective-permute-start.10 = (bf16[96,512]{1,0:T(8,128)(2,1)S(1)}, bf16[96,512]{1,0:T(8,128)(2,1)S(1)}, u32[]{:S(2)}, u32[]{:S(2)}) collective-permute-start(bf16[96,512]{1,0:T(8,128)(2,1)S(1)} %add_convert_fusion.1.refs_0_), channel_id=1, source_target_pairs={{0,2},{1,3},{2,0},{3,1},{4,6},{5,7},{6,4},{7,5},{8,10},{9,11},{10,... | collective-permute-start | bytes 294920 | tf_op jit(solution)/shard_map/ppermute | solution.py:283
  24.2 4.7 %collective-permute-start.12 = (bf16[48,512]{1,0:T(8,128)(2,1)S(1)}, bf16[48,512]{1,0:T(8,128)(2,1)S(1)}, u32[]{:S(2)}, u32[]{:S(2)}) collective-permute-start(bf16[48,512]{1,0:T(8,128)(2,1)S(1)} %add_convert_fusion.3.refs_2_), channel_id=1, source_target_pairs={{0,2},{1,3},{2,0},{3,1},{4,6},{5,7},{6,4},{7,5},{8,10},{9,11},{10,... | collective-permute-start | bytes 147464 | tf_op jit(solution)/shard_map/ppermute | solution.py:283
  29.7 4.1 %collective-permute-start.13 = (bf16[24,896]{1,0:T(8,128)(2,1)S(1)}, bf16[24,896]{1,0:T(8,128)(2,1)S(1)}, u32[]{:S(2)}, u32[]{:S(2)}) collective-permute-start(bf16[24,896]{1,0:T(8,128)(2,1)S(1)} %get-tuple-element.41), channel_id=1, source_target_pairs={{0,4},{4,0},{8,12},{12,8},{16,20},{20,16},{24,28},{28,24},{1,5},{5... | collective-permute-start | bytes 129032 | tf_op jit(solution)/shard_map/ppermute | solution.py:277
  31.3 8.5 %collective-permute-start.3 = (bf16[144,512]{1,0:T(8,128)(2,1)S(1)}, bf16[144,512]{1,0:T(8,128)(2,1)S(1)}, u32[]{:S(2)}, u32[]{:S(2)}) collective-permute-start(bf16[144,512]{1,0:T(8,128)(2,1)S(1)} %add_convert_fusion.refs_0_), channel_id=1, source_target_pairs={{0,2},{1,3},{2,0},{3,1},{4,6},{5,7},{6,4},{7,5},{8,10},{9,11},{10,... | collective-permute-start | bytes 442376 | tf_op jit(solution)/shard_map/ppermute | solution.py:283
  32.8 9.4 %collective-permute-start.15 = (bf16[24,896]{1,0:T(8,128)(2,1)S(1)}, bf16[24,896]{1,0:T(8,128)(2,1)S(1)}, u32[]{:S(2)}, u32[]{:S(2)}) collective-permute-start(bf16[24,896]{1,0:T(8,128)(2,1)S(1)} %get-tuple-element.43), channel_id=1, source_target_pairs={{0,4},{4,0},{8,12},{12,8},{16,20},{20,16},{24,28},{28,24},{1,5},{5... | collective-permute-start | bytes 129032 | tf_op jit(solution)/shard_map/ppermute | solution.py:277
  33.8 16.2 %collective-permute-start.14 = (bf16[24,896]{1,0:T(8,128)(2,1)S(1)}, bf16[24,896]{1,0:T(8,128)(2,1)S(1)}, u32[]{:S(2)}, u32[]{:S(2)}) collective-permute-start(bf16[24,896]{1,0:T(8,128)(2,1)S(1)} %add_convert_fusion.5), channel_id=1, source_target_pairs={{0,16},{4,20},{8,24},{12,28},{16,0},{20,4},{24,8},{28,12},{1,17},{... | collective-permute-start | bytes 129032 | tf_op jit(solution)/shard_map/ppermute | solution.py:274
  40.5 4.6 %collective-permute-start.4 = (bf16[48,896]{1,0:T(8,128)(2,1)S(1)}, bf16[48,896]{1,0:T(8,128)(2,1)S(1)}, u32[]{:S(2)}, u32[]{:S(2)}) collective-permute-start(bf16[48,896]{1,0:T(8,128)(2,1)S(1)} %get-tuple-element.37), channel_id=1, source_target_pairs={{0,4},{4,0},{8,12},{12,8},{16,20},{20,16},{24,28},{28,24},{1,5},{5... | collective-permute-start | bytes 258056 | tf_op jit(solution)/shard_map/ppermute | solution.py:277
  42.3 7.7 %collective-permute-start.16 = (bf16[24,896]{1,0:T(8,128)(2,1)S(1)}, bf16[24,896]{1,0:T(8,128)(2,1)S(1)}, u32[]{:S(2)}, u32[]{:S(2)}) collective-permute-start(bf16[24,896]{1,0:T(8,128)(2,1)S(1)} %add_convert_fusion.4), channel_id=1, source_target_pairs={{0,24},{4,28},{8,16},{12,20},{16,8},{20,12},{24,0},{28,4},{1,25},{... | collective-permute-start | bytes 129032 | tf_op jit(solution)/shard_map/ppermute | solution.py:274
  45.1 4.9 %collective-permute-start.5 = (bf16[24,896]{1,0:T(8,128)(2,1)S(1)}, bf16[24,896]{1,0:T(8,128)(2,1)S(1)}, u32[]{:S(2)}, u32[]{:S(2)}) collective-permute-start(bf16[24,896]{1,0:T(8,128)(2,1)S(1)} %get-tuple-element.54), channel_id=1, source_target_pairs={{0,8},{4,12},{8,0},{12,4},{16,24},{20,28},{24,16},{28,20},{1,9},{5... | collective-permute-start | bytes 129032 | tf_op jit(solution)/shard_map/ppermute | solution.py:274

commit v5 on v4

--- a/solution.py
+++ b/solution.py
@@ -97,15 +97,16 @@
     p0, p1 = p0.astype(BF16), p1.astype(BF16)
     p0_ref[...] = p0
     p1_ref[...] = p1
-    both = jnp.concatenate([p0, p1], axis=1)
     copies[2].wait()
+    message = dot(p0, held[0, :tok])
     copies[3].wait()
-    message = dot(both, held[0])
+    message = message + dot(p1, held[0, tok:])
     for d in range(window):
         messages[d][:PAIR] = message[d * PAIR : (d + 1) * PAIR].astype(BF16)
     copies[4].wait()
+    message = dot(p0, held[1, :tok])
     copies[5].wait()
-    message = dot(both, held[1]) * scale
+    message = (message + dot(p1, held[1, tok:])) * scale
     for d in range(window):
         messages[d][PAIR:] = message[d * PAIR : (d + 1) * PAIR].astype(BF16)
 

time: 51.4 us -> 51.4 us (level)
  no operation moved by 1% of the time
where the time goes in v5:
time: 51.4 us; the launch traced here: 51.2 us
  starting transfers between devices  23.7 us (46%)
  Pallas kernels  13.9 us (27%)
  waiting for transfers between devices  12.6 us (25%)
  between operations  0.79 us (2%)
    ppermute x6, starting transfers between devices, across(): return lax.ppermute(v, 'expert', perm)  13.1 us
    ppermute x5, starting transfers between devices, other_half(): return lax.ppermute(v, 'expert', [(e, e ^ 1) for e in range(expert_count)])  6.18 us
    ppermute x6, waiting for transfers between devices, across(): return lax.ppermute(v, 'expert', perm)  5.24 us
    ppermute x6, starting transfers between devices, reduced(): got = lax.ppermute(part, 'fsdp', [(f, f ^ bit) for f in range(fsdp_count)])  4.45 us
    ppermute x6, waiting for transfers between devices, reduced(): got = lax.ppermute(part, 'fsdp', [(f, f ^ bit) for f in range(fsdp_count)])  4.14 us
    pallas_call x5, Pallas kernels, call(): pl.pallas_call(kernel, out_shape=outs, in_specs=[space] * len(args), out_...  3.66 us
    ppermute x5, waiting for transfers between devices, other_half(): return lax.ppermute(v, 'expert', [(e, e ^ 1) for e in range(expert_count)])  3.22 us
    pallas_call x1, Pallas kernels, body(): pl.pallas_call(load_kernel, out_shape=(shape(gate_weight.shape),) * 2 + (...  3.16 us
  transfers between devices with their start and end apart: 17, of which 7 were waited for; matrix products, arithmetic and copies ran while one was open for 0% of the time, Pallas kernels for 21%

profile of v5, /device:TPU:0, one launch (start us, length us, event | category | flops | bytes accessed | tf_op | source)
XLA Modules:
  0.0 51.2 jit_solution(6437424067461925938)
XLA Ops:
  0.6 1.9 %shard_map.102 = (bf16[48,896]{1,0:T(8,128)(2,1)S(1)}, bf16[48,896]{1,0:T(8,128)(2,1)S(1)}, bf16[48,896]{1,0:T(8,128)(2,1)S(1)}, bf16[48,896]{1,0:T(8,128)(2,1)S...) custom-call(s32[1]{0:T(128)} %bitcast.refs_0_, s32[8,256]{1,0:T(8,128)} %bitcast.3, f32[8,256]{1,0:T(8,128)} %bitcast.4, ...), custom_call_target="tpu_custom_call" | custom-call | tf_op jit(solution)/shard_map/pallas_call | solution.py:299
  2.5 4.1 %collective-permute-start.6 = (bf16[48,896]{1,0:T(8,128)(2,1)S(1)}, bf16[48,896]{1,0:T(8,128)(2,1)S(1)}, u32[]{:S(2)}, u32[]{:S(2)}) collective-permute-start(bf16[48,896]{1,0:T(8,128)(2,1)S(1)} %get-tuple-element.38), channel_id=1, source_target_pairs={{0,16},{4,20},{8,24},{12,28},{16,0},{20,4},{24,8},{28,12},{1,17},{... | collective-permute-start | bytes 258056 | tf_op jit(solution)/shard_map/ppermute | solution.py:275
  6.7 1.3 %collective-permute-start.7 = (bf16[48,896]{1,0:T(8,128)(2,1)S(1)}, bf16[48,896]{1,0:T(8,128)(2,1)S(1)}, u32[]{:S(2)}, u32[]{:S(2)}) collective-permute-start(bf16[48,896]{1,0:T(8,128)(2,1)S(1)} %get-tuple-element.39), channel_id=1, source_target_pairs={{0,24},{4,28},{8,16},{12,20},{16,8},{20,12},{24,0},{28,4},{1,25},{... | collective-permute-start | bytes 258056 | tf_op jit(solution)/shard_map/ppermute | solution.py:275
  8.0 0.2 collective-permute-start
  8.2 4.7 %collective-permute-done.6.refs_0_.refs_3_ = bf16[48,896]{1,0:T(8,128)(2,1)S(1)} collective-permute-done((bf16[48,896]{1,0:T(8,128)(2,1)S(1)}, bf16[48,896]{1,0:T(8,128)(2,1)S(1)}, u32[]{:S(2)}, u32[]{:S(2)}) %collective-permute-start.6) | collective-permute-done | bytes 86048 | tf_op jit(solution)/shard_map/ppermute | solution.py:275
  13.0 0.5 collective-permute-done.7.refs_1_.refs_4_
  13.5 1.8 %collective-permute-start.8 = (bf16[96,896]{1,0:T(8,128)(2,1)S(1)}, bf16[96,896]{1,0:T(8,128)(2,1)S(1)}, u32[]{:S(2)}, u32[]{:S(2)}) collective-permute-start(bf16[96,896]{1,0:T(8,128)(2,1)S(1)} %pad_maximum_fusion.1), channel_id=1, source_target_pairs={{0,4},{4,0},{8,12},{12,8},{16,20},{20,16},{24,28},{28,24},{1,5},{5... | collective-permute-start | bytes 516104 | tf_op jit(solution)/shard_map/ppermute | solution.py:278
  15.3 0.0 collective-permute-done.refs_1_
  15.3 0.5 %collective-permute-start.1 = (bf16[96,896]{1,0:T(8,128)(2,1)S(1)}, bf16[96,896]{1,0:T(8,128)(2,1)S(1)}, u32[]{:S(2)}, u32[]{:S(2)}) collective-permute-start(bf16[96,896]{1,0:T(8,128)(2,1)S(1)} %pad_maximum_fusion), channel_id=1, source_target_pairs={{0,4},{4,0},{8,12},{12,8},{16,20},{20,16},{24,28},{28,24},{1,5},{5... | collective-permute-start | bytes 516104 | tf_op jit(solution)/shard_map/ppermute | solution.py:278
  15.9 3.2 %shard_map.103 = (bf16[1,1792,512]{2,1,0:T(8,128)(2,1)S(1)}, bf16[1,1792,512]{2,1,0:T(8,128)(2,1)S(1)}, bf16[512,1792]{1,0:T(8,128)(2,1)S(1)}, bf16[512,1792]{1,0:T(8,128)(2,1)S(1)}, bf16[1792,512]{1,0:T(8,128)(2,1)S(1)}) custom-call(bf16[1,1792,512]{2,1,0:T(8,128)(2,1)} %refs_0_.1, bf16[1,1792,512]{2,1,0:T(8,128)(2,1)} %refs_1_.1, bf16[1,512,1792]{2,1,0:T(8,128)(2,1)} %refs_2_.1), custom_call_target="tpu_custom_call" | custom-call | tf_op jit(solution)/shard_map/pallas_call | solution.py:314
  19.0 0.6 %collective-permute-done.8.refs_2_.refs_5_ = bf16[96,896]{1,0:T(8,128)(2,1)S(1)} collective-permute-done((bf16[96,896]{1,0:T(8,128)(2,1)S(1)}, bf16[96,896]{1,0:T(8,128)(2,1)S(1)}, u32[]{:S(2)}, u32[]{:S(2)}) %collective-permute-start.8) | collective-permute-done | bytes 172064 | tf_op jit(solution)/shard_map/ppermute | solution.py:278
  19.7 0.7 %shard_map.106 = bf16[96,512]{1,0:T(8,128)(2,1)S(1)} custom-call(bf16[48,896]{1,0:T(8,128)(2,1)S(1)} %collective-permute-done.6.refs_0_.refs_3_, bf16[48,896]{1,0:T(8,128)(2,1)S(1)} %collective-permute-done.7.refs_1_.refs_4_, bf16[96,896]{1,0:T(8,128)(2,1)S(1)} %collective-permute-done.8.refs_2_.refs_5_, ...), custom_call_target="tpu_custom_call" | custom-call | tf_op jit(solution)/shard_map/pallas_call | solution.py:35
  20.4 0.1 collective-permute-start.9
  20.5 0.4 shard_map.107
  20.9 0.6 %collective-permute-start.11 = (bf16[48,512]{1,0:T(8,128)(2,1)S(1)}, bf16[48,512]{1,0:T(8,128)(2,1)S(1)}, u32[]{:S(2)}, u32[]{:S(2)}) collective-permute-start(bf16[48,512]{1,0:T(8,128)(2,1)S(1)} %shard_map.107), channel_id=1, source_target_pairs={{0,1},{1,0},{2,3},{3,2},{4,5},{5,4},{6,7},{7,6},{8,9},{9,8},{10,11... | collective-permute-start | bytes 147464 | tf_op jit(solution)/shard_map/ppermute | solution.py:284
  21.4 0.1 collective-permute-done.1.refs_2_
  21.5 1.0 %shard_map.104 = bf16[144,512]{1,0:T(8,128)(2,1)S(1)} custom-call(bf16[48,896]{1,0:T(8,128)(2,1)S(1)} %get-tuple-element.29.refs_0_, bf16[48,896]{1,0:T(8,128)(2,1)S(1)} %collective-permute-done.refs_1_, bf16[96,896]{1,0:T(8,128)(2,1)S(1)} %collective-permute-done.1.refs_2_, bf16[1,1792,512]{2,1,0:T(8,128)(2,1)S(1)} %get-tuple-element.31.refs_3_, ...), custom_call_target="tpu_custom_call" | custom-call | tf_op jit(solution)/shard_map/pallas_call | solution.py:35
  22.5 0.1 collective-permute-start.2
  22.6 0.0 collective-permute-done.9
  22.6 1.6 %collective-permute-start.10 = (bf16[96,512]{1,0:T(8,128)(2,1)S(1)}, bf16[96,512]{1,0:T(8,128)(2,1)S(1)}, u32[]{:S(2)}, u32[]{:S(2)}) collective-permute-start(bf16[96,512]{1,0:T(8,128)(2,1)S(1)} %add_convert_fusion.1.refs_0_), channel_id=1, source_target_pairs={{0,2},{1,3},{2,0},{3,1},{4,6},{5,7},{6,4},{7,5},{8,10},{9,11},{10,... | collective-permute-start | bytes 294920 | tf_op jit(solution)/shard_map/ppermute | solution.py:284
  24.2 0.0 collective-permute-done.11
  24.2 0.6 %collective-permute-start.12 = (bf16[48,512]{1,0:T(8,128)(2,1)S(1)}, bf16[48,512]{1,0:T(8,128)(2,1)S(1)}, u32[]{:S(2)}, u32[]{:S(2)}) collective-permute-start(bf16[48,512]{1,0:T(8,128)(2,1)S(1)} %add_convert_fusion.3.refs_2_), channel_id=1, source_target_pairs={{0,2},{1,3},{2,0},{3,1},{4,6},{5,7},{6,4},{7,5},{8,10},{9,11},{10,... | collective-permute-start | bytes 147464 | tf_op jit(solution)/shard_map/ppermute | solution.py:284
  24.8 4.1 %collective-permute-done.12.refs_3_ = bf16[48,512]{1,0:T(8,128)(2,1)S(1)} collective-permute-done((bf16[48,512]{1,0:T(8,128)(2,1)S(1)}, bf16[48,512]{1,0:T(8,128)(2,1)S(1)}, u32[]{:S(2)}, u32[]{:S(2)}) %collective-permute-start.12) | collective-permute-done | bytes 49184 | tf_op jit(solution)/shard_map/ppermute | solution.py:284
  28.9 0.0 collective-permute-done.10.refs_1_
  28.9 0.8 %shard_map.108 = (bf16[96,512]{1,0:T(8,128)(2,1)S(1)}, bf16[96,512]{1,0:T(8,128)(2,1)S(1)}, bf16[96,512]{1,0:T(8,128)(2,1)S(1)}, bf16[24,896]{1,0:T(8,128)(2,1)S...) custom-call(bf16[96,512]{1,0:T(8,128)(2,1)S(1)} %add_convert_fusion.1.refs_0_, ...), custom_call_target="tpu_custom_call" | custom-call | tf_op jit(solution)/shard_map/pallas_call | solution.py:35
  29.7 1.6 %collective-permute-start.13 = (bf16[24,896]{1,0:T(8,128)(2,1)S(1)}, bf16[24,896]{1,0:T(8,128)(2,1)S(1)}, u32[]{:S(2)}, u32[]{:S(2)}) collective-permute-start(bf16[24,896]{1,0:T(8,128)(2,1)S(1)} %get-tuple-element.41), channel_id=1, source_target_pairs={{0,4},{4,0},{8,12},{12,8},{16,20},{20,16},{24,28},{28,24},{1,5},{5... | collective-permute-start | bytes 129032 | tf_op jit(solution)/shard_map/ppermute | solution.py:278
  31.2 0.0 collective-permute-done.2
  31.3 1.6 %collective-permute-start.3 = (bf16[144,512]{1,0:T(8,128)(2,1)S(1)}, bf16[144,512]{1,0:T(8,128)(2,1)S(1)}, u32[]{:S(2)}, u32[]{:S(2)}) collective-permute-start(bf16[144,512]{1,0:T(8,128)(2,1)S(1)} %add_convert_fusion.refs_0_), channel_id=1, source_target_pairs={{0,2},{1,3},{2,0},{3,1},{4,6},{5,7},{6,4},{7,5},{8,10},{9,11},{10,... | collective-permute-start | bytes 442376 | tf_op jit(solution)/shard_map/ppermute | solution.py:284
  32.9 0.5 %collective-permute-start.15 = (bf16[24,896]{1,0:T(8,128)(2,1)S(1)}, bf16[24,896]{1,0:T(8,128)(2,1)S(1)}, u32[]{:S(2)}, u32[]{:S(2)}) collective-permute-start(bf16[24,896]{1,0:T(8,128)(2,1)S(1)} %get-tuple-element.43), channel_id=1, source_target_pairs={{0,4},{4,0},{8,12},{12,8},{16,20},{20,16},{24,28},{28,24},{1,5},{5... | collective-permute-start | bytes 129032 | tf_op jit(solution)/shard_map/ppermute | solution.py:278
  33.4 0.4 collective-permute-done.13
  33.8 6.0 %collective-permute-start.14 = (bf16[24,896]{1,0:T(8,128)(2,1)S(1)}, bf16[24,896]{1,0:T(8,128)(2,1)S(1)}, u32[]{:S(2)}, u32[]{:S(2)}) collective-permute-start(bf16[24,896]{1,0:T(8,128)(2,1)S(1)} %add_convert_fusion.5), channel_id=1, source_target_pairs={{0,16},{4,20},{8,24},{12,28},{16,0},{20,4},{24,8},{28,12},{1,17},{... | collective-permute-start | bytes 129032 | tf_op jit(solution)/shard_map/ppermute | solution.py:275
  39.8 0.0 collective-permute-done.3.refs_1_
  39.8 0.8 %shard_map.105 = (bf16[96,512]{1,0:T(8,128)(2,1)S(1)}, bf16[96,512]{1,0:T(8,128)(2,1)S(1)}, bf16[96,512]{1,0:T(8,128)(2,1)S(1)}, bf16[48,896]{1,0:T(8,128)(2,1)S(1)}, bf16[48,896]{1,0:T(8,128)(2,1)S(1)}) custom-call(bf16[144,512]{1,0:T(8,128)(2,1)S(1)} %add_convert_fusion.refs_0_, bf16[144,512]{1,0:T(8,128)(2,1)S(1)} %collective-permute-done.3.refs_1_, ...), custom_call_target="tpu_custom_call" | custom-call | tf_op jit(solution)/shard_map/pallas_call | solution.py:35
  40.5 1.8 %collective-permute-start.4 = (bf16[48,896]{1,0:T(8,128)(2,1)S(1)}, bf16[48,896]{1,0:T(8,128)(2,1)S(1)}, u32[]{:S(2)}, u32[]{:S(2)}) collective-permute-start(bf16[48,896]{1,0:T(8,128)(2,1)S(1)} %get-tuple-element.37), channel_id=1, source_target_pairs={{0,4},{4,0},{8,12},{12,8},{16,20},{20,16},{24,28},{28,24},{1,5},{5... | collective-permute-start | bytes 258056 | tf_op jit(solution)/shard_map/ppermute | solution.py:278
  42.3 0.0 collective-permute-done.15
  42.3 0.6 %collective-permute-start.16 = (bf16[24,896]{1,0:T(8,128)(2,1)S(1)}, bf16[24,896]{1,0:T(8,128)(2,1)S(1)}, u32[]{:S(2)}, u32[]{:S(2)}) collective-permute-start(bf16[24,896]{1,0:T(8,128)(2,1)S(1)} %add_convert_fusion.4), channel_id=1, source_target_pairs={{0,24},{4,28},{8,16},{12,20},{16,8},{20,12},{24,0},{28,4},{1,25},{... | collective-permute-start | bytes 129032 | tf_op jit(solution)/shard_map/ppermute | solution.py:275
  42.9 2.2 %collective-permute-done.4 = bf16[48,896]{1,0:T(8,128)(2,1)S(1)} collective-permute-done((bf16[48,896]{1,0:T(8,128)(2,1)S(1)}, bf16[48,896]{1,0:T(8,128)(2,1)S(1)}, u32[]{:S(2)}, u32[]{:S(2)}) %collective-permute-start.4) | collective-permute-done | bytes 86048 | tf_op jit(solution)/shard_map/ppermute | solution.py:278
  45.1 0.8 %collective-permute-start.5 = (bf16[24,896]{1,0:T(8,128)(2,1)S(1)}, bf16[24,896]{1,0:T(8,128)(2,1)S(1)}, u32[]{:S(2)}, u32[]{:S(2)}) collective-permute-start(bf16[24,896]{1,0:T(8,128)(2,1)S(1)} %get-tuple-element.54), channel_id=1, source_target_pairs={{0,8},{4,12},{8,0},{12,4},{16,24},{20,28},{24,16},{28,20},{1,9},{5... | collective-permute-start | bytes 129032 | tf_op jit(solution)/shard_map/ppermute | solution.py:275
  45.9 1.7 %shard_map.111 = bf16[1,512,1792]{2,1,0:T(8,128)(2,1)} custom-call(bf16[48,896]{1,0:T(8,128)(2,1)S(1)} %get-tuple-element.29.refs_0_, bf16[48,896]{1,0:T(8,128)(2,1)S(1)} %collective-permute-done.refs_1_, bf16[96,896]{1,0:T(8,128)(2,1)S(1)} %collective-permute-done.1.refs_2_, bf16[48,896]{1,0:T(8,128)(2,1)S(1)} %collective-permute-done.6.refs_0_.refs_3_, ...), custom_call_target="tpu_custom_call" | custom-call | tf_op jit(solution)/shard_map/pallas_call | solution.py:381
  47.6 2.3 %shard_map.110 = (bf16[1,1792,512]{2,1,0:T(8,128)(2,1)}, bf16[1,1792,512]{2,1,0:T(8,128)(2,1)}) custom-call(bf16[48,896]{1,0:T(8,128)(2,1)S(1)} %get-tuple-element.29.refs_0_, bf16[48,896]{1,0:T(8,128)(2,1)S(1)} %collective-permute-done.refs_1_, bf16[96,896]{1,0:T(8,128)(2,1)S(1)} %collective-permute-done.1.refs_2_, ...), custom_call_target="tpu_custom_call" | custom-call | tf_op jit(solution)/shard_map/pallas_call | solution.py:371
  50.0 0.0 collective-permute-done.14.refs_2_
  50.0 0.0 collective-permute-done.16.refs_3_
  50.0 0.0 collective-permute-done.5.refs_1_
  50.0 1.2 %shard_map.109 = bf16[256,1792]{1,0:T(8,128)(2,1)} custom-call(bf16[24,896]{1,0:T(8,128)(2,1)S(1)} %get-tuple-element.55.refs_0_, bf16[24,896]{1,0:T(8,128)(2,1)S(1)} %collective-permute-done.5.refs_1_, bf16[24,896]{1,0:T(8,128)(2,1)S(1)} %collective-permute-done.14.refs_2_, bf16[24,896]{1,0:T(8,128)(2,1)S(1)} %collective-permute-done.16.refs_3_, ...), custom_call_target="tpu_custom_call" | custom-call | tf_op jit(solution)/shard_map/pallas_call | solution.py:391
  (9 shorter events, 0.2 us)
Async XLA Ops:
  2.5 10.4 %collective-permute-start.6 = (bf16[48,896]{1,0:T(8,128)(2,1)S(1)}, bf16[48,896]{1,0:T(8,128)(2,1)S(1)}, u32[]{:S(2)}, u32[]{:S(2)}) collective-permute-start(bf16[48,896]{1,0:T(8,128)(2,1)S(1)} %get-tuple-element.38), channel_id=1, source_target_pairs={{0,16},{4,20},{8,24},{12,28},{16,0},{20,4},{24,8},{28,12},{1,17},{... | collective-permute-start | bytes 258056 | tf_op jit(solution)/shard_map/ppermute | solution.py:275
  6.7 6.8 %collective-permute-start.7 = (bf16[48,896]{1,0:T(8,128)(2,1)S(1)}, bf16[48,896]{1,0:T(8,128)(2,1)S(1)}, u32[]{:S(2)}, u32[]{:S(2)}) collective-permute-start(bf16[48,896]{1,0:T(8,128)(2,1)S(1)} %get-tuple-element.39), channel_id=1, source_target_pairs={{0,24},{4,28},{8,16},{12,20},{16,8},{20,12},{24,0},{28,4},{1,25},{... | collective-permute-start | bytes 258056 | tf_op jit(solution)/shard_map/ppermute | solution.py:275
  8.0 7.3 %collective-permute-start = (bf16[48,896]{1,0:T(8,128)(2,1)S(1)}, bf16[48,896]{1,0:T(8,128)(2,1)S(1)}, u32[]{:S(2)}, u32[]{:S(2)}) collective-permute-start(bf16[48,896]{1,0:T(8,128)(2,1)S(1)} %get-tuple-element.30), channel_id=1, source_target_pairs={{0,8},{4,12},{8,0},{12,4},{16,24},{20,28},{24,16},{28,20},{1,9},{5... | collective-permute-start | bytes 258056 | tf_op jit(solution)/shard_map/ppermute | solution.py:275
  13.5 6.2 %collective-permute-start.8 = (bf16[96,896]{1,0:T(8,128)(2,1)S(1)}, bf16[96,896]{1,0:T(8,128)(2,1)S(1)}, u32[]{:S(2)}, u32[]{:S(2)}) collective-permute-start(bf16[96,896]{1,0:T(8,128)(2,1)S(1)} %pad_maximum_fusion.1), channel_id=1, source_target_pairs={{0,4},{4,0},{8,12},{12,8},{16,20},{20,16},{24,28},{28,24},{1,5},{5... | collective-permute-start | bytes 516104 | tf_op jit(solution)/shard_map/ppermute | solution.py:278
  15.3 6.2 %collective-permute-start.1 = (bf16[96,896]{1,0:T(8,128)(2,1)S(1)}, bf16[96,896]{1,0:T(8,128)(2,1)S(1)}, u32[]{:S(2)}, u32[]{:S(2)}) collective-permute-start(bf16[96,896]{1,0:T(8,128)(2,1)S(1)} %pad_maximum_fusion), channel_id=1, source_target_pairs={{0,4},{4,0},{8,12},{12,8},{16,20},{20,16},{24,28},{28,24},{1,5},{5... | collective-permute-start | bytes 516104 | tf_op jit(solution)/shard_map/ppermute | solution.py:278
  20.4 2.2 %collective-permute-start.9 = (bf16[96,512]{1,0:T(8,128)(2,1)S(1)}, bf16[96,512]{1,0:T(8,128)(2,1)S(1)}, u32[]{:S(2)}, u32[]{:S(2)}) collective-permute-start(bf16[96,512]{1,0:T(8,128)(2,1)S(1)} %shard_map.106), channel_id=1, source_target_pairs={{0,1},{1,0},{2,3},{3,2},{4,5},{5,4},{6,7},{7,6},{8,9},{9,8},{10,11... | collective-permute-start | bytes 294920 | tf_op jit(solution)/shard_map/ppermute | solution.py:284
  20.9 3.3 %collective-permute-start.11 = (bf16[48,512]{1,0:T(8,128)(2,1)S(1)}, bf16[48,512]{1,0:T(8,128)(2,1)S(1)}, u32[]{:S(2)}, u32[]{:S(2)}) collective-permute-start(bf16[48,512]{1,0:T(8,128)(2,1)S(1)} %shard_map.107), channel_id=1, source_target_pairs={{0,1},{1,0},{2,3},{3,2},{4,5},{5,4},{6,7},{7,6},{8,9},{9,8},{10,11... | collective-permute-start | bytes 147464 | tf_op jit(solution)/shard_map/ppermute | solution.py:284
  22.5 8.7 %collective-permute-start.2 = (bf16[144,512]{1,0:T(8,128)(2,1)S(1)}, bf16[144,512]{1,0:T(8,128)(2,1)S(1)}, u32[]{:S(2)}, u32[]{:S(2)}) collective-permute-start(bf16[144,512]{1,0:T(8,128)(2,1)S(1)} %shard_map.104), channel_id=1, source_target_pairs={{0,1},{1,0},{2,3},{3,2},{4,5},{5,4},{6,7},{7,6},{8,9},{9,8},{10,11... | collective-permute-start | bytes 442376 | tf_op jit(solution)/shard_map/ppermute | solution.py:284
  22.6 6.3 %collective-permute-start.10 = (bf16[96,512]{1,0:T(8,128)(2,1)S(1)}, bf16[96,512]{1,0:T(8,128)(2,1)S(1)}, u32[]{:S(2)}, u32[]{:S(2)}) collective-permute-start(bf16[96,512]{1,0:T(8,128)(2,1)S(1)} %add_convert_fusion.1.refs_0_), channel_id=1, source_target_pairs={{0,2},{1,3},{2,0},{3,1},{4,6},{5,7},{6,4},{7,5},{8,10},{9,11},{10,... | collective-permute-start | bytes 294920 | tf_op jit(solution)/shard_map/ppermute | solution.py:284
  24.2 4.7 %collective-permute-start.12 = (bf16[48,512]{1,0:T(8,128)(2,1)S(1)}, bf16[48,512]{1,0:T(8,128)(2,1)S(1)}, u32[]{:S(2)}, u32[]{:S(2)}) collective-permute-start(bf16[48,512]{1,0:T(8,128)(2,1)S(1)} %add_convert_fusion.3.refs_2_), channel_id=1, source_target_pairs={{0,2},{1,3},{2,0},{3,1},{4,6},{5,7},{6,4},{7,5},{8,10},{9,11},{10,... | collective-permute-start | bytes 147464 | tf_op jit(solution)/shard_map/ppermute | solution.py:284
  29.7 4.1 %collective-permute-start.13 = (bf16[24,896]{1,0:T(8,128)(2,1)S(1)}, bf16[24,896]{1,0:T(8,128)(2,1)S(1)}, u32[]{:S(2)}, u32[]{:S(2)}) collective-permute-start(bf16[24,896]{1,0:T(8,128)(2,1)S(1)} %get-tuple-element.41), channel_id=1, source_target_pairs={{0,4},{4,0},{8,12},{12,8},{16,20},{20,16},{24,28},{28,24},{1,5},{5... | collective-permute-start | bytes 129032 | tf_op jit(solution)/shard_map/ppermute | solution.py:278
  31.3 8.5 %collective-permute-start.3 = (bf16[144,512]{1,0:T(8,128)(2,1)S(1)}, bf16[144,512]{1,0:T(8,128)(2,1)S(1)}, u32[]{:S(2)}, u32[]{:S(2)}) collective-permute-start(bf16[144,512]{1,0:T(8,128)(2,1)S(1)} %add_convert_fusion.refs_0_), channel_id=1, source_target_pairs={{0,2},{1,3},{2,0},{3,1},{4,6},{5,7},{6,4},{7,5},{8,10},{9,11},{10,... | collective-permute-start | bytes 442376 | tf_op jit(solution)/shard_map/ppermute | solution.py:284
  32.9 9.4 %collective-permute-start.15 = (bf16[24,896]{1,0:T(8,128)(2,1)S(1)}, bf16[24,896]{1,0:T(8,128)(2,1)S(1)}, u32[]{:S(2)}, u32[]{:S(2)}) collective-permute-start(bf16[24,896]{1,0:T(8,128)(2,1)S(1)} %get-tuple-element.43), channel_id=1, source_target_pairs={{0,4},{4,0},{8,12},{12,8},{16,20},{20,16},{24,28},{28,24},{1,5},{5... | collective-permute-start | bytes 129032 | tf_op jit(solution)/shard_map/ppermute | solution.py:278
  33.8 16.2 %collective-permute-start.14 = (bf16[24,896]{1,0:T(8,128)(2,1)S(1)}, bf16[24,896]{1,0:T(8,128)(2,1)S(1)}, u32[]{:S(2)}, u32[]{:S(2)}) collective-permute-start(bf16[24,896]{1,0:T(8,128)(2,1)S(1)} %add_convert_fusion.5), channel_id=1, source_target_pairs={{0,16},{4,20},{8,24},{12,28},{16,0},{20,4},{24,8},{28,12},{1,17},{... | collective-permute-start | bytes 129032 | tf_op jit(solution)/shard_map/ppermute | solution.py:275
  40.5 4.6 %collective-permute-start.4 = (bf16[48,896]{1,0:T(8,128)(2,1)S(1)}, bf16[48,896]{1,0:T(8,128)(2,1)S(1)}, u32[]{:S(2)}, u32[]{:S(2)}) collective-permute-start(bf16[48,896]{1,0:T(8,128)(2,1)S(1)} %get-tuple-element.37), channel_id=1, source_target_pairs={{0,4},{4,0},{8,12},{12,8},{16,20},{20,16},{24,28},{28,24},{1,5},{5... | collective-permute-start | bytes 258056 | tf_op jit(solution)/shard_map/ppermute | solution.py:278
  42.3 7.7 %collective-permute-start.16 = (bf16[24,896]{1,0:T(8,128)(2,1)S(1)}, bf16[24,896]{1,0:T(8,128)(2,1)S(1)}, u32[]{:S(2)}, u32[]{:S(2)}) collective-permute-start(bf16[24,896]{1,0:T(8,128)(2,1)S(1)} %add_convert_fusion.4), channel_id=1, source_target_pairs={{0,24},{4,28},{8,16},{12,20},{16,8},{20,12},{24,0},{28,4},{1,25},{... | collective-permute-start | bytes 129032 | tf_op jit(solution)/shard_map/ppermute | solution.py:275
  45.1 4.9 %collective-permute-start.5 = (bf16[24,896]{1,0:T(8,128)(2,1)S(1)}, bf16[24,896]{1,0:T(8,128)(2,1)S(1)}, u32[]{:S(2)}, u32[]{:S(2)}) collective-permute-start(bf16[24,896]{1,0:T(8,128)(2,1)S(1)} %get-tuple-element.54), channel_id=1, source_target_pairs={{0,8},{4,12},{8,0},{12,4},{16,24},{20,28},{24,16},{28,20},{1,9},{5... | collective-permute-start | bytes 129032 | tf_op jit(solution)/shard_map/ppermute | solution.py:275
